TPU v7x, 32 devices: a whole 2x2x4 slice. The times are simulated.
32 devices in a mesh: dp: 4 (over y, x), tensor: 8 (over z, core).
Axes of the slice: x: 2, y: 2, z: 4, core: 2. Of those that a mesh axis runs over, the one named last changes fastest.
Arguments:
- tokens: bfloat16 [2048, 2048], P(('dp', 'tensor')), may hold values from -6 to 6
- cotangent: bfloat16 [2048, 2048], P(('dp', 'tensor')), may hold values from -6 to 6
- w_query: bfloat16 [2048, 2048], P(None, 'tensor'), may hold values from -0.125 to 0.125
- w_key: bfloat16 [2048, 2048], P(None, 'tensor'), may hold values from -0.125 to 0.125
- w_value: bfloat16 [2048, 2048], P(None, 'tensor'), may hold values from -0.125 to 0.125
- w_out: bfloat16 [2048, 2048], P('tensor'), may hold values from -0.125 to 0.125
- w_gate: bfloat16 [2048, 8192], P(None, 'tensor'), may hold values from -0.125 to 0.125
- w_up: bfloat16 [2048, 8192], P(None, 'tensor'), may hold values from -0.125 to 0.125
- w_down: bfloat16 [8192, 2048], P('tensor'), may hold values from -0.0625 to 0.0625
- q_gain: float32 [2048], P('tensor'), may hold values from 0.1 to 1.9
- k_gain: float32 [2048], P('tensor'), may hold values from 0.1 to 1.9
- attn_gain: float32 [2048], replicated, may hold values from 0.1 to 1.9
- ffn_gain: float32 [2048], replicated, may hold values from 0.1 to 1.9
Outputs:
- layer_out: float32 [2048, 2048], P(('dp', 'tensor'))
- grad_tokens: float32 [2048, 2048], P(('dp', 'tensor'))
- grad_w_query: float32 [2048, 2048], P(None, 'tensor')
- grad_w_key: float32 [2048, 2048], P(None, 'tensor')
- grad_w_value: float32 [2048, 2048], P(None, 'tensor')
- grad_w_out: float32 [2048, 2048], P('tensor')
- grad_w_gate: float32 [2048, 8192], P(None, 'tensor')
- grad_w_up: float32 [2048, 8192], P(None, 'tensor')
- grad_w_down: float32 [8192, 2048], P('tensor')
- grad_q_gain: float32 [2048], P('tensor')
- grad_k_gain: float32 [2048], P('tensor')
- grad_attn_gain: float32 [2048], replicated
- grad_ffn_gain: float32 [2048], replicated
All inputs are finite; a program needn't handle non-finite values.
Results may differ from a plain program's by a relative error of at most 0.015.
Values may be sent and summed in bfloat16 or wider, within the bound.
No kernel may reach another device: no remote copies, remote signals or barrier semaphores. Data moves between devices by JAX's collectives and lax.ppermute only.
A program may use at most 192 MiB of HBM per device.

v0:
```python
import functools
import math

import jax
import jax.numpy as jnp
from jax import lax
from jax.experimental import pallas as pl
from jax.experimental.pallas import tpu as pltpu
from jax.sharding import PartitionSpec as P

HD = 128
SEQ = 256

epsilon = 1e-06
rope_base = 500000.0

MIB = 1 << 20


def row_scale(matrix):
    return lax.rsqrt(jnp.mean(matrix * matrix, axis=1, keepdims=True) + epsilon)


def norm_back(grad_normed, normed, inverse):
    return inverse * (grad_normed - normed * jnp.mean(grad_normed * normed, axis=1, keepdims=True))


def product(left, right):
    return jnp.dot(left, right, preferred_element_type=jnp.float32)


def times_transposed(left, right):
    return lax.dot_general(
        left, right, (((1,), (1,)), ((), ())), preferred_element_type=jnp.float32
    )


def transposed_times(left, right):
    return lax.dot_general(
        left, right, (((0,), (0,)), ((), ())), preferred_element_type=jnp.float32
    )


def column(row, width):
    return jnp.broadcast_to(row, (width, row.shape[1])).T


def row_sums(matrix):
    return jnp.sum(matrix.T, axis=0, keepdims=True)


def sequence_rows(ref, s, chunk, half, lanes):
    top = ref[s * chunk : (s + 1) * chunk, lanes]
    bottom = ref[half + s * chunk : half + (s + 1) * chunk, lanes]
    return jnp.concatenate([top, bottom], axis=0)


def store_rows(ref, s, chunk, half, lanes, value):
    ref[s * chunk : (s + 1) * chunk, lanes] = value[:chunk]
    ref[half + s * chunk : half + (s + 1) * chunk, lanes] = value[chunk:]


def block_row(ref, i, blocks):
    count = ref.shape[1] // 2
    return jnp.concatenate(
        [ref[b : b + 1, i * count : (i + 1) * count] for b in blocks], axis=1
    )


def sequence_blocks(ref, s, chunk):
    count = ref.shape[1] // 2
    steps = chunk // count
    pairs = ref.shape[0] // 2
    return [h * pairs + s * steps + k for h in range(2) for k in range(steps)]


def store_blocks(ref, i, blocks, row):
    count = ref.shape[1] // 2
    for j, b in enumerate(blocks):
        ref[b : b + 1, i * count : (i + 1) * count] = row[:, j * count : (j + 1) * count]


def causal_mask(pos_ref, s, chunk, half):
    key_pos = jnp.concatenate(
        [
            pos_ref[:, s * chunk : (s + 1) * chunk],
            pos_ref[:, half + s * chunk : half + (s + 1) * chunk],
        ],
        axis=1,
    )
    length = 2 * chunk
    key_all = jnp.broadcast_to(key_pos, (length, length))
    return key_all.T >= key_all


def attend_kernel(model_width, orders, *refs):
    parts = refs[: len(orders) + 1]
    (
        query_ref,
        keys_ref,
        values_ref,
        q_gain_ref,
        k_gain_ref,
        cos_ref,
        sin_ref,
        pos_ref,
        attended_ref,
        q_rot_ref,
        k_rot_ref,
        squares_ref,
    ) = refs[len(parts) :]
    for i, row in enumerate(summed_blocks(parts, orders)):
        squares_ref[i : i + 1, :] = row
    rows, width = query_ref.shape
    half = rows // 2
    chunk = SEQ // 2
    for s in range(rows // SEQ):
        every = slice(None)
        cos = sequence_rows(cos_ref, s, chunk, half, every)
        sin = sequence_rows(sin_ref, s, chunk, half, every)
        mask = causal_mask(pos_ref, s, chunk, half)
        blocks = sequence_blocks(squares_ref, s, chunk)
        q_inv = column(lax.rsqrt(block_row(squares_ref, 0, blocks) / model_width + epsilon), HD)
        k_inv = column(lax.rsqrt(block_row(squares_ref, 1, blocks) / model_width + epsilon), HD)
        for h in range(width // HD):
            lanes = slice(h * HD, (h + 1) * HD)
            q = sequence_rows(query_ref, s, chunk, half, lanes) * q_inv * q_gain_ref[:, lanes]
            k = sequence_rows(keys_ref, s, chunk, half, lanes) * k_inv * k_gain_ref[:, lanes]
            q = (q * cos + pltpu.roll(q, HD // 2, 1) * sin).astype(jnp.bfloat16)
            k = (k * cos + pltpu.roll(k, HD // 2, 1) * sin).astype(jnp.bfloat16)
            store_rows(q_rot_ref, s, chunk, half, lanes, q)
            store_rows(k_rot_ref, s, chunk, half, lanes, k)
            scores = times_transposed(q, k) * (1.0 / math.sqrt(HD))
            scores = jnp.where(mask, scores, -1e30)
            shifted = jnp.exp(scores - jnp.max(scores, axis=1, keepdims=True))
            probs = (shifted / jnp.sum(shifted, axis=1, keepdims=True)).astype(jnp.bfloat16)
            v = sequence_rows(values_ref, s, chunk, half, lanes)
            store_rows(
                attended_ref, s, chunk, half, lanes, product(probs, v).astype(jnp.bfloat16)
            )


def attend(query, keys, values, squares, orders, q_gain, k_gain, tables, model_width):
    rows, width = query.shape
    out = jax.ShapeDtypeStruct((rows, width), jnp.bfloat16)
    return pl.pallas_call(
        functools.partial(attend_kernel, model_width, orders),
        out_shape=(
            out,
            out,
            out,
            jax.ShapeDtypeStruct(squares[0].shape, jnp.float32),
        ),
        name="attend",
        compiler_params=pltpu.CompilerParams(vmem_limit_bytes=16 * MIB),
        cost_estimate=pl.CostEstimate(
            flops=4 * rows * SEQ * width,
            bytes_accessed=16 * rows * width,
            transcendentals=rows * SEQ * width // HD,
        ),
    )(*squares, query, keys, values, q_gain[None, :], k_gain[None, :], *tables)


def attend_back_kernel(
    model_width,
    grad_ref,
    q_rot_ref,
    k_rot_ref,
    values_ref,
    query_ref,
    keys_ref,
    squares_ref,
    q_gain_ref,
    k_gain_ref,
    cos_ref,
    sin_ref,
    pos_ref,
    grad_values_ref,
    grad_q_ref,
    grad_k_ref,
    inner_ref,
    gain_ref,
):
    rows, width = query_ref.shape
    half = rows // 2
    chunk = SEQ // 2
    scale = 1.0 / math.sqrt(HD)
    gain_ref[...] = jnp.zeros_like(gain_ref)
    for s in range(rows // SEQ):
        every = slice(None)
        cos = sequence_rows(cos_ref, s, chunk, half, every)
        sin = sequence_rows(sin_ref, s, chunk, half, every)
        mask = causal_mask(pos_ref, s, chunk, half)
        blocks = sequence_blocks(squares_ref, s, chunk)
        q_inv = column(lax.rsqrt(block_row(squares_ref, 0, blocks) / model_width + epsilon), HD)
        k_inv = column(lax.rsqrt(block_row(squares_ref, 1, blocks) / model_width + epsilon), HD)
        q_inner = jnp.zeros((1, SEQ), jnp.float32)
        k_inner = jnp.zeros((1, SEQ), jnp.float32)
        for h in range(width // HD):
            lanes = slice(h * HD, (h + 1) * HD)
            q = sequence_rows(q_rot_ref, s, chunk, half, lanes)
            k = sequence_rows(k_rot_ref, s, chunk, half, lanes)
            v = sequence_rows(values_ref, s, chunk, half, lanes)
            g = sequence_rows(grad_ref, s, chunk, half, lanes)
            scores = times_transposed(q, k) * scale
            scores = jnp.where(mask, scores, -1e30)
            shifted = jnp.exp(scores - jnp.max(scores, axis=1, keepdims=True))
            probs = shifted / jnp.sum(shifted, axis=1, keepdims=True)
            grad_v = transposed_times(probs.astype(jnp.bfloat16), g).astype(jnp.bfloat16)
            store_rows(grad_values_ref, s, chunk, half, lanes, grad_v)
            grad_probs = times_transposed(g, v)
            inner = jnp.sum(probs * grad_probs, axis=1, keepdims=True)
            grad_scores = (probs * (grad_probs - inner) * scale).astype(jnp.bfloat16)
            grad_q = product(grad_scores, k)
            grad_k = transposed_times(grad_scores, q)
            grad_q = grad_q * cos - pltpu.roll(grad_q, HD // 2, 1) * sin
            grad_k = grad_k * cos - pltpu.roll(grad_k, HD // 2, 1) * sin
            q_part = grad_q * (sequence_rows(query_ref, s, chunk, half, lanes) * q_inv)
            k_part = grad_k * (sequence_rows(keys_ref, s, chunk, half, lanes) * k_inv)
            gain_ref[0:1, lanes] += jnp.sum(q_part, axis=0, keepdims=True)
            gain_ref[1:2, lanes] += jnp.sum(k_part, axis=0, keepdims=True)
            q_inner += row_sums(q_part * q_gain_ref[:, lanes])
            k_inner += row_sums(k_part * k_gain_ref[:, lanes])
            store_rows(grad_q_ref, s, chunk, half, lanes, grad_q * q_gain_ref[:, lanes])
            store_rows(grad_k_ref, s, chunk, half, lanes, grad_k * k_gain_ref[:, lanes])
        store_blocks(inner_ref, 0, blocks, q_inner)
        store_blocks(inner_ref, 1, blocks, k_inner)


def attend_back(
    grad_attended, q_rot, k_rot, values, query, keys, squares, q_gain, k_gain, tables, model_width
):
    rows, width = query.shape
    wide = jax.ShapeDtypeStruct((rows, width), jnp.float32)
    return pl.pallas_call(
        functools.partial(attend_back_kernel, model_width),
        out_shape=(
            jax.ShapeDtypeStruct((rows, width), jnp.bfloat16),
            wide,
            wide,
            jax.ShapeDtypeStruct(squares.shape, jnp.float32),
            jax.ShapeDtypeStruct((2, width), jnp.float32),
        ),
        name="attend_back",
        compiler_params=pltpu.CompilerParams(vmem_limit_bytes=20 * MIB),
        cost_estimate=pl.CostEstimate(
            flops=10 * rows * SEQ * width,
            bytes_accessed=26 * rows * width,
            transcendentals=rows * SEQ * width // HD,
        ),
    )(
        grad_attended,
        q_rot,
        k_rot,
        values,
        query,
        keys,
        squares,
        q_gain[None, :],
        k_gain[None, :],
        *tables,
    )


def finish_kernel(model_width, orders, *refs):
    parts = refs[: len(orders) + 1]
    (
        query_ref,
        keys_ref,
        grad_q_ref,
        grad_k_ref,
        grad_values_ref,
        squares_ref,
        out_ref,
        rest_ref,
        inner_ref,
    ) = refs[len(parts) :]
    _, width = query_ref.shape
    count = squares_ref.shape[0]
    blocks = list(range(count))
    for i, row in enumerate(summed_blocks([part.at[:count] for part in parts], orders)):
        inner_ref[i : i + 1, :] = row
    rest = [part[count:, :] for part in parts]
    while len(rest) > 1:
        rest = [rest[i] + rest[i + 1] for i in range(0, len(rest), 2)]
    rest_ref[...] = rest[0]
    for i, source, target in ((0, query_ref, grad_q_ref), (1, keys_ref, grad_k_ref)):
        inverse = column(
            lax.rsqrt(block_row(squares_ref, i, blocks) / model_width + epsilon), HD
        )
        inner = column(block_row(inner_ref, i, blocks) / model_width, HD)
        for h in range(width // HD):
            lanes = slice(h * HD, (h + 1) * HD)
            normed = source[:, lanes] * inverse
            value = inverse * (target[:, lanes] - normed * inner)
            start = i * width + h * HD
            out_ref[:, start : start + HD] = value.astype(jnp.bfloat16)
    out_ref[:, 2 * width :] = grad_values_ref[...]


def finish(query, keys, grad_q, grad_k, grad_values, squares, inner, orders, model_width):
    rows, width = query.shape
    count, lanes = squares.shape
    return pl.pallas_call(
        functools.partial(finish_kernel, model_width, orders),
        out_shape=(
            jax.ShapeDtypeStruct((rows, 3 * width), jnp.bfloat16),
            jax.ShapeDtypeStruct((inner[0].shape[0] - count, lanes), jnp.float32),
        ),
        scratch_shapes=[pltpu.VMEM((count, lanes), jnp.float32)],
        name="finish",
        compiler_params=pltpu.CompilerParams(vmem_limit_bytes=16 * MIB),
        cost_estimate=pl.CostEstimate(
            flops=10 * rows * width, bytes_accessed=24 * rows * width, transcendentals=0
        ),
    )(*inner, query, keys, grad_q, grad_k, grad_values, squares)


def summed_blocks(refs, orders):
    rows = []
    for i in range(refs[0].shape[0]):
        total = refs[0][i : i + 1, :]
        for order, other in zip(orders, refs[1:]):
            total = total + other[order[i] : order[i] + 1, :]
        rows.append(total)
    return rows


def add_blocks_kernel(orders, *refs):
    own, others, out = refs[0], refs[1:-1], refs[-1]
    count = len(orders[0])
    for i in range(count):
        total = own[i : i + 1, :]
        for order, other in zip(orders, others):
            total = total + other[order[i] : order[i] + 1, :]
        out[i : i + 1, :] = total
    if own.shape[0] > count:
        rest = [own[count:, :]] + [other[count:, :] for other in others]
        while len(rest) > 1:
            rest = [rest[i] + rest[i + 1] for i in range(0, len(rest), 2)]
        out[count:, :] = rest[0]


def add_pieces_kernel(*refs):
    total = refs[0][...]
    for ref in refs[1:-1]:
        total = total + ref[...].astype(jnp.float32)
    refs[-1][...] = total.astype(jnp.bfloat16)


def add_pieces(own, others):
    return pl.pallas_call(
        add_pieces_kernel,
        out_shape=jax.ShapeDtypeStruct(own.shape, jnp.bfloat16),
        name="add_pieces",
        compiler_params=pltpu.CompilerParams(vmem_limit_bytes=4 * MIB),
    )(own, *others)


def add_blocks(own, others, orders):
    return pl.pallas_call(
        functools.partial(add_blocks_kernel, orders),
        out_shape=jax.ShapeDtypeStruct(own.shape, own.dtype),
        name="add_blocks",
        compiler_params=pltpu.CompilerParams(vmem_limit_bytes=4 * MIB),
    )(own, *others)


def joined(refs):
    return refs[0][...] if len(refs) == 1 else jnp.concatenate([r[...] for r in refs], axis=0)


def project_kernel(pieces, *refs):
    rows = joined(refs[:pieces])
    w_query_ref, w_key_ref, w_value_ref, query_ref, keys_ref, values_ref, squares_ref = refs[
        pieces:
    ]
    blocks = list(range(squares_ref.shape[0]))
    for i, weight, out in ((0, w_query_ref, query_ref), (1, w_key_ref, keys_ref)):
        value = product(rows, weight[...])
        out[...] = value
        square = value * value
        folded = square[:, :HD]
        for h in range(1, value.shape[1] // HD):
            folded = folded + square[:, h * HD : (h + 1) * HD]
        store_blocks(squares_ref, i, blocks, row_sums(folded))
    values_ref[...] = product(rows, w_value_ref[...]).astype(jnp.bfloat16)


def project(rows, w_query, w_key, w_value, tensor_size):
    count = sum(piece.shape[0] for piece in rows)
    depth, width = w_query.shape
    wide = jax.ShapeDtypeStruct((count, width), jnp.float32)
    return pl.pallas_call(
        functools.partial(project_kernel, len(rows)),
        out_shape=(
            wide,
            wide,
            jax.ShapeDtypeStruct((count, width), jnp.bfloat16),
            jax.ShapeDtypeStruct((tensor_size, 2 * count // tensor_size), jnp.float32),
        ),
        name="project",
        compiler_params=pltpu.CompilerParams(vmem_limit_bytes=20 * MIB),
        cost_estimate=pl.CostEstimate(
            flops=6 * count * depth * width,
            bytes_accessed=2 * count * depth + 6 * depth * width + 10 * count * width,
            transcendentals=0,
        ),
    )(*rows, w_query, w_key, w_value)


def ffn_kernel(pieces, *refs):
    rows = joined(refs[:pieces])
    w_gate_ref, w_up_ref, gate_ref, up_ref, swiglu_ref = refs[pieces:]
    gate = product(rows, w_gate_ref[...])
    up = product(rows, w_up_ref[...])
    gate_ref[...] = gate
    up_ref[...] = up
    swiglu_ref[...] = (gate * jax.nn.sigmoid(gate) * up).astype(jnp.bfloat16)


def ffn(rows, w_gate, w_up):
    count = sum(piece.shape[0] for piece in rows)
    depth, units = w_gate.shape
    tile = min(256, units)
    weight = pl.BlockSpec((depth, tile), lambda j: (0, j))
    out = pl.BlockSpec((count, tile), lambda j: (0, j))
    wide = jax.ShapeDtypeStruct((count, units), jnp.float32)
    return pl.pallas_call(
        functools.partial(ffn_kernel, len(rows)),
        grid=(units // tile,),
        in_specs=[pl.BlockSpec(piece.shape, lambda j: (0, 0)) for piece in rows]
        + [weight, weight],
        out_specs=(out, out, out),
        out_shape=(wide, wide, jax.ShapeDtypeStruct((count, units), jnp.bfloat16)),
        name="ffn",
        compiler_params=pltpu.CompilerParams(vmem_limit_bytes=20 * MIB),
        cost_estimate=pl.CostEstimate(
            flops=4 * count * depth * units,
            bytes_accessed=2 * count * depth + 4 * depth * units + 10 * count * units,
            transcendentals=count * units,
        ),
    )(*rows, w_gate, w_up)


def ffn_back_kernel(pieces, *refs):
    grad = joined(refs[:pieces])
    w_down_ref, gate_ref, up_ref, grad_gate_ref, grad_up_ref = refs[pieces:]
    grad_swiglu = times_transposed(grad, w_down_ref[...])
    gate = gate_ref[...]
    sig = jax.nn.sigmoid(gate)
    grad_gate = grad_swiglu * up_ref[...] * sig * (1.0 + gate * (1.0 - sig))
    grad_gate_ref[...] = grad_gate.astype(jnp.bfloat16)
    grad_up_ref[...] = (grad_swiglu * (gate * sig)).astype(jnp.bfloat16)


def ffn_back(grad, w_down, gate, up):
    count = sum(piece.shape[0] for piece in grad)
    units, depth = w_down.shape
    tile = min(256, units)
    out = pl.BlockSpec((count, tile), lambda j: (0, j))
    narrow = jax.ShapeDtypeStruct((count, units), jnp.bfloat16)
    return pl.pallas_call(
        functools.partial(ffn_back_kernel, len(grad)),
        grid=(units // tile,),
        in_specs=[pl.BlockSpec(piece.shape, lambda j: (0, 0)) for piece in grad]
        + [pl.BlockSpec((tile, depth), lambda j: (j, 0)), out, out],
        out_specs=(out, out),
        out_shape=(narrow, narrow),
        name="ffn_back",
        compiler_params=pltpu.CompilerParams(vmem_limit_bytes=20 * MIB),
        cost_estimate=pl.CostEstimate(
            flops=2 * count * depth * units,
            bytes_accessed=2 * count * depth + 2 * depth * units + 12 * count * units,
            transcendentals=count * units,
        ),
    )(*grad, w_down, gate, up)


def weight_grad_kernel(left_counts, right_counts, rights, outs, *refs):
    groups = len(left_counts)
    left, at = [], 0
    for count in left_counts:
        left.append(joined(refs[at : at + count]))
        at += count
    out_refs = refs[len(refs) - rights * outs :]
    for r in range(rights):
        right = []
        for count in right_counts:
            right.append(refs[at : at + count])
            at += count
        width = right[0][0].shape[1] // outs
        for o in range(outs):
            sums = []
            for g in range(groups):
                pieces = [ref[:, o * width : (o + 1) * width] for ref in right[g]]
                whole = pieces[0] if len(pieces) == 1 else jnp.concatenate(pieces, axis=0)
                sums.append(transposed_times(left[g], whole))
            while len(sums) > 1:
                sums = [sums[i] - sums[i + 1] * -1.0 for i in range(0, len(sums), 2)]
            out_refs[r * outs + o][...] = sums[0]


def weight_grad(left, *rights, outs=1):
    depth = left[0][0].shape[1]
    tile = min(256, depth)
    left_pieces = [piece for group in left for piece in group]
    right_pieces = [piece for right in rights for group in right for piece in group]
    rows = sum(piece.shape[0] for piece in left_pieces)
    widths = [right[0][0].shape[1] // outs for right in rights for _ in range(outs)]
    return pl.pallas_call(
        functools.partial(
            weight_grad_kernel,
            [len(group) for group in left],
            [len(group) for group in rights[0]],
            len(rights),
            outs,
        ),
        grid=(depth // tile,),
        in_specs=[pl.BlockSpec((piece.shape[0], tile), lambda i: (0, i)) for piece in left_pieces]
        + [pl.BlockSpec(piece.shape, lambda i: (0, 0)) for piece in right_pieces],
        out_specs=[pl.BlockSpec((tile, width), lambda i: (i, 0)) for width in widths],
        out_shape=[jax.ShapeDtypeStruct((depth, width), jnp.float32) for width in widths],
        name="weight_grad",
        compiler_params=pltpu.CompilerParams(vmem_limit_bytes=44 * MIB),
        cost_estimate=pl.CostEstimate(
            flops=2 * rows * depth * sum(widths),
            bytes_accessed=2 * rows * (depth + sum(widths)) + 4 * depth * sum(widths),
            transcendentals=0,
        ),
    )(*left_pieces, *right_pieces)


def build(dp_size, tensor_size):
    pairs = tensor_size // 2

    def swap(value, axis, mask):
        size = dp_size if axis == "dp" else tensor_size
        return lax.ppermute(value, axis, [(i, i ^ mask) for i in range(size)])

    def tensor_gather(own):
        near = [own] + [swap(own, "tensor", 2 * k) for k in range(1, pairs)]
        return near + [swap(near[k], "tensor", 1) for k in range(pairs)]

    def tensor_scatter(partial_of, rows):
        half = rows // 2
        far = partial_of(half, rows).astype(jnp.bfloat16)
        far = swap(far, "tensor", 1)
        near = partial_of(0, half) + far.astype(jnp.float32)
        count = half // pairs
        total = near[:count]
        for k in range(1, pairs):
            block = near[k * count : (k + 1) * count].astype(jnp.bfloat16)
            total = total + swap(block, "tensor", 2 * k).astype(jnp.float32)
        return total

    def row_sum(value):
        def order(mask):
            out = []
            for i in range(tensor_size):
                wanted = (2 * (i % pairs) + i // pairs) ^ mask
                out.append((wanted % 2) * pairs + wanted // 2)
            return out

        value = add_blocks(value, [swap(value, "tensor", 1)], [order(1)])
        others = [swap(value, "tensor", 2 * k) for k in range(1, pairs)]
        return [value] + others, [order(2 * k) for k in range(1, pairs)]

    def tree_sum(values):
        while len(values) > 1:
            values = [values[i] + values[i + 1] for i in range(0, len(values), 2)]
        return values[0]

    def dp_gather(own):
        return [[own]] + [[swap(own, "dp", j)] for j in range(1, dp_size)]

    def dp_gather_shared(pieces):
        near = jnp.concatenate(pieces[:pairs], axis=0)
        groups = [[near] + pieces[pairs:]]
        for j in range(1, dp_size):
            piece = swap(near, "dp", j)
            groups.append([piece, swap(piece, "tensor", 1)])
        return groups

    def dp_sum(matrix):
        rows = matrix.shape[0] // dp_size
        rounded = matrix.astype(jnp.bfloat16)
        me = lax.axis_index("dp")
        zero = jnp.zeros_like(me)
        own = lax.dynamic_slice_in_dim(matrix, me * rows, rows, 0)
        others = []
        for j in range(1, dp_size):
            piece = lax.dynamic_slice_in_dim(rounded, (me ^ j) * rows, rows, 0)
            others.append(swap(piece, "dp", j))
        total = add_pieces(own, others)
        result = jnp.zeros(matrix.shape, jnp.float32)
        for j in range(dp_size):
            piece = total if j == 0 else swap(total, "dp", j)
            result = lax.dynamic_update_slice(
                result, piece.astype(jnp.float32), ((me ^ j) * rows, zero)
            )
        return result

    def positions(rows):
        count = rows // tensor_size
        index = jnp.arange(rows, dtype=jnp.int32)
        block = index // count
        mask = 2 * (block % pairs) + block // pairs
        owner = lax.axis_index("tensor").astype(jnp.int32) ^ mask
        return (owner * count + index % count) % SEQ

    def tables_of(rows):
        pos = positions(rows)
        half_width = HD // 2
        exponent = jnp.arange(half_width, dtype=jnp.float32) * (2.0 / HD)
        frequency = rope_base ** (-exponent)
        angles = pos.astype(jnp.float32)[:, None] * frequency[None, :]
        cos, sin = jnp.cos(angles), jnp.sin(angles)
        return (
            jnp.concatenate([cos, cos], axis=1),
            jnp.concatenate([-sin, sin], axis=1),
            pos[None, :],
        )

    def shards(
        tokens,
        cotangent,
        w_query,
        w_key,
        w_value,
        w_out,
        w_gate,
        w_up,
        w_down,
        q_gain,
        k_gain,
        attn_gain,
        ffn_gain,
    ):
        model_width = tokens.shape[1]
        rows = tokens.shape[0] * tensor_size
        width = w_query.shape[1]
        tables = tables_of(rows)

        gathered = tensor_gather(tokens)
        query, keys, values, squares = project(gathered, w_query, w_key, w_value, tensor_size)
        square_parts, orders = row_sum(squares)
        attended, q_rot, k_rot, squares = attend(
            query, keys, values, square_parts, orders, q_gain, k_gain, tables, model_width
        )
        attn_rows = tensor_scatter(lambda a, b: product(attended[a:b], w_out), rows)
        a_inverse = row_scale(attn_rows)
        a_normed = attn_rows * a_inverse
        mixed = tokens.astype(jnp.float32) + a_normed * attn_gain
        mixed_b = tensor_gather(mixed.astype(jnp.bfloat16))
        gate, up_proj, swiglu = ffn(mixed_b, w_gate, w_up)
        ffn_rows = tensor_scatter(lambda a, b: product(swiglu[a:b], w_down), rows)
        m_inverse = row_scale(ffn_rows)
        m_normed = ffn_rows * m_inverse
        layer_out = mixed + m_normed * ffn_gain
        grad_out = cotangent.astype(jnp.float32)
        ffn_gain_part = jnp.sum(grad_out * m_normed, axis=0)
        grad_ffn = tensor_gather(
            norm_back(grad_out * ffn_gain, m_normed, m_inverse).astype(jnp.bfloat16)
        )
        grad_gate, grad_up = ffn_back(grad_ffn, w_down, gate, up_proj)
        grad_mixed = grad_out + tensor_scatter(
            lambda a, b: times_transposed(grad_gate[a:b], w_gate)
            + times_transposed(grad_up[a:b], w_up),
            rows,
        )
        attn_gain_part = jnp.sum(grad_mixed * a_normed, axis=0)
        grad_attn = jnp.concatenate(tensor_gather(
            norm_back(grad_mixed * attn_gain, a_normed, a_inverse).astype(jnp.bfloat16)
        ), axis=0)
        grad_attended = times_transposed(grad_attn, w_out).astype(jnp.bfloat16)
        grad_values, grad_q, grad_k, inner, gain_parts = attend_back(
            grad_attended,
            q_rot,
            k_rot,
            values,
            query,
            keys,
            squares,
            q_gain,
            k_gain,
            tables,
            model_width,
        )
        lanes = inner.shape[1]
        inner_parts, orders = row_sum(
            jnp.concatenate(
                [inner, attn_gain_part.reshape(-1, lanes), ffn_gain_part.reshape(-1, lanes)]
            ),
        )
        grad_qkv, post_gains = finish(
            query, keys, grad_q, grad_k, grad_values, squares, inner_parts, orders, model_width
        )
        grad_tokens = grad_mixed + tensor_scatter(
            lambda a, b: times_transposed(grad_qkv[a:b, :width], w_query)
            + times_transposed(grad_qkv[a:b, width : 2 * width], w_key)
            + times_transposed(grad_qkv[a:b, 2 * width :], w_value),
            rows,
        )

        tokens_all = dp_gather_shared(gathered)
        mixed_all = dp_gather_shared(mixed_b)
        grad_ffn_all = dp_gather_shared(grad_ffn)
        swiglus, grad_gates, grad_ups = [[swiglu]], [[grad_gate]], [[grad_up]]
        for j in range(1, dp_size):
            gate_j, up_j, swiglu_j = ffn(mixed_all[j], w_gate, w_up)
            grad_gate_j, grad_up_j = ffn_back(grad_ffn_all[j], w_down, gate_j, up_j)
            swiglus.append([swiglu_j])
            grad_gates.append([grad_gate_j])
            grad_ups.append([grad_up_j])
        (grad_w_down,) = weight_grad(swiglus, grad_ffn_all)
        grad_w_gate, grad_w_up = weight_grad(mixed_all, grad_gates, grad_ups)
        grad_w_out = dp_sum(transposed_times(attended, grad_attn))
        grad_w_query, grad_w_key, grad_w_value = weight_grad(
            tokens_all, dp_gather(grad_qkv), outs=3
        )
        own_gains = jnp.concatenate([post_gains.reshape(-1), gain_parts.reshape(-1)])
        gains = tree_sum([piece for group in dp_gather(own_gains) for piece in group])
        return (
            layer_out,
            grad_tokens,
            grad_w_query,
            grad_w_key,
            grad_w_value,
            grad_w_out,
            grad_w_gate,
            grad_w_up,
            grad_w_down,
            gains[2 * model_width : 2 * model_width + width],
            gains[2 * model_width + width :],
            gains[:model_width],
            gains[model_width : 2 * model_width],
        )

    return shards


def solution(mesh):
    placed = (
        P(("dp", "tensor"), None),
        P(("dp", "tensor"), None),
        P(None, "tensor"),
        P(None, "tensor"),
        P(None, "tensor"),
        P("tensor", None),
        P(None, "tensor"),
        P(None, "tensor"),
        P("tensor", None),
        P("tensor"),
        P("tensor"),
        P(),
        P(),
    )
    return jax.shard_map(
        build(mesh.shape["dp"], mesh.shape["tensor"]),
        mesh=mesh,
        in_specs=placed,
        out_specs=(
            P(("dp", "tensor"), None),
            P(("dp", "tensor"), None),
            P(None, "tensor"),
            P(None, "tensor"),
            P(None, "tensor"),
            P("tensor", None),
            P(None, "tensor"),
            P(None, "tensor"),
            P("tensor", None),
            P("tensor"),
            P("tensor"),
            P(),
            P(),
        ),
        check_vma=False,
    )
```

profile of v0, /device:TPU:0, one launch (start us, length us, event | category | flops | bytes accessed | tf_op | source)
XLA Modules:
  0.0 446.1 jit_solution(512859127787759972)
XLA Ops:
  0.7 3.1 collective-permute-start
  3.8 2.6 collective-permute-start.1
  6.4 8.8 %collective-permute-done.refs_1_ = bf16[64,2048]{1,0:T(8,128)(2,1)S(1)} collective-permute-done((bf16[64,2048]{1,0:T(8,128)(2,1)}, bf16[64,2048]{1,0:T(8,128)(2,1)S(1)}, u32[]{:S(2)}, u32[]{:S(2)}) %collective-permute-start) | collective-permute-done | bytes 262176 | tf_op jit(solution)/shard_map/ppermute | solution.py:539
  15.2 10.1 %collective-permute-done.1.refs_2_ = bf16[64,2048]{1,0:T(8,128)(2,1)S(1)} collective-permute-done((bf16[64,2048]{1,0:T(8,128)(2,1)}, bf16[64,2048]{1,0:T(8,128)(2,1)S(1)}, u32[]{:S(2)}, u32[]{:S(2)}) %collective-permute-start.1) | collective-permute-done | bytes 262176 | tf_op jit(solution)/shard_map/ppermute | solution.py:539
  31.8 1.9 project.1
  35.1 2.5 collective-permute-start.10
  37.5 3.5 collective-permute-start.8
  42.7 2.9 collective-permute-done.9.refs_2_
  45.6 1.9 attend.1
  48.1 2.6 collective-permute-done.11
  51.4 1.9 collective-permute-start.13
  53.3 2.5 collective-permute-start.14
  55.8 8.3 %collective-permute-done.12 = bf16[64,2048]{1,0:T(8,128)(2,1)S(1)} collective-permute-done((bf16[64,2048]{1,0:T(8,128)(2,1)S(1)}, bf16[64,2048]{1,0:T(8,128)(2,1)S(1)}, u32[]{:S(2)}, u32[]{:S(2)}) %collective-permute-start.12) | collective-permute-done | bytes 262176 | tf_op jit(solution)/shard_map/ppermute | solution.py:539
  64.1 8.8 %collective-permute-done.13 = bf16[64,2048]{1,0:T(8,128)(2,1)S(1)} collective-permute-done((bf16[64,2048]{1,0:T(8,128)(2,1)S(1)}, bf16[64,2048]{1,0:T(8,128)(2,1)S(1)}, u32[]{:S(2)}, u32[]{:S(2)}) %collective-permute-start.13) | collective-permute-done | bytes 262176 | tf_op jit(solution)/shard_map/ppermute | solution.py:539
  73.3 5.4 %collective-permute-start.15 = (bf16[64,2048]{1,0:T(8,128)(2,1)S(1)}, bf16[64,2048]{1,0:T(8,128)(2,1)S(1)}, u32[]{:S(2)}, u32[]{:S(2)}) collective-permute-start(bf16[64,2048]{1,0:T(8,128)(2,1)S(1)} %fusion.29.refs_0_), channel_id=1, source_target_pairs={{0,2},{1,3},{2,0},{3,1},{4,6},{5,7},{6,4},{7,5},{8,10},{9,11},{10,... | collective-permute-start | bytes 786440 | tf_op jit(solution)/shard_map/ppermute | solution.py:539
  78.7 2.4 collective-permute-start.17
  81.1 7.3 %collective-permute-done.15.refs_1_ = bf16[64,2048]{1,0:T(8,128)(2,1)S(1)} collective-permute-done((bf16[64,2048]{1,0:T(8,128)(2,1)S(1)}, bf16[64,2048]{1,0:T(8,128)(2,1)S(1)}, u32[]{:S(2)}, u32[]{:S(2)}) %collective-permute-start.15) | collective-permute-done | bytes 262176 | tf_op jit(solution)/shard_map/ppermute | solution.py:539
  88.5 11.5 %collective-permute-done.16.refs_2_ = bf16[64,2048]{1,0:T(8,128)(2,1)S(1)} collective-permute-done((bf16[64,2048]{1,0:T(8,128)(2,1)S(1)}, bf16[64,2048]{1,0:T(8,128)(2,1)S(1)}, u32[]{:S(2)}, u32[]{:S(2)}) %collective-permute-start.16) | collective-permute-done | bytes 262176 | tf_op jit(solution)/shard_map/ppermute | solution.py:539
  101.9 7.1 %ffn.4 = (f32[512,1024]{1,0:T(8,128)S(1)}, f32[512,1024]{1,0:T(8,128)S(1)}, bf16[512,1024]{1,0:T(8,128)(2,1)S(1)}) custom-call(bf16[64,2048]{1,0:T(8,128)(2,1)S(1)} %fusion.29.refs_0_, bf16[64,2048]{1,0:T(8,128)(2,1)S(1)} %collective-permute-done.15.refs_1_, bf16[64,2048]{1,0:T(8,128)(2,1)S(1)} %collective-permute-done.16.refs_2_, ...), custom_call_target="tpu_custom_call" | custom-call | flops 4294967296 | bytes 15728640 | tf_op jit(solution)/shard_map/ffn/pallas_call | solution.py:429
  111.2 2.5 collective-permute-done.22
  115.1 4.0 collective-permute-start.23
  119.0 2.4 collective-permute-start.25
  125.5 4.4 collective-permute-done.23
  130.0 2.4 collective-permute-start.71
  132.4 7.9 %collective-permute-done.24 = bf16[64,2048]{1,0:T(8,128)(2,1)S(1)} collective-permute-done((bf16[64,2048]{1,0:T(8,128)(2,1)S(1)}, bf16[64,2048]{1,0:T(8,128)(2,1)S(1)}, u32[]{:S(2)}, u32[]{:S(2)}) %collective-permute-start.24) | collective-permute-done | bytes 262176 | tf_op jit(solution)/shard_map/ppermute | solution.py:539
  141.1 5.2 %collective-permute-start.26 = (bf16[64,2048]{1,0:T(8,128)(2,1)S(1)}, bf16[64,2048]{1,0:T(8,128)(2,1)}, u32[]{:S(2)}, u32[]{:S(2)}) collective-permute-start(bf16[64,2048]{1,0:T(8,128)(2,1)S(1)} %fusion.10.refs_0_), channel_id=1, source_target_pairs={{0,2},{1,3},{2,0},{3,1},{4,6},{5,7},{6,4},{7,5},{8,10},{9,11},{10,... | collective-permute-start | bytes 786440 | tf_op jit(solution)/shard_map/ppermute | solution.py:539
  146.3 2.6 collective-permute-done.67.refs_0_.refs_5_
  151.0 1.7 constant_dynamic-update-slice_fusion.10
  152.7 18.5 %collective-permute-done.69.refs_0_.refs_7_ = bf16[256,2048]{1,0:T(8,128)(2,1)} collective-permute-done((bf16[256,2048]{1,0:T(8,128)(2,1)}, bf16[256,2048]{1,0:T(8,128)(2,1)}, u32[]{:S(2)}, u32[]{:S(2)}) %collective-permute-start.69) | collective-permute-done | bytes 1048608 | tf_op jit(solution)/shard_map/ppermute | solution.py:539
  172.2 1.7 constant_dynamic-update-slice_fusion.9
  173.9 1.7 constant_dynamic-update-slice_fusion.8.refs_0_
  176.2 2.4 copy-done.2
  178.6 1.6 copy-done.15
  180.1 1.6 copy-done.17
  181.7 5.0 %ffn_back.4 = (bf16[512,1024]{1,0:T(8,128)(2,1)S(1)}, bf16[512,1024]{1,0:T(8,128)(2,1)S(1)}) custom-call(bf16[64,2048]{1,0:T(8,128)(2,1)S(1)} %fusion.10.refs_0_, bf16[64,2048]{1,0:T(8,128)(2,1)} %collective-permute-done.26.refs_1_, bf16[64,2048]{1,0:T(8,128)(2,1)} %collective-permute-done.27.refs_2_, bf16[64,2048]{1,0:T(8,128)(2,1)} %collective-permute-done.28.refs_3_, ...), custom_call_target="tpu_custom_call" | custom-call | flops 2147483648 | bytes 12582912 | tf_op jit(solution)/shard_map/ffn_back/pallas_call | solution.py:463
  188.1 1.6 copy-done.11
  194.3 7.8 %ffn.5 = (f32[512,1024]{1,0:T(8,128)S(1)}, f32[512,1024]{1,0:T(8,128)S(1)}, bf16[512,1024]{1,0:T(8,128)(2,1)S(1)}) custom-call(bf16[256,2048]{1,0:T(8,128)(2,1)} %collective-permute-done.67.refs_0_.refs_5_, bf16[256,2048]{1,0:T(8,128)(2,1)S(1)} %collective-permute-done.68.refs_1_.refs_6_, bf16[2048,1024]{1,0:T(8,128)(2,1)S(1)} %copy-done.11, ...), custom_call_target="tpu_custom_call" | custom-call | flops 4294967296 | bytes 15728640 | tf_op jit(solution)/shard_map/ffn/pallas_call | solution.py:429
  207.0 2.5 collective-permute-start.36
  209.5 7.5 %ffn.6 = (f32[512,1024]{1,0:T(8,128)S(1)}, f32[512,1024]{1,0:T(8,128)S(1)}, bf16[512,1024]{1,0:T(8,128)(2,1)S(1)}) custom-call(bf16[256,2048]{1,0:T(8,128)(2,1)} %collective-permute-done.69.refs_0_.refs_7_, bf16[256,2048]{1,0:T(8,128)(2,1)S(1)} %collective-permute-done.70.refs_1_.refs_8_, bf16[2048,1024]{1,0:T(8,128)(2,1)S(1)} %copy-done.11, ...), custom_call_target="tpu_custom_call" | custom-call | flops 4294967296 | bytes 15728640 | tf_op jit(solution)/shard_map/ffn/pallas_call | solution.py:429
  220.9 6.2 %collective-permute-done.35 = bf16[64,2048]{1,0:T(8,128)(2,1)S(1)} collective-permute-done((bf16[64,2048]{1,0:T(8,128)(2,1)S(1)}, bf16[64,2048]{1,0:T(8,128)(2,1)S(1)}, u32[]{:S(2)}, u32[]{:S(2)}) %collective-permute-start.35) | collective-permute-done | bytes 262176 | tf_op jit(solution)/shard_map/ppermute | solution.py:539
  228.6 5.0 %collective-permute-start.37 = (bf16[64,2048]{1,0:T(8,128)(2,1)S(1)}, bf16[64,2048]{1,0:T(8,128)(2,1)S(1)}, u32[]{:S(2)}, u32[]{:S(2)}) collective-permute-start(bf16[64,2048]{1,0:T(8,128)(2,1)S(1)} %get-tuple-element.98), channel_id=1, source_target_pairs={{0,2},{1,3},{2,0},{3,1},{4,6},{5,7},{6,4},{7,5},{8,10},{9,11},{10,... | collective-permute-start | bytes 786440 | tf_op jit(solution)/shard_map/ppermute | solution.py:539
  234.1 7.7 %ffn.7 = (f32[512,1024]{1,0:T(8,128)S(1)}, f32[512,1024]{1,0:T(8,128)S(1)}, bf16[512,1024]{1,0:T(8,128)(2,1)S(1)}) custom-call(bf16[256,2048]{1,0:T(8,128)(2,1)} %collective-permute-done.71.refs_0_.refs_9_, bf16[256,2048]{1,0:T(8,128)(2,1)S(1)} %collective-permute-done.72.refs_1_.refs_10_, bf16[2048,1024]{1,0:T(8,128)(2,1)S(1)} %copy-done.11, ...), custom_call_target="tpu_custom_call" | custom-call | flops 4294967296 | bytes 15728640 | tf_op jit(solution)/shard_map/ffn/pallas_call | solution.py:429
  243.7 2.2 collective-permute-start.39
  247.2 7.1 %collective-permute-done.39 = bf16[64,2048]{1,0:T(8,128)(2,1)} collective-permute-done((bf16[64,2048]{1,0:T(8,128)(2,1)S(1)}, bf16[64,2048]{1,0:T(8,128)(2,1)}, u32[]{:S(2)}, u32[]{:S(2)}) %collective-permute-start.39) | collective-permute-done | bytes 262176 | tf_op jit(solution)/shard_map/ppermute | solution.py:539
  258.4 3.8 ffn_back.7
  262.8 3.8 ffn_back.6
  267.7 3.8 ffn_back.5
  274.8 24.6 %weight_grad.4 = (f32[2048,1024]{1,0:T(8,128)}, f32[2048,1024]{1,0:T(8,128)}) custom-call(bf16[256,2048]{1,0:T(8,128)(2,1)} %pad_maximum_fusion.refs_0_, bf16[64,2048]{1,0:T(8,128)(2,1)S(1)} %copy-done.64, bf16[64,2048]{1,0:T(8,128)(2,1)S(1)} %copy-done.66, bf16[64,2048]{1,0:T(8,128)(2,1)S(1)} %copy-done.68, bf16[64,2048]{1,0:T(8,128)(2,1)S(1)} %copy-done.70, ...), custom_call_target="tpu_custom_call" | custom-call | flops 17179869184 | bytes 33554432 | tf_op jit(solution)/shard_map/weight_grad/pallas_call | solution.py:511
  301.9 13.7 %weight_grad.5 = f32[1024,2048]{1,0:T(8,128)} custom-call(bf16[512,1024]{1,0:T(8,128)(2,1)S(1)} %copy-done.24, bf16[512,1024]{1,0:T(8,128)(2,1)S(1)} %copy-done.72, bf16[512,1024]{1,0:T(8,128)(2,1)S(1)} %copy-done.74, bf16[512,1024]{1,0:T(8,128)(2,1)S(1)} %copy-done.76, bf16[256,2048]{1,0:T(8,128)(2,1)S(1)} %pad_maximum_fusion.1.refs_4_, ...), custom_call_target="tpu_custom_call" | custom-call | flops 8589934592 | bytes 20971520 | tf_op jit(solution)/shard_map/weight_grad/pallas_call | solution.py:511
  319.5 4.2 attend_back.1
  325.0 4.5 %collective-permute-start.45 = (f32[40,128]{1,0:T(8,128)S(1)}, f32[40,128]{1,0:T(8,128)S(1)}, u32[]{:S(2)}, u32[]{:S(2)}) collective-permute-start(f32[40,128]{1,0:T(8,128)S(1)} %add_blocks.3.refs_0_), channel_id=1, source_target_pairs={{0,2},{1,3},{2,0},{3,1},{4,6},{5,7},{6,4},{7,5},{8,10},{9,11},{10,... | collective-permute-start | bytes 61448 | tf_op jit(solution)/shard_map/ppermute | solution.py:539
  329.6 2.4 collective-permute-start.47
  340.1 17.6 %collective-permute-done.79 = f32[4608]{0:T(1024)S(1)} collective-permute-done((f32[4608]{0:T(1024)S(1)}, f32[4608]{0:T(1024)S(1)}, u32[]{:S(2)}, u32[]{:S(2)}) %collective-permute-start.79) | collective-permute-done | bytes 18464 | tf_op jit(solution)/shard_map/ppermute | solution.py:539
  357.7 2.0 collective-permute-start.81
  366.9 2.4 collective-permute-done.61.refs_1_
  369.3 4.8 %collective-permute-done.62.refs_2_ = bf16[64,2048]{1,0:T(8,128)(2,1)S(1)} collective-permute-done((bf16[64,2048]{1,0:T(8,128)(2,1)S(1)}, bf16[64,2048]{1,0:T(8,128)(2,1)S(1)}, u32[]{:S(2)}, u32[]{:S(2)}) %collective-permute-start.62) | collective-permute-done | bytes 262176 | tf_op jit(solution)/shard_map/ppermute | solution.py:539
  375.6 7.4 %collective-permute-done.64 = bf16[64,2048]{1,0:T(8,128)(2,1)S(1)} collective-permute-done((bf16[64,2048]{1,0:T(8,128)(2,1)S(1)}, bf16[64,2048]{1,0:T(8,128)(2,1)S(1)}, u32[]{:S(2)}, u32[]{:S(2)}) %collective-permute-start.64) | collective-permute-done | bytes 262176 | tf_op jit(solution)/shard_map/ppermute | solution.py:539
  384.5 6.4 %collective-permute-done.65 = bf16[64,2048]{1,0:T(8,128)(2,1)S(1)} collective-permute-done((bf16[64,2048]{1,0:T(8,128)(2,1)S(1)}, bf16[64,2048]{1,0:T(8,128)(2,1)S(1)}, u32[]{:S(2)}, u32[]{:S(2)}) %collective-permute-start.65) | collective-permute-done | bytes 262176 | tf_op jit(solution)/shard_map/ppermute | solution.py:539
  390.9 1.9 collective-permute-start.66
  392.8 6.0 %collective-permute-done.66 = bf16[64,2048]{1,0:T(8,128)(2,1)S(1)} collective-permute-done((bf16[64,2048]{1,0:T(8,128)(2,1)S(1)}, bf16[64,2048]{1,0:T(8,128)(2,1)S(1)}, u32[]{:S(2)}, u32[]{:S(2)}) %collective-permute-start.66) | collective-permute-done | bytes 262176 | tf_op jit(solution)/shard_map/ppermute | solution.py:539
  403.6 1.7 collective-permute-start.50
  405.3 13.9 %collective-permute-done.58.refs_12_ = bf16[512,768]{1,0:T(8,128)(2,1)S(1)} collective-permute-done((bf16[512,768]{1,0:T(8,128)(2,1)S(1)}, bf16[512,768]{1,0:T(8,128)(2,1)S(1)}, u32[]{:S(2)}, u32[]{:S(2)}) %collective-permute-start.58) | collective-permute-done | bytes 786464 | tf_op jit(solution)/shard_map/ppermute | solution.py:539
  420.7 12.2 %collective-permute-done.59.refs_13_ = bf16[512,768]{1,0:T(8,128)(2,1)S(1)} collective-permute-done((bf16[512,768]{1,0:T(8,128)(2,1)S(1)}, bf16[512,768]{1,0:T(8,128)(2,1)S(1)}, u32[]{:S(2)}, u32[]{:S(2)}) %collective-permute-start.59) | collective-permute-done | bytes 786464 | tf_op jit(solution)/shard_map/ppermute | solution.py:539
  434.0 11.0 %weight_grad.3 = (f32[2048,256]{1,0:T(8,128)}, f32[2048,256]{1,0:T(8,128)}, f32[2048,256]{1,0:T(8,128)}) custom-call(bf16[256,2048]{1,0:T(8,128)(2,1)} %constant_dynamic-update-slice_fusion.8.refs_0_, bf16[64,2048]{1,0:T(8,128)(2,1)S(1)} %copy-done.56, bf16[64,2048]{1,0:T(8,128)(2,1)S(1)} %copy-done.58, bf16[64,2048]{1,0:T(8,128)(2,1)S(1)} %copy-done.60, ...), custom_call_target="tpu_custom_call" | custom-call | flops 6442450944 | bytes 17825792 | tf_op jit(solution)/shard_map/weight_grad/pallas_call | solution.py:511
  (365 shorter events, 87.3 us)
Async XLA Ops:
  0.7 14.5 %collective-permute-start = (bf16[64,2048]{1,0:T(8,128)(2,1)}, bf16[64,2048]{1,0:T(8,128)(2,1)S(1)}, u32[]{:S(2)}, u32[]{:S(2)}) collective-permute-start(bf16[64,2048]{1,0:T(8,128)(2,1)} %refs_0_.1), channel_id=1, source_target_pairs={{0,2},{1,3},{2,0},{3,1},{4,6},{5,7},{6,4},{7,5},{8,10},{9,11},{10,... | collective-permute-start | bytes 786440 | tf_op jit(solution)/shard_map/ppermute | solution.py:539
  3.8 21.5 %collective-permute-start.1 = (bf16[64,2048]{1,0:T(8,128)(2,1)}, bf16[64,2048]{1,0:T(8,128)(2,1)S(1)}, u32[]{:S(2)}, u32[]{:S(2)}) collective-permute-start(bf16[64,2048]{1,0:T(8,128)(2,1)} %refs_0_.1), channel_id=1, source_target_pairs={{0,4},{1,5},{2,6},{3,7},{4,0},{5,1},{6,2},{7,3},{8,12},{9,13},{10,... | collective-permute-start | bytes 786440 | tf_op jit(solution)/shard_map/ppermute | solution.py:539
  6.4 18.9 %collective-permute-start.2 = (bf16[64,2048]{1,0:T(8,128)(2,1)}, bf16[64,2048]{1,0:T(8,128)(2,1)S(1)}, u32[]{:S(2)}, u32[]{:S(2)}) collective-permute-start(bf16[64,2048]{1,0:T(8,128)(2,1)} %refs_0_.1), channel_id=1, source_target_pairs={{0,6},{1,7},{2,4},{3,5},{4,2},{5,3},{6,0},{7,1},{8,14},{9,15},{10,... | collective-permute-start | bytes 786440 | tf_op jit(solution)/shard_map/ppermute | solution.py:539
  6.4 20.5 %collective-permute-start.3 = (bf16[64,2048]{1,0:T(8,128)(2,1)}, bf16[64,2048]{1,0:T(8,128)(2,1)S(1)}, u32[]{:S(2)}, u32[]{:S(2)}) collective-permute-start(bf16[64,2048]{1,0:T(8,128)(2,1)} %refs_0_.1), channel_id=1, source_target_pairs={{0,1},{1,0},{2,3},{3,2},{4,5},{5,4},{6,7},{7,6},{8,9},{9,8},{10,11... | collective-permute-start | bytes 786440 | tf_op jit(solution)/shard_map/ppermute | solution.py:539
  15.2 11.7 %collective-permute-start.4 = (bf16[64,2048]{1,0:T(8,128)(2,1)S(1)}, bf16[64,2048]{1,0:T(8,128)(2,1)S(1)}, u32[]{:S(2)}, u32[]{:S(2)}) collective-permute-start(bf16[64,2048]{1,0:T(8,128)(2,1)S(1)} %collective-permute-done.refs_1_), channel_id=1, source_target_pairs={{0,1},{1,0},{2,3},{3,2},{4,5},{5,4},{6,7},{7,6},{8,9},{9,8},{10,11... | collective-permute-start | bytes 786440 | tf_op jit(solution)/shard_map/ppermute | solution.py:539
  51.3 12.7 %collective-permute-start.12 = (bf16[64,2048]{1,0:T(8,128)(2,1)S(1)}, bf16[64,2048]{1,0:T(8,128)(2,1)S(1)}, u32[]{:S(2)}, u32[]{:S(2)}) collective-permute-start(bf16[64,2048]{1,0:T(8,128)(2,1)S(1)} %get-tuple-element.116), channel_id=1, source_target_pairs={{0,2},{1,3},{2,0},{3,1},{4,6},{5,7},{6,4},{7,5},{8,10},{9,11},{10,... | collective-permute-start | bytes 786440 | tf_op jit(solution)/shard_map/ppermute | solution.py:539
  51.4 21.4 %collective-permute-start.13 = (bf16[64,2048]{1,0:T(8,128)(2,1)S(1)}, bf16[64,2048]{1,0:T(8,128)(2,1)S(1)}, u32[]{:S(2)}, u32[]{:S(2)}) collective-permute-start(bf16[64,2048]{1,0:T(8,128)(2,1)S(1)} %get-tuple-element.118), channel_id=1, source_target_pairs={{0,4},{1,5},{2,6},{3,7},{4,0},{5,1},{6,2},{7,3},{8,12},{9,13},{10,... | collective-permute-start | bytes 786440 | tf_op jit(solution)/shard_map/ppermute | solution.py:539
  53.3 19.5 %collective-permute-start.14 = (bf16[64,2048]{1,0:T(8,128)(2,1)S(1)}, bf16[64,2048]{1,0:T(8,128)(2,1)S(1)}, u32[]{:S(2)}, u32[]{:S(2)}) collective-permute-start(bf16[64,2048]{1,0:T(8,128)(2,1)S(1)} %get-tuple-element.117), channel_id=1, source_target_pairs={{0,6},{1,7},{2,4},{3,5},{4,2},{5,3},{6,0},{7,1},{8,14},{9,15},{10,... | collective-permute-start | bytes 786440 | tf_op jit(solution)/shard_map/ppermute | solution.py:539
  73.3 15.2 %collective-permute-start.15 = (bf16[64,2048]{1,0:T(8,128)(2,1)S(1)}, bf16[64,2048]{1,0:T(8,128)(2,1)S(1)}, u32[]{:S(2)}, u32[]{:S(2)}) collective-permute-start(bf16[64,2048]{1,0:T(8,128)(2,1)S(1)} %fusion.29.refs_0_), channel_id=1, source_target_pairs={{0,2},{1,3},{2,0},{3,1},{4,6},{5,7},{6,4},{7,5},{8,10},{9,11},{10,... | collective-permute-start | bytes 786440 | tf_op jit(solution)/shard_map/ppermute | solution.py:539
  78.7 21.3 %collective-permute-start.16 = (bf16[64,2048]{1,0:T(8,128)(2,1)S(1)}, bf16[64,2048]{1,0:T(8,128)(2,1)S(1)}, u32[]{:S(2)}, u32[]{:S(2)}) collective-permute-start(bf16[64,2048]{1,0:T(8,128)(2,1)S(1)} %fusion.29.refs_0_), channel_id=1, source_target_pairs={{0,4},{1,5},{2,6},{3,7},{4,0},{5,1},{6,2},{7,3},{8,12},{9,13},{10,... | collective-permute-start | bytes 786440 | tf_op jit(solution)/shard_map/ppermute | solution.py:539
  78.7 21.3 %collective-permute-start.17 = (bf16[64,2048]{1,0:T(8,128)(2,1)S(1)}, bf16[64,2048]{1,0:T(8,128)(2,1)S(1)}, u32[]{:S(2)}, u32[]{:S(2)}) collective-permute-start(bf16[64,2048]{1,0:T(8,128)(2,1)S(1)} %fusion.29.refs_0_), channel_id=1, source_target_pairs={{0,6},{1,7},{2,4},{3,5},{4,2},{5,3},{6,0},{7,1},{8,14},{9,15},{10,... | collective-permute-start | bytes 786440 | tf_op jit(solution)/shard_map/ppermute | solution.py:539
  81.1 19.4 %collective-permute-start.18 = (bf16[64,2048]{1,0:T(8,128)(2,1)S(1)}, bf16[64,2048]{1,0:T(8,128)(2,1)S(1)}, u32[]{:S(2)}, u32[]{:S(2)}) collective-permute-start(bf16[64,2048]{1,0:T(8,128)(2,1)S(1)} %fusion.29.refs_0_), channel_id=1, source_target_pairs={{0,1},{1,0},{2,3},{3,2},{4,5},{5,4},{6,7},{7,6},{8,9},{9,8},{10,11... | collective-permute-start | bytes 786440 | tf_op jit(solution)/shard_map/ppermute | solution.py:539
  88.5 12.1 %collective-permute-start.19 = (bf16[64,2048]{1,0:T(8,128)(2,1)S(1)}, bf16[64,2048]{1,0:T(8,128)(2,1)S(1)}, u32[]{:S(2)}, u32[]{:S(2)}) collective-permute-start(bf16[64,2048]{1,0:T(8,128)(2,1)S(1)} %collective-permute-done.15.refs_1_), channel_id=1, source_target_pairs={{0,1},{1,0},{2,3},{3,2},{4,5},{5,4},{6,7},{7,6},{8,9},{9,8},{10,11... | collective-permute-start | bytes 786440 | tf_op jit(solution)/shard_map/ppermute | solution.py:539
  115.1 14.9 %collective-permute-start.23 = (bf16[64,2048]{1,0:T(8,128)(2,1)S(1)}, bf16[64,2048]{1,0:T(8,128)(2,1)S(1)}, u32[]{:S(2)}, u32[]{:S(2)}) collective-permute-start(bf16[64,2048]{1,0:T(8,128)(2,1)S(1)} %get-tuple-element.113), channel_id=1, source_target_pairs={{0,2},{1,3},{2,0},{3,1},{4,6},{5,7},{6,4},{7,5},{8,10},{9,11},{10,... | collective-permute-start | bytes 786440 | tf_op jit(solution)/shard_map/ppermute | solution.py:539
  119.0 21.3 %collective-permute-start.24 = (bf16[64,2048]{1,0:T(8,128)(2,1)S(1)}, bf16[64,2048]{1,0:T(8,128)(2,1)S(1)}, u32[]{:S(2)}, u32[]{:S(2)}) collective-permute-start(bf16[64,2048]{1,0:T(8,128)(2,1)S(1)} %get-tuple-element.115), channel_id=1, source_target_pairs={{0,4},{1,5},{2,6},{3,7},{4,0},{5,1},{6,2},{7,3},{8,12},{9,13},{10,... | collective-permute-start | bytes 786440 | tf_op jit(solution)/shard_map/ppermute | solution.py:539
  119.0 21.3 %collective-permute-start.25 = (bf16[64,2048]{1,0:T(8,128)(2,1)S(1)}, bf16[64,2048]{1,0:T(8,128)(2,1)S(1)}, u32[]{:S(2)}, u32[]{:S(2)}) collective-permute-start(bf16[64,2048]{1,0:T(8,128)(2,1)S(1)} %get-tuple-element.114), channel_id=1, source_target_pairs={{0,6},{1,7},{2,4},{3,5},{4,2},{5,3},{6,0},{7,1},{8,14},{9,15},{10,... | collective-permute-start | bytes 786440 | tf_op jit(solution)/shard_map/ppermute | solution.py:539
  122.5 26.3 %collective-permute-start.67 = (bf16[256,2048]{1,0:T(8,128)(2,1)}, bf16[256,2048]{1,0:T(8,128)(2,1)}, u32[]{:S(2)}, u32[]{:S(2)}) collective-permute-start(bf16[256,2048]{1,0:T(8,128)(2,1)} %pad_maximum_fusion.refs_0_), channel_id=1, source_target_pairs={{0,8},{8,0},{16,24},{24,16},{1,9},{9,1},{17,25},{25,17},{2,10},{10... | collective-permute-start | bytes 3145736 | tf_op jit(solution)/shard_map/ppermute | solution.py:539
  124.0 47.1 %collective-permute-start.69 = (bf16[256,2048]{1,0:T(8,128)(2,1)}, bf16[256,2048]{1,0:T(8,128)(2,1)}, u32[]{:S(2)}, u32[]{:S(2)}) collective-permute-start(bf16[256,2048]{1,0:T(8,128)(2,1)} %pad_maximum_fusion.refs_0_), channel_id=1, source_target_pairs={{0,16},{8,24},{16,0},{24,8},{1,17},{9,25},{17,1},{25,9},{2,18},{10... | collective-permute-start | bytes 3145736 | tf_op jit(solution)/shard_map/ppermute | solution.py:539
  130.0 45.6 %collective-permute-start.71 = (bf16[256,2048]{1,0:T(8,128)(2,1)}, bf16[256,2048]{1,0:T(8,128)(2,1)}, u32[]{:S(2)}, u32[]{:S(2)}) collective-permute-start(bf16[256,2048]{1,0:T(8,128)(2,1)} %pad_maximum_fusion.refs_0_), channel_id=1, source_target_pairs={{0,24},{8,16},{16,8},{24,0},{1,25},{9,17},{17,9},{25,1},{2,26},{10... | collective-permute-start | bytes 3145736 | tf_op jit(solution)/shard_map/ppermute | solution.py:539
  141.1 30.1 %collective-permute-start.26 = (bf16[64,2048]{1,0:T(8,128)(2,1)S(1)}, bf16[64,2048]{1,0:T(8,128)(2,1)}, u32[]{:S(2)}, u32[]{:S(2)}) collective-permute-start(bf16[64,2048]{1,0:T(8,128)(2,1)S(1)} %fusion.10.refs_0_), channel_id=1, source_target_pairs={{0,2},{1,3},{2,0},{3,1},{4,6},{5,7},{6,4},{7,5},{8,10},{9,11},{10,... | collective-permute-start | bytes 786440 | tf_op jit(solution)/shard_map/ppermute | solution.py:539
  146.3 25.4 %collective-permute-start.27 = (bf16[64,2048]{1,0:T(8,128)(2,1)S(1)}, bf16[64,2048]{1,0:T(8,128)(2,1)}, u32[]{:S(2)}, u32[]{:S(2)}) collective-permute-start(bf16[64,2048]{1,0:T(8,128)(2,1)S(1)} %fusion.10.refs_0_), channel_id=1, source_target_pairs={{0,4},{1,5},{2,6},{3,7},{4,0},{5,1},{6,2},{7,3},{8,12},{9,13},{10,... | collective-permute-start | bytes 786440 | tf_op jit(solution)/shard_map/ppermute | solution.py:539
  148.9 22.9 %collective-permute-start.28 = (bf16[64,2048]{1,0:T(8,128)(2,1)S(1)}, bf16[64,2048]{1,0:T(8,128)(2,1)}, u32[]{:S(2)}, u32[]{:S(2)}) collective-permute-start(bf16[64,2048]{1,0:T(8,128)(2,1)S(1)} %fusion.10.refs_0_), channel_id=1, source_target_pairs={{0,6},{1,7},{2,4},{3,5},{4,2},{5,3},{6,0},{7,1},{8,14},{9,15},{10,... | collective-permute-start | bytes 786440 | tf_op jit(solution)/shard_map/ppermute | solution.py:539
  175.6 18.8 %collective-permute-start.68 = (bf16[256,2048]{1,0:T(8,128)(2,1)}, bf16[256,2048]{1,0:T(8,128)(2,1)S(1)}, u32[]{:S(2)}, u32[]{:S(2)}) collective-permute-start(bf16[256,2048]{1,0:T(8,128)(2,1)} %collective-permute-done.67.refs_0_.refs_5_), channel_id=1, source_target_pairs={{0,1},{1,0},{2,3},{3,2},{4,5},{5,4},{6,7},{7,6},{8,9},{9,8},{10,11... | collective-permute-start | bytes 3145736 | tf_op jit(solution)/shard_map/ppermute | solution.py:539
  175.6 31.3 %collective-permute-start.70 = (bf16[256,2048]{1,0:T(8,128)(2,1)}, bf16[256,2048]{1,0:T(8,128)(2,1)S(1)}, u32[]{:S(2)}, u32[]{:S(2)}) collective-permute-start(bf16[256,2048]{1,0:T(8,128)(2,1)} %collective-permute-done.69.refs_0_.refs_7_), channel_id=1, source_target_pairs={{0,1},{1,0},{2,3},{3,2},{4,5},{5,4},{6,7},{7,6},{8,9},{9,8},{10,11... | collective-permute-start | bytes 3145736 | tf_op jit(solution)/shard_map/ppermute | solution.py:539
  176.1 57.6 %collective-permute-start.72 = (bf16[256,2048]{1,0:T(8,128)(2,1)}, bf16[256,2048]{1,0:T(8,128)(2,1)S(1)}, u32[]{:S(2)}, u32[]{:S(2)}) collective-permute-start(bf16[256,2048]{1,0:T(8,128)(2,1)} %collective-permute-done.71.refs_0_.refs_9_), channel_id=1, source_target_pairs={{0,1},{1,0},{2,3},{3,2},{4,5},{5,4},{6,7},{7,6},{8,9},{9,8},{10,11... | collective-permute-start | bytes 3145736 | tf_op jit(solution)/shard_map/ppermute | solution.py:539
  191.1 12.4 %collective-permute-start.33 = (bf16[256,2048]{1,0:T(8,128)(2,1)S(1)}, bf16[256,2048]{1,0:T(8,128)(2,1)S(1)}, u32[]{:S(2)}, u32[]{:S(2)}) collective-permute-start(bf16[256,2048]{1,0:T(8,128)(2,1)S(1)} %fusion.5), channel_id=1, source_target_pairs={{0,1},{1,0},{2,3},{3,2},{4,5},{5,4},{6,7},{7,6},{8,9},{9,8},{10,11... | collective-permute-start | bytes 3145736 | tf_op jit(solution)/shard_map/ppermute | solution.py:539
  192.8 26.1 %collective-permute-start.77 = (bf16[256,2048]{1,0:T(8,128)(2,1)S(1)}, bf16[256,2048]{1,0:T(8,128)(2,1)S(1)}, u32[]{:S(2)}, u32[]{:S(2)}) collective-permute-start(bf16[256,2048]{1,0:T(8,128)(2,1)S(1)} %pad_maximum_fusion.1.refs_4_), channel_id=1, source_target_pairs={{0,24},{8,16},{16,8},{24,0},{1,25},{9,17},{17,9},{25,1},{2,26},{10... | collective-permute-start | bytes 3145736 | tf_op jit(solution)/shard_map/ppermute | solution.py:539
  204.9 14.6 %collective-permute-start.34 = (bf16[64,2048]{1,0:T(8,128)(2,1)S(1)}, bf16[64,2048]{1,0:T(8,128)(2,1)S(1)}, u32[]{:S(2)}, u32[]{:S(2)}) collective-permute-start(bf16[64,2048]{1,0:T(8,128)(2,1)S(1)} %get-tuple-element.110), channel_id=1, source_target_pairs={{0,2},{1,3},{2,0},{3,1},{4,6},{5,7},{6,4},{7,5},{8,10},{9,11},{10,... | collective-permute-start | bytes 786440 | tf_op jit(solution)/shard_map/ppermute | solution.py:539
  205.8 21.3 %collective-permute-start.35 = (bf16[64,2048]{1,0:T(8,128)(2,1)S(1)}, bf16[64,2048]{1,0:T(8,128)(2,1)S(1)}, u32[]{:S(2)}, u32[]{:S(2)}) collective-permute-start(bf16[64,2048]{1,0:T(8,128)(2,1)S(1)} %get-tuple-element.112), channel_id=1, source_target_pairs={{0,4},{1,5},{2,6},{3,7},{4,0},{5,1},{6,2},{7,3},{8,12},{9,13},{10,... | collective-permute-start | bytes 786440 | tf_op jit(solution)/shard_map/ppermute | solution.py:539
  207.0 20.1 %collective-permute-start.36 = (bf16[64,2048]{1,0:T(8,128)(2,1)S(1)}, bf16[64,2048]{1,0:T(8,128)(2,1)S(1)}, u32[]{:S(2)}, u32[]{:S(2)}) collective-permute-start(bf16[64,2048]{1,0:T(8,128)(2,1)S(1)} %get-tuple-element.111), channel_id=1, source_target_pairs={{0,6},{1,7},{2,4},{3,5},{4,2},{5,3},{6,0},{7,1},{8,14},{9,15},{10,... | collective-permute-start | bytes 786440 | tf_op jit(solution)/shard_map/ppermute | solution.py:539
  218.9 24.3 %collective-permute-start.73 = (bf16[256,2048]{1,0:T(8,128)(2,1)S(1)}, bf16[256,2048]{1,0:T(8,128)(2,1)S(1)}, u32[]{:S(2)}, u32[]{:S(2)}) collective-permute-start(bf16[256,2048]{1,0:T(8,128)(2,1)S(1)} %pad_maximum_fusion.1.refs_4_), channel_id=1, source_target_pairs={{0,8},{8,0},{16,24},{24,16},{1,9},{9,1},{17,25},{25,17},{2,10},{10... | collective-permute-start | bytes 3145736 | tf_op jit(solution)/shard_map/ppermute | solution.py:539
  219.5 24.0 %collective-permute-start.75 = (bf16[256,2048]{1,0:T(8,128)(2,1)S(1)}, bf16[256,2048]{1,0:T(8,128)(2,1)S(1)}, u32[]{:S(2)}, u32[]{:S(2)}) collective-permute-start(bf16[256,2048]{1,0:T(8,128)(2,1)S(1)} %pad_maximum_fusion.1.refs_4_), channel_id=1, source_target_pairs={{0,16},{8,24},{16,0},{24,8},{1,17},{9,25},{17,1},{25,9},{2,18},{10... | collective-permute-start | bytes 3145736 | tf_op jit(solution)/shard_map/ppermute | solution.py:539
  227.1 31.1 %collective-permute-start.78 = (bf16[256,2048]{1,0:T(8,128)(2,1)S(1)}, bf16[256,2048]{1,0:T(8,128)(2,1)S(1)}, u32[]{:S(2)}, u32[]{:S(2)}) collective-permute-start(bf16[256,2048]{1,0:T(8,128)(2,1)S(1)} %collective-permute-done.77.refs_0_.refs_13_), channel_id=1, source_target_pairs={{0,1},{1,0},{2,3},{3,2},{4,5},{5,4},{6,7},{7,6},{8,9},{9,8},{10,11... | collective-permute-start | bytes 3145736 | tf_op jit(solution)/shard_map/ppermute | solution.py:539
  228.6 15.1 %collective-permute-start.37 = (bf16[64,2048]{1,0:T(8,128)(2,1)S(1)}, bf16[64,2048]{1,0:T(8,128)(2,1)S(1)}, u32[]{:S(2)}, u32[]{:S(2)}) collective-permute-start(bf16[64,2048]{1,0:T(8,128)(2,1)S(1)} %get-tuple-element.98), channel_id=1, source_target_pairs={{0,2},{1,3},{2,0},{3,1},{4,6},{5,7},{6,4},{7,5},{8,10},{9,11},{10,... | collective-permute-start | bytes 786440 | tf_op jit(solution)/shard_map/ppermute | solution.py:539
  233.7 13.5 %collective-permute-start.38 = (bf16[64,2048]{1,0:T(8,128)(2,1)S(1)}, bf16[64,2048]{1,0:T(8,128)(2,1)S(1)}, u32[]{:S(2)}, u32[]{:S(2)}) collective-permute-start(bf16[64,2048]{1,0:T(8,128)(2,1)S(1)} %get-tuple-element.98), channel_id=1, source_target_pairs={{0,4},{1,5},{2,6},{3,7},{4,0},{5,1},{6,2},{7,3},{8,12},{9,13},{10,... | collective-permute-start | bytes 786440 | tf_op jit(solution)/shard_map/ppermute | solution.py:539
  243.2 24.5 %collective-permute-start.74 = (bf16[256,2048]{1,0:T(8,128)(2,1)S(1)}, bf16[256,2048]{1,0:T(8,128)(2,1)S(1)}, u32[]{:S(2)}, u32[]{:S(2)}) collective-permute-start(bf16[256,2048]{1,0:T(8,128)(2,1)S(1)} %collective-permute-done.73.refs_0_.refs_9_), channel_id=1, source_target_pairs={{0,1},{1,0},{2,3},{3,2},{4,5},{5,4},{6,7},{7,6},{8,9},{9,8},{10,11... | collective-permute-start | bytes 3145736 | tf_op jit(solution)/shard_map/ppermute | solution.py:539
  243.5 18.7 %collective-permute-start.76 = (bf16[256,2048]{1,0:T(8,128)(2,1)S(1)}, bf16[256,2048]{1,0:T(8,128)(2,1)S(1)}, u32[]{:S(2)}, u32[]{:S(2)}) collective-permute-start(bf16[256,2048]{1,0:T(8,128)(2,1)S(1)} %collective-permute-done.75.refs_0_.refs_11_), channel_id=1, source_target_pairs={{0,1},{1,0},{2,3},{3,2},{4,5},{5,4},{6,7},{7,6},{8,9},{9,8},{10,11... | collective-permute-start | bytes 3145736 | tf_op jit(solution)/shard_map/ppermute | solution.py:539
  243.7 10.6 %collective-permute-start.39 = (bf16[64,2048]{1,0:T(8,128)(2,1)S(1)}, bf16[64,2048]{1,0:T(8,128)(2,1)}, u32[]{:S(2)}, u32[]{:S(2)}) collective-permute-start(bf16[64,2048]{1,0:T(8,128)(2,1)S(1)} %get-tuple-element.98), channel_id=1, source_target_pairs={{0,6},{1,7},{2,4},{3,5},{4,2},{5,3},{6,0},{7,1},{8,14},{9,15},{10,... | collective-permute-start | bytes 786440 | tf_op jit(solution)/shard_map/ppermute | solution.py:539
  247.2 9.5 %collective-permute-start.40 = (bf16[64,2048]{1,0:T(8,128)(2,1)S(1)}, bf16[64,2048]{1,0:T(8,128)(2,1)S(1)}, u32[]{:S(2)}, u32[]{:S(2)}) collective-permute-start(bf16[64,2048]{1,0:T(8,128)(2,1)S(1)} %get-tuple-element.98), channel_id=1, source_target_pairs={{0,1},{1,0},{2,3},{3,2},{4,5},{5,4},{6,7},{7,6},{8,9},{9,8},{10,11... | collective-permute-start | bytes 786440 | tf_op jit(solution)/shard_map/ppermute | solution.py:539
  254.2 109.8 %collective-permute-start.52 = (bf16[256,2048]{1,0:T(8,128)(2,1)}, bf16[256,2048]{1,0:T(8,128)(2,1)}, u32[]{:S(2)}, u32[]{:S(2)}) collective-permute-start(bf16[256,2048]{1,0:T(8,128)(2,1)} %constant_dynamic-update-slice_fusion.8.refs_0_), channel_id=1, source_target_pairs={{0,8},{8,0},{16,24},{24,16},{1,9},{9,1},{17,25},{25,17},{2,10},{10... | collective-permute-start | bytes 3145736 | tf_op jit(solution)/shard_map/ppermute | solution.py:539
  256.6 109.8 %collective-permute-start.54 = (bf16[256,2048]{1,0:T(8,128)(2,1)}, bf16[256,2048]{1,0:T(8,128)(2,1)}, u32[]{:S(2)}, u32[]{:S(2)}) collective-permute-start(bf16[256,2048]{1,0:T(8,128)(2,1)} %constant_dynamic-update-slice_fusion.8.refs_0_), channel_id=1, source_target_pairs={{0,16},{8,24},{16,0},{24,8},{1,17},{9,25},{17,1},{25,9},{2,18},{10... | collective-permute-start | bytes 3145736 | tf_op jit(solution)/shard_map/ppermute | solution.py:539
  258.3 57.3 %collective-permute-start.41 = (bf16[64,2048]{1,0:T(8,128)(2,1)S(1)}, bf16[64,2048]{1,0:T(8,128)(2,1)}, u32[]{:S(2)}, u32[]{:S(2)}) collective-permute-start(bf16[64,2048]{1,0:T(8,128)(2,1)S(1)} %collective-permute-done.37), channel_id=1, source_target_pairs={{0,1},{1,0},{2,3},{3,2},{4,5},{5,4},{6,7},{7,6},{8,9},{9,8},{10,11... | collective-permute-start | bytes 786440 | tf_op jit(solution)/shard_map/ppermute | solution.py:539
  262.2 54.3 %collective-permute-start.42 = (bf16[64,2048]{1,0:T(8,128)(2,1)S(1)}, bf16[64,2048]{1,0:T(8,128)(2,1)}, u32[]{:S(2)}, u32[]{:S(2)}) collective-permute-start(bf16[64,2048]{1,0:T(8,128)(2,1)S(1)} %collective-permute-done.38), channel_id=1, source_target_pairs={{0,1},{1,0},{2,3},{3,2},{4,5},{5,4},{6,7},{7,6},{8,9},{9,8},{10,11... | collective-permute-start | bytes 786440 | tf_op jit(solution)/shard_map/ppermute | solution.py:539
  267.6 49.9 %collective-permute-start.43 = (bf16[64,2048]{1,0:T(8,128)(2,1)}, bf16[64,2048]{1,0:T(8,128)(2,1)S(1)}, u32[]{:S(2)}, u32[]{:S(2)}) collective-permute-start(bf16[64,2048]{1,0:T(8,128)(2,1)} %collective-permute-done.39), channel_id=1, source_target_pairs={{0,1},{1,0},{2,3},{3,2},{4,5},{5,4},{6,7},{7,6},{8,9},{9,8},{10,11... | collective-permute-start | bytes 786440 | tf_op jit(solution)/shard_map/ppermute | solution.py:539
  325.0 7.0 %collective-permute-start.45 = (f32[40,128]{1,0:T(8,128)S(1)}, f32[40,128]{1,0:T(8,128)S(1)}, u32[]{:S(2)}, u32[]{:S(2)}) collective-permute-start(f32[40,128]{1,0:T(8,128)S(1)} %add_blocks.3.refs_0_), channel_id=1, source_target_pairs={{0,2},{1,3},{2,0},{3,1},{4,6},{5,7},{6,4},{7,5},{8,10},{9,11},{10,... | collective-permute-start | bytes 61448 | tf_op jit(solution)/shard_map/ppermute | solution.py:539
  332.1 34.4 %collective-permute-start.56 = (bf16[256,2048]{1,0:T(8,128)(2,1)}, bf16[256,2048]{1,0:T(8,128)(2,1)S(1)}, u32[]{:S(2)}, u32[]{:S(2)}) collective-permute-start(bf16[256,2048]{1,0:T(8,128)(2,1)} %constant_dynamic-update-slice_fusion.8.refs_0_), channel_id=1, source_target_pairs={{0,24},{8,16},{16,8},{24,0},{1,25},{9,17},{17,9},{25,1},{2,26},{10... | collective-permute-start | bytes 3145736 | tf_op jit(solution)/shard_map/ppermute | solution.py:539
  335.6 22.0 %collective-permute-start.79 = (f32[4608]{0:T(1024)S(1)}, f32[4608]{0:T(1024)S(1)}, u32[]{:S(2)}, u32[]{:S(2)}) collective-permute-start(f32[4608]{0:T(1024)S(1)} %pad_maximum_fusion.5), channel_id=1, source_target_pairs={{0,8},{8,0},{16,24},{24,16},{1,9},{9,1},{17,25},{25,17},{2,10},{10... | collective-permute-start | bytes 55304 | tf_op jit(solution)/shard_map/ppermute | solution.py:539
  336.7 23.4 %collective-permute-start.80 = (f32[4608]{0:T(1024)S(1)}, f32[4608]{0:T(1024)S(1)}, u32[]{:S(2)}, u32[]{:S(2)}) collective-permute-start(f32[4608]{0:T(1024)S(1)} %pad_maximum_fusion.5), channel_id=1, source_target_pairs={{0,16},{8,24},{16,0},{24,8},{1,17},{9,25},{17,1},{25,9},{2,18},{10... | collective-permute-start | bytes 55304 | tf_op jit(solution)/shard_map/ppermute | solution.py:539
  360.1 9.2 %collective-permute-start.61 = (bf16[64,2048]{1,0:T(8,128)(2,1)S(1)}, bf16[64,2048]{1,0:T(8,128)(2,1)S(1)}, u32[]{:S(2)}, u32[]{:S(2)}) collective-permute-start(bf16[64,2048]{1,0:T(8,128)(2,1)S(1)} %get-tuple-element.106), channel_id=1, source_target_pairs={{0,8},{8,0},{16,24},{24,16},{1,9},{9,1},{17,25},{25,17},{2,10},{10... | collective-permute-start | bytes 786440 | tf_op jit(solution)/shard_map/ppermute | solution.py:539
  362.6 11.6 %collective-permute-start.62 = (bf16[64,2048]{1,0:T(8,128)(2,1)S(1)}, bf16[64,2048]{1,0:T(8,128)(2,1)S(1)}, u32[]{:S(2)}, u32[]{:S(2)}) collective-permute-start(bf16[64,2048]{1,0:T(8,128)(2,1)S(1)} %get-tuple-element.105), channel_id=1, source_target_pairs={{0,16},{8,24},{16,0},{24,8},{1,17},{9,25},{17,1},{25,9},{2,18},{10... | collective-permute-start | bytes 786440 | tf_op jit(solution)/shard_map/ppermute | solution.py:539
  364.1 10.1 %collective-permute-start.63 = (bf16[64,2048]{1,0:T(8,128)(2,1)S(1)}, bf16[64,2048]{1,0:T(8,128)(2,1)S(1)}, u32[]{:S(2)}, u32[]{:S(2)}) collective-permute-start(bf16[64,2048]{1,0:T(8,128)(2,1)S(1)} %get-tuple-element.104), channel_id=1, source_target_pairs={{0,24},{8,16},{16,8},{24,0},{1,25},{9,17},{17,9},{25,1},{2,26},{10... | collective-permute-start | bytes 786440 | tf_op jit(solution)/shard_map/ppermute | solution.py:539
  366.4 33.5 %collective-permute-start.53 = (bf16[256,2048]{1,0:T(8,128)(2,1)}, bf16[256,2048]{1,0:T(8,128)(2,1)S(1)}, u32[]{:S(2)}, u32[]{:S(2)}) collective-permute-start(bf16[256,2048]{1,0:T(8,128)(2,1)} %collective-permute-done.52.refs_5_), channel_id=1, source_target_pairs={{0,1},{1,0},{2,3},{3,2},{4,5},{5,4},{6,7},{7,6},{8,9},{9,8},{10,11... | collective-permute-start | bytes 3145736 | tf_op jit(solution)/shard_map/ppermute | solution.py:539
  366.4 36.7 %collective-permute-start.55 = (bf16[256,2048]{1,0:T(8,128)(2,1)}, bf16[256,2048]{1,0:T(8,128)(2,1)S(1)}, u32[]{:S(2)}, u32[]{:S(2)}) collective-permute-start(bf16[256,2048]{1,0:T(8,128)(2,1)} %collective-permute-done.54.refs_7_), channel_id=1, source_target_pairs={{0,1},{1,0},{2,3},{3,2},{4,5},{5,4},{6,7},{7,6},{8,9},{9,8},{10,11... | collective-permute-start | bytes 3145736 | tf_op jit(solution)/shard_map/ppermute | solution.py:539
  369.3 34.3 %collective-permute-start.57 = (bf16[256,2048]{1,0:T(8,128)(2,1)S(1)}, bf16[256,2048]{1,0:T(8,128)(2,1)S(1)}, u32[]{:S(2)}, u32[]{:S(2)}) collective-permute-start(bf16[256,2048]{1,0:T(8,128)(2,1)S(1)} %collective-permute-done.56.refs_9_), channel_id=1, source_target_pairs={{0,1},{1,0},{2,3},{3,2},{4,5},{5,4},{6,7},{7,6},{8,9},{9,8},{10,11... | collective-permute-start | bytes 3145736 | tf_op jit(solution)/shard_map/ppermute | solution.py:539
  374.1 27.3 %collective-permute-start.48 = (bf16[256,2048]{1,0:T(8,128)(2,1)S(1)}, bf16[256,2048]{1,0:T(8,128)(2,1)S(1)}, u32[]{:S(2)}, u32[]{:S(2)}) collective-permute-start(bf16[256,2048]{1,0:T(8,128)(2,1)S(1)} %fusion.4), channel_id=1, source_target_pairs={{0,1},{1,0},{2,3},{3,2},{4,5},{5,4},{6,7},{7,6},{8,9},{9,8},{10,11... | collective-permute-start | bytes 3145736 | tf_op jit(solution)/shard_map/ppermute | solution.py:539
  374.3 8.8 %collective-permute-start.64 = (bf16[64,2048]{1,0:T(8,128)(2,1)S(1)}, bf16[64,2048]{1,0:T(8,128)(2,1)S(1)}, u32[]{:S(2)}, u32[]{:S(2)}) collective-permute-start(bf16[64,2048]{1,0:T(8,128)(2,1)S(1)} %add_pieces.1), channel_id=1, source_target_pairs={{0,8},{8,0},{16,24},{24,16},{1,9},{9,1},{17,25},{25,17},{2,10},{10... | collective-permute-start | bytes 786440 | tf_op jit(solution)/shard_map/ppermute | solution.py:539
  383.0 7.9 %collective-permute-start.65 = (bf16[64,2048]{1,0:T(8,128)(2,1)S(1)}, bf16[64,2048]{1,0:T(8,128)(2,1)S(1)}, u32[]{:S(2)}, u32[]{:S(2)}) collective-permute-start(bf16[64,2048]{1,0:T(8,128)(2,1)S(1)} %add_pieces.1), channel_id=1, source_target_pairs={{0,16},{8,24},{16,0},{24,8},{1,17},{9,25},{17,1},{25,9},{2,18},{10... | collective-permute-start | bytes 786440 | tf_op jit(solution)/shard_map/ppermute | solution.py:539
  390.9 7.9 %collective-permute-start.66 = (bf16[64,2048]{1,0:T(8,128)(2,1)S(1)}, bf16[64,2048]{1,0:T(8,128)(2,1)S(1)}, u32[]{:S(2)}, u32[]{:S(2)}) collective-permute-start(bf16[64,2048]{1,0:T(8,128)(2,1)S(1)} %add_pieces.1), channel_id=1, source_target_pairs={{0,24},{8,16},{16,8},{24,0},{1,25},{9,17},{17,9},{25,1},{2,26},{10... | collective-permute-start | bytes 786440 | tf_op jit(solution)/shard_map/ppermute | solution.py:539
  398.8 20.4 %collective-permute-start.58 = (bf16[512,768]{1,0:T(8,128)(2,1)S(1)}, bf16[512,768]{1,0:T(8,128)(2,1)S(1)}, u32[]{:S(2)}, u32[]{:S(2)}) collective-permute-start(bf16[512,768]{1,0:T(8,128)(2,1)S(1)} %get-tuple-element.70.refs_11_), channel_id=1, source_target_pairs={{0,8},{8,0},{16,24},{24,16},{1,9},{9,1},{17,25},{25,17},{2,10},{10... | collective-permute-start | bytes 2359304 | tf_op jit(solution)/shard_map/ppermute | solution.py:539
  399.9 33.0 %collective-permute-start.59 = (bf16[512,768]{1,0:T(8,128)(2,1)S(1)}, bf16[512,768]{1,0:T(8,128)(2,1)S(1)}, u32[]{:S(2)}, u32[]{:S(2)}) collective-permute-start(bf16[512,768]{1,0:T(8,128)(2,1)S(1)} %get-tuple-element.70.refs_11_), channel_id=1, source_target_pairs={{0,16},{8,24},{16,0},{24,8},{1,17},{9,25},{17,1},{25,9},{2,18},{10... | collective-permute-start | bytes 2359304 | tf_op jit(solution)/shard_map/ppermute | solution.py:539
  401.4 32.5 %collective-permute-start.60 = (bf16[512,768]{1,0:T(8,128)(2,1)S(1)}, bf16[512,768]{1,0:T(8,128)(2,1)S(1)}, u32[]{:S(2)}, u32[]{:S(2)}) collective-permute-start(bf16[512,768]{1,0:T(8,128)(2,1)S(1)} %get-tuple-element.70.refs_11_), channel_id=1, source_target_pairs={{0,24},{8,16},{16,8},{24,0},{1,25},{9,17},{17,9},{25,1},{2,26},{10... | collective-permute-start | bytes 2359304 | tf_op jit(solution)/shard_map/ppermute | solution.py:539
  403.2 41.8 %collective-permute-start.49 = (bf16[64,2048]{1,0:T(8,128)(2,1)S(1)}, bf16[64,2048]{1,0:T(8,128)(2,1)S(1)}, u32[]{:S(2)}, u32[]{:S(2)}) collective-permute-start(bf16[64,2048]{1,0:T(8,128)(2,1)S(1)} %get-tuple-element.107), channel_id=1, source_target_pairs={{0,2},{1,3},{2,0},{3,1},{4,6},{5,7},{6,4},{7,5},{8,10},{9,11},{10,... | collective-permute-start | bytes 786440 | tf_op jit(solution)/shard_map/ppermute | solution.py:539
  403.6 41.3 %collective-permute-start.50 = (bf16[64,2048]{1,0:T(8,128)(2,1)S(1)}, bf16[64,2048]{1,0:T(8,128)(2,1)S(1)}, u32[]{:S(2)}, u32[]{:S(2)}) collective-permute-start(bf16[64,2048]{1,0:T(8,128)(2,1)S(1)} %get-tuple-element.109), channel_id=1, source_target_pairs={{0,4},{1,5},{2,6},{3,7},{4,0},{5,1},{6,2},{7,3},{8,12},{9,13},{10,... | collective-permute-start | bytes 786440 | tf_op jit(solution)/shard_map/ppermute | solution.py:539
  419.2 25.7 %collective-permute-start.51 = (bf16[64,2048]{1,0:T(8,128)(2,1)S(1)}, bf16[64,2048]{1,0:T(8,128)(2,1)S(1)}, u32[]{:S(2)}, u32[]{:S(2)}) collective-permute-start(bf16[64,2048]{1,0:T(8,128)(2,1)S(1)} %get-tuple-element.108), channel_id=1, source_target_pairs={{0,6},{1,7},{2,4},{3,5},{4,2},{5,3},{6,0},{7,1},{8,14},{9,15},{10,... | collective-permute-start | bytes 786440 | tf_op jit(solution)/shard_map/ppermute | solution.py:539
  (110 other events, 1197.9 us)
where the time goes:
time: 453 us; the launch traced here: 446 us
  waiting for transfers between devices  193 us (43%)
  Pallas kernels  104 us (23%)
  starting transfers between devices  93.7 us (21%)
  local copies, waits for them, and re-layouts  32 us (7%)
  matrix products  13.1 us (3%)
  other arithmetic  7.2 us (2%)
    ppermute x82, waiting for transfers between devices, swap(): return lax.ppermute(value, axis, [(i, i ^ mask) for i in range(size)])  193 us
    ppermute x82, starting transfers between devices, swap(): return lax.ppermute(value, axis, [(i, i ^ mask) for i in range(size)])  93.7 us
    pallas_call x3, Pallas kernels, weight_grad(): pl.pallas_call(functools.partial(weight_grad_kernel, [len(group) for grou...  49.2 us
    pallas_call x4, Pallas kernels, ffn(): pl.pallas_call(functools.partial(ffn_kernel, len(rows)), grid=(units // t...  30.1 us
    unnamed x194, local copies, waits for them, and re-layouts  28.6 us
    pallas_call x4, Pallas kernels, ffn_back(): pl.pallas_call(functools.partial(ffn_back_kernel, len(grad)), grid=(units...  16.4 us
  transfers between devices with their start and end apart: 82, of which 37 were waited for; matrix products, arithmetic and copies ran while one was open for 6% of the time, Pallas kernels for 21%

commit v1 on v0

--- a/solution.py
+++ b/solution.py
@@ -60,24 +60,26 @@
     ref[half + s * chunk : half + (s + 1) * chunk, lanes] = value[chunk:]
 
 
-def block_row(ref, i, blocks):
-    count = ref.shape[1] // 2
+def block_row(ref, i, blocks, count):
     return jnp.concatenate(
         [ref[b : b + 1, i * count : (i + 1) * count] for b in blocks], axis=1
     )
 
 
-def sequence_blocks(ref, s, chunk):
-    count = ref.shape[1] // 2
+def sequence_blocks(ref, s, chunk, count):
     steps = chunk // count
     pairs = ref.shape[0] // 2
     return [h * pairs + s * steps + k for h in range(2) for k in range(steps)]
 
 
-def store_blocks(ref, i, blocks, row):
-    count = ref.shape[1] // 2
+def store_blocks(ref, i, blocks, row, count):
     for j, b in enumerate(blocks):
         ref[b : b + 1, i * count : (i + 1) * count] = row[:, j * count : (j + 1) * count]
+
+
+def inverse_column(squares_ref, i, blocks, count, model_width):
+    squares = block_row(squares_ref, i, blocks, count)
+    return column(lax.rsqrt(squares / model_width + epsilon), HD)
 
 
 def causal_mask(pos_ref, s, chunk, half):
@@ -119,11 +121,14 @@
         cos = sequence_rows(cos_ref, s, chunk, half, every)
         sin = sequence_rows(sin_ref, s, chunk, half, every)
         mask = causal_mask(pos_ref, s, chunk, half)
-        blocks = sequence_blocks(squares_ref, s, chunk)
-        q_inv = column(lax.rsqrt(block_row(squares_ref, 0, blocks) / model_width + epsilon), HD)
-        k_inv = column(lax.rsqrt(block_row(squares_ref, 1, blocks) / model_width + epsilon), HD)
-        for h in range(width // HD):
-            lanes = slice(h * HD, (h + 1) * HD)
+        count = rows // squares_ref.shape[0]
+        blocks = sequence_blocks(squares_ref, s, chunk, count)
+        q_inv = inverse_column(squares_ref, 0, blocks, count, model_width)
+        k_inv = inverse_column(squares_ref, 1, blocks, count, model_width)
+
+        @pl.loop(0, width // HD)
+        def _(h):
+            lanes = pl.ds(pl.multiple_of(h * HD, HD), HD)
             q = sequence_rows(query_ref, s, chunk, half, lanes) * q_inv * q_gain_ref[:, lanes]
             k = sequence_rows(keys_ref, s, chunk, half, lanes) * k_inv * k_gain_ref[:, lanes]
             q = (q * cos + pltpu.roll(q, HD // 2, 1) * sin).astype(jnp.bfloat16)
@@ -161,27 +166,31 @@
     )(*squares, query, keys, values, q_gain[None, :], k_gain[None, :], *tables)
 
 
-def attend_back_kernel(
-    model_width,
-    grad_ref,
-    q_rot_ref,
-    k_rot_ref,
-    values_ref,
-    query_ref,
-    keys_ref,
-    squares_ref,
-    q_gain_ref,
-    k_gain_ref,
-    cos_ref,
-    sin_ref,
-    pos_ref,
-    grad_values_ref,
-    grad_q_ref,
-    grad_k_ref,
-    inner_ref,
-    gain_ref,
-):
+def attend_back_kernel(model_width, pieces, *refs):
+    (
+        w_out_ref,
+        q_rot_ref,
+        k_rot_ref,
+        values_ref,
+        query_ref,
+        keys_ref,
+        squares_ref,
+        q_gain_ref,
+        k_gain_ref,
+        cos_ref,
+        sin_ref,
+        pos_ref,
+        grad_values_ref,
+        grad_q_ref,
+        grad_k_ref,
+        inner_ref,
+        gain_ref,
+        grad_ref,
+    ) = refs[pieces:]
     rows, width = query_ref.shape
+    grad = times_transposed(joined(refs[:pieces]), w_out_ref[...])
+    grad_ref[...] = grad.astype(jnp.bfloat16)
+    inner_ref[...] = jnp.zeros_like(inner_ref)
     half = rows // 2
     chunk = SEQ // 2
     scale = 1.0 / math.sqrt(HD)
@@ -191,13 +200,14 @@
         cos = sequence_rows(cos_ref, s, chunk, half, every)
         sin = sequence_rows(sin_ref, s, chunk, half, every)
         mask = causal_mask(pos_ref, s, chunk, half)
-        blocks = sequence_blocks(squares_ref, s, chunk)
-        q_inv = column(lax.rsqrt(block_row(squares_ref, 0, blocks) / model_width + epsilon), HD)
-        k_inv = column(lax.rsqrt(block_row(squares_ref, 1, blocks) / model_width + epsilon), HD)
-        q_inner = jnp.zeros((1, SEQ), jnp.float32)
-        k_inner = jnp.zeros((1, SEQ), jnp.float32)
-        for h in range(width // HD):
-            lanes = slice(h * HD, (h + 1) * HD)
+        count = rows // squares_ref.shape[0]
+        blocks = sequence_blocks(squares_ref, s, chunk, count)
+        q_inv = inverse_column(squares_ref, 0, blocks, count, model_width)
+        k_inv = inverse_column(squares_ref, 1, blocks, count, model_width)
+
+        def head(h, inners):
+            q_inner, k_inner = inners
+            lanes = pl.ds(pl.multiple_of(h * HD, HD), HD)
             q = sequence_rows(q_rot_ref, s, chunk, half, lanes)
             k = sequence_rows(k_rot_ref, s, chunk, half, lanes)
             v = sequence_rows(values_ref, s, chunk, half, lanes)
@@ -219,21 +229,25 @@
             k_part = grad_k * (sequence_rows(keys_ref, s, chunk, half, lanes) * k_inv)
             gain_ref[0:1, lanes] += jnp.sum(q_part, axis=0, keepdims=True)
             gain_ref[1:2, lanes] += jnp.sum(k_part, axis=0, keepdims=True)
-            q_inner += row_sums(q_part * q_gain_ref[:, lanes])
-            k_inner += row_sums(k_part * k_gain_ref[:, lanes])
+            q_inner = q_inner + row_sums(q_part * q_gain_ref[:, lanes])
+            k_inner = k_inner + row_sums(k_part * k_gain_ref[:, lanes])
             store_rows(grad_q_ref, s, chunk, half, lanes, grad_q * q_gain_ref[:, lanes])
             store_rows(grad_k_ref, s, chunk, half, lanes, grad_k * k_gain_ref[:, lanes])
-        store_blocks(inner_ref, 0, blocks, q_inner)
-        store_blocks(inner_ref, 1, blocks, k_inner)
+            return q_inner, k_inner
+
+        zero = jnp.zeros((1, SEQ), jnp.float32)
+        q_inner, k_inner = lax.fori_loop(0, width // HD, head, (zero, zero))
+        store_blocks(inner_ref, 0, blocks, q_inner, count)
+        store_blocks(inner_ref, 1, blocks, k_inner, count)
 
 
 def attend_back(
-    grad_attended, q_rot, k_rot, values, query, keys, squares, q_gain, k_gain, tables, model_width
+    grad_attn, w_out, q_rot, k_rot, values, query, keys, squares, q_gain, k_gain, tables, model_width
 ):
     rows, width = query.shape
     wide = jax.ShapeDtypeStruct((rows, width), jnp.float32)
     return pl.pallas_call(
-        functools.partial(attend_back_kernel, model_width),
+        functools.partial(attend_back_kernel, model_width, len(grad_attn)),
         out_shape=(
             jax.ShapeDtypeStruct((rows, width), jnp.bfloat16),
             wide,
@@ -241,15 +255,17 @@
             jax.ShapeDtypeStruct(squares.shape, jnp.float32),
             jax.ShapeDtypeStruct((2, width), jnp.float32),
         ),
+        scratch_shapes=[pltpu.VMEM((rows, width), jnp.bfloat16)],
         name="attend_back",
-        compiler_params=pltpu.CompilerParams(vmem_limit_bytes=20 * MIB),
+        compiler_params=pltpu.CompilerParams(vmem_limit_bytes=16 * MIB),
         cost_estimate=pl.CostEstimate(
             flops=10 * rows * SEQ * width,
             bytes_accessed=26 * rows * width,
             transcendentals=rows * SEQ * width // HD,
         ),
     )(
-        grad_attended,
+        *grad_attn,
+        w_out,
         q_rot,
         k_rot,
         values,
@@ -271,49 +287,203 @@
         grad_k_ref,
         grad_values_ref,
         squares_ref,
+        gains_ref,
         out_ref,
-        rest_ref,
         inner_ref,
+        gain_rows_ref,
     ) = refs[len(parts) :]
-    _, width = query_ref.shape
-    count = squares_ref.shape[0]
-    blocks = list(range(count))
-    for i, row in enumerate(summed_blocks([part.at[:count] for part in parts], orders)):
+    rows, width = query_ref.shape
+    blocks = list(range(squares_ref.shape[0]))
+    count = rows // len(blocks)
+    sums = summed_blocks([part.at[: len(blocks)] for part in parts], orders)
+    for i, row in enumerate(sums):
         inner_ref[i : i + 1, :] = row
-    rest = [part[count:, :] for part in parts]
-    while len(rest) > 1:
-        rest = [rest[i] + rest[i + 1] for i in range(0, len(rest), 2)]
-    rest_ref[...] = rest[0]
     for i, source, target in ((0, query_ref, grad_q_ref), (1, keys_ref, grad_k_ref)):
-        inverse = column(
-            lax.rsqrt(block_row(squares_ref, i, blocks) / model_width + epsilon), HD
-        )
-        inner = column(block_row(inner_ref, i, blocks) / model_width, HD)
+        inverse = inverse_column(squares_ref, i, blocks, count, model_width)
+        inner = column(block_row(inner_ref, i, blocks, count) / model_width, HD)
         for h in range(width // HD):
             lanes = slice(h * HD, (h + 1) * HD)
             normed = source[:, lanes] * inverse
             value = inverse * (target[:, lanes] - normed * inner)
             start = i * width + h * HD
-            out_ref[:, start : start + HD] = value.astype(jnp.bfloat16)
-    out_ref[:, 2 * width :] = grad_values_ref[...]
-
-
-def finish(query, keys, grad_q, grad_k, grad_values, squares, inner, orders, model_width):
+            out_ref[:rows, start : start + HD] = value.astype(jnp.bfloat16)
+    out_ref[:rows, 2 * width :] = grad_values_ref[...]
+    rest = [part[len(blocks) :, :] for part in parts]
+    while len(rest) > 1:
+        rest = [rest[i] + rest[i + 1] for i in range(0, len(rest), 2)]
+    rest = rest[0]
+    gains = [rest[i : i + 1, :] for i in range(rest.shape[0])]
+    for i in range(2):
+        gains += [gains_ref[i : i + 1, h * HD : (h + 1) * HD] for h in range(width // HD)]
+    gain_rows_ref[...] = jnp.zeros_like(gain_rows_ref)
+    across = 3 * width // HD
+    half = gain_rows_ref.shape[0] // 2
+    for i, gain in enumerate(gains):
+        r, lanes = i // across, slice(i % across * HD, (i % across + 1) * HD)
+        gain_rows_ref[r : r + 1, lanes] = gain
+    high = gain_rows_ref[:half, :].astype(jnp.bfloat16).astype(jnp.float32)
+    gain_rows_ref[half:, :] = gain_rows_ref[:half, :] - high
+    out_ref[rows:, :] = gain_rows_ref[...].astype(jnp.bfloat16)
+
+
+def gain_row_count(model_width, width):
+    blocks = (2 * model_width + 2 * width) // HD
+    return 16 * pl.cdiv(pl.cdiv(blocks, 3 * width // HD), 8)
+
+
+def finish(query, keys, grad_q, grad_k, grad_values, squares, inner, gains, orders, model_width):
     rows, width = query.shape
-    count, lanes = squares.shape
+    extra = gain_row_count(model_width, width)
     return pl.pallas_call(
         functools.partial(finish_kernel, model_width, orders),
-        out_shape=(
-            jax.ShapeDtypeStruct((rows, 3 * width), jnp.bfloat16),
-            jax.ShapeDtypeStruct((inner[0].shape[0] - count, lanes), jnp.float32),
-        ),
-        scratch_shapes=[pltpu.VMEM((count, lanes), jnp.float32)],
+        out_shape=jax.ShapeDtypeStruct((rows + extra, 3 * width), jnp.bfloat16),
+        scratch_shapes=[
+            pltpu.VMEM(squares.shape, jnp.float32),
+            pltpu.VMEM((extra, 3 * width), jnp.float32),
+        ],
         name="finish",
         compiler_params=pltpu.CompilerParams(vmem_limit_bytes=16 * MIB),
         cost_estimate=pl.CostEstimate(
             flops=10 * rows * width, bytes_accessed=24 * rows * width, transcendentals=0
         ),
-    )(*inner, query, keys, grad_q, grad_k, grad_values, squares)
+    )(*inner, query, keys, grad_q, grad_k, grad_values, squares, gains)
+
+
+def sum_gains_kernel(*refs):
+    groups = refs[:-4]
+    half = groups[0].shape[0] // 2
+    values = []
+    for ref in groups:
+        values.append(ref[:half, :].astype(jnp.float32) + ref[half:, :].astype(jnp.float32))
+    while len(values) > 1:
+        values = [values[i] + values[i + 1] for i in range(0, len(values), 2)]
+    total = values[0]
+    across = total.shape[1] // HD
+    at = 0
+    for out in refs[-4:]:
+        for j in range(out.shape[1] // HD):
+            r, c = at // across, at % across
+            out[:, j * HD : (j + 1) * HD] = total[r : r + 1, c * HD : (c + 1) * HD]
+            at += 1
+
+
+def sum_gains(groups, model_width, width):
+    extra = gain_row_count(model_width, width)
+    at = [group.shape[0] // extra - 1 for group in groups]
+    shapes = [(1, model_width), (1, model_width), (1, width), (1, width)]
+    outs = pl.pallas_call(
+        sum_gains_kernel,
+        grid=(1,),
+        in_specs=[pl.BlockSpec((extra, 3 * width), lambda i, j=j: (j, 0)) for j in at],
+        out_specs=[pl.BlockSpec(shape, lambda i: (0, 0)) for shape in shapes],
+        out_shape=[jax.ShapeDtypeStruct(shape, jnp.float32) for shape in shapes],
+        name="sum_gains",
+        compiler_params=pltpu.CompilerParams(vmem_limit_bytes=4 * MIB),
+    )(*groups)
+    return [out[0] for out in outs]
+
+
+def back_product(grad_ref, weights):
+    width = weights[0].shape[1]
+    return sum(
+        times_transposed(grad_ref[:, i * width : (i + 1) * width], weight[...])
+        for i, weight in enumerate(weights)
+    )
+
+
+def far_kernel(grad_ref, *refs):
+    refs[-1][...] = back_product(grad_ref, refs[:-1]).astype(jnp.bfloat16)
+
+
+def near_kernel(count, grad_ref, far_ref, *refs):
+    own_ref, others = refs[3], refs[4:]
+    total = back_product(grad_ref, refs[:3]) + far_ref[...].astype(jnp.float32)
+    own_ref[...] = total[:count]
+    for k, ref in enumerate(others):
+        ref[...] = total[(k + 1) * count : (k + 2) * count].astype(jnp.bfloat16)
+
+
+def tokens_back(grad, weights, half, part, far=None, count=None):
+    depth, width = weights[0].shape
+    tile = min(512, depth)
+    specs = [pl.BlockSpec((half, 3 * width), lambda j: (part, 0))]
+    arrays = [grad]
+    if far is not None:
+        specs.append(pl.BlockSpec((half, tile), lambda j: (0, j)))
+        arrays.append(far)
+    specs += [pl.BlockSpec((tile, width), lambda j: (j, 0))] * 3
+    if far is None:
+        kernel, sizes = far_kernel, [(half, jnp.bfloat16)]
+    else:
+        kernel = functools.partial(near_kernel, count)
+        sizes = [(count, jnp.float32)] + [(count, jnp.bfloat16)] * (half // count - 1)
+    return pl.pallas_call(
+        kernel,
+        grid=(depth // tile,),
+        in_specs=specs,
+        out_specs=[pl.BlockSpec((size, tile), lambda j: (0, j)) for size, _ in sizes],
+        out_shape=[jax.ShapeDtypeStruct((size, depth), kind) for size, kind in sizes],
+        name="tokens_back",
+        compiler_params=pltpu.CompilerParams(vmem_limit_bytes=16 * MIB),
+        cost_estimate=pl.CostEstimate(
+            flops=6 * half * depth * width,
+            bytes_accessed=6 * depth * width + 8 * half * depth,
+            transcendentals=0,
+        ),
+    )(*arrays, *weights)
+
+
+def out_grad_kernel(pieces, *refs):
+    attended_ref, me_ref = refs[pieces : pieces + 2]
+    own_ref, others, grad_ref = refs[pieces + 2], refs[pieces + 3 : -1], refs[-1]
+    count = own_ref.shape[0]
+    grad_ref[...] = transposed_times(attended_ref[...], joined(refs[:pieces]))
+    me = me_ref[0]
+    own_ref[...] = grad_ref[pl.ds(pl.multiple_of(me * count, count), count), :]
+    for j, ref in enumerate(others):
+        start = pl.multiple_of((me ^ (j + 1)) * count, count)
+        ref[...] = grad_ref[pl.ds(start, count), :].astype(jnp.bfloat16)
+
+
+def out_grad(attended, grad_attn, me, dp_size):
+    width, depth = attended.shape[1], grad_attn[0].shape[1]
+    piece = (width // dp_size, depth)
+    return pl.pallas_call(
+        functools.partial(out_grad_kernel, len(grad_attn)),
+        in_specs=[pl.BlockSpec(array.shape, lambda: (0, 0)) for array in (*grad_attn, attended)]
+        + [pl.BlockSpec(memory_space=pltpu.SMEM)],
+        out_shape=[jax.ShapeDtypeStruct(piece, jnp.float32)]
+        + [jax.ShapeDtypeStruct(piece, jnp.bfloat16)] * (dp_size - 1),
+        scratch_shapes=[pltpu.VMEM((width, depth), jnp.float32)],
+        name="out_grad",
+        compiler_params=pltpu.CompilerParams(vmem_limit_bytes=16 * MIB),
+        cost_estimate=pl.CostEstimate(
+            flops=2 * attended.shape[0] * width * depth,
+            bytes_accessed=2 * attended.shape[0] * (width + depth) + 3 * width * depth,
+            transcendentals=0,
+        ),
+    )(*grad_attn, attended, me)
+
+
+def assemble_kernel(*refs):
+    me = refs[-2][0]
+    out_ref = refs[-1]
+    for j, ref in enumerate(refs[:-2]):
+        count = ref.shape[0]
+        start = pl.multiple_of((me ^ j) * count, count)
+        out_ref[pl.ds(start, count), :] = ref[...].astype(jnp.float32)
+
+
+def assemble(pieces, me):
+    count, depth = pieces[0].shape
+    return pl.pallas_call(
+        assemble_kernel,
+        in_specs=[pl.BlockSpec((count, depth), lambda: (0, 0)) for _ in pieces]
+        + [pl.BlockSpec(memory_space=pltpu.SMEM)],
+        out_shape=jax.ShapeDtypeStruct((len(pieces) * count, depth), jnp.float32),
+        name="assemble",
+        compiler_params=pltpu.CompilerParams(vmem_limit_bytes=8 * MIB),
+    )(*pieces, me)
 
 
 def summed_blocks(refs, orders):
@@ -366,6 +536,14 @@
     )(own, *others)
 
 
+def in_hbm(array):
+    return pltpu.with_memory_space_constraint(array, pltpu.HBM)
+
+
+def resident(shape):
+    return pl.BlockSpec(shape, lambda i: (0, 0), pipeline_mode=pl.Buffered(1))
+
+
 def joined(refs):
     return refs[0][...] if len(refs) == 1 else jnp.concatenate([r[...] for r in refs], axis=0)
 
@@ -376,6 +554,9 @@
         pieces:
     ]
     blocks = list(range(squares_ref.shape[0]))
+    count = rows.shape[0] // len(blocks)
+    if 2 * count < squares_ref.shape[1]:
+        squares_ref[...] = jnp.zeros_like(squares_ref)
     for i, weight, out in ((0, w_query_ref, query_ref), (1, w_key_ref, keys_ref)):
         value = product(rows, weight[...])
         out[...] = value
@@ -383,7 +564,7 @@
         folded = square[:, :HD]
         for h in range(1, value.shape[1] // HD):
             folded = folded + square[:, h * HD : (h + 1) * HD]
-        store_blocks(squares_ref, i, blocks, row_sums(folded))
+        store_blocks(squares_ref, i, blocks, row_sums(folded), count)
     values_ref[...] = product(rows, w_value_ref[...]).astype(jnp.bfloat16)
 
 
@@ -397,16 +578,16 @@
             wide,
             wide,
             jax.ShapeDtypeStruct((count, width), jnp.bfloat16),
-            jax.ShapeDtypeStruct((tensor_size, 2 * count // tensor_size), jnp.float32),
+            jax.ShapeDtypeStruct((tensor_size, max(HD, 2 * count // tensor_size)), jnp.float32),
         ),
         name="project",
-        compiler_params=pltpu.CompilerParams(vmem_limit_bytes=20 * MIB),
+        compiler_params=pltpu.CompilerParams(vmem_limit_bytes=16 * MIB),
         cost_estimate=pl.CostEstimate(
             flops=6 * count * depth * width,
             bytes_accessed=2 * count * depth + 6 * depth * width + 10 * count * width,
             transcendentals=0,
         ),
-    )(*rows, w_query, w_key, w_value)
+    )(*[in_hbm(array) for array in (*rows, w_query, w_key, w_value)])
 
 
 def ffn_kernel(pieces, *refs):
@@ -429,12 +610,12 @@
     return pl.pallas_call(
         functools.partial(ffn_kernel, len(rows)),
         grid=(units // tile,),
-        in_specs=[pl.BlockSpec(piece.shape, lambda j: (0, 0)) for piece in rows]
+        in_specs=[resident(piece.shape) for piece in rows]
         + [weight, weight],
         out_specs=(out, out, out),
         out_shape=(wide, wide, jax.ShapeDtypeStruct((count, units), jnp.bfloat16)),
         name="ffn",
-        compiler_params=pltpu.CompilerParams(vmem_limit_bytes=20 * MIB),
+        compiler_params=pltpu.CompilerParams(vmem_limit_bytes=16 * MIB),
         cost_estimate=pl.CostEstimate(
             flops=4 * count * depth * units,
             bytes_accessed=2 * count * depth + 4 * depth * units + 10 * count * units,
@@ -454,7 +635,7 @@
     grad_up_ref[...] = (grad_swiglu * (gate * sig)).astype(jnp.bfloat16)
 
 
-def ffn_back(grad, w_down, gate, up):
+def ffn_back(grad, w_down, gate, up, place=lambda array: array):
     count = sum(piece.shape[0] for piece in grad)
     units, depth = w_down.shape
     tile = min(256, units)
@@ -463,18 +644,18 @@
     return pl.pallas_call(
         functools.partial(ffn_back_kernel, len(grad)),
         grid=(units // tile,),
-        in_specs=[pl.BlockSpec(piece.shape, lambda j: (0, 0)) for piece in grad]
+        in_specs=[resident(piece.shape) for piece in grad]
         + [pl.BlockSpec((tile, depth), lambda j: (j, 0)), out, out],
         out_specs=(out, out),
         out_shape=(narrow, narrow),
         name="ffn_back",
-        compiler_params=pltpu.CompilerParams(vmem_limit_bytes=20 * MIB),
+        compiler_params=pltpu.CompilerParams(vmem_limit_bytes=16 * MIB),
         cost_estimate=pl.CostEstimate(
             flops=2 * count * depth * units,
             bytes_accessed=2 * count * depth + 2 * depth * units + 12 * count * units,
             transcendentals=count * units,
         ),
-    )(*grad, w_down, gate, up)
+    )(*grad, *[place(array) for array in (w_down, gate, up)])
 
 
 def weight_grad_kernel(left_counts, right_counts, rights, outs, *refs):
@@ -501,13 +682,19 @@
             out_refs[r * outs + o][...] = sums[0]
 
 
-def weight_grad(left, *rights, outs=1):
+def weight_grad(left, *rights, outs=1, extra=0):
     depth = left[0][0].shape[1]
-    tile = min(256, depth)
     left_pieces = [piece for group in left for piece in group]
-    right_pieces = [piece for right in rights for group in right for piece in group]
+    right_pieces, counts = [], []
+    for right in rights:
+        for group in right:
+            right_pieces += group
+            counts += [piece.shape[0] for piece in group[:-1]] + [group[-1].shape[0] - extra]
     rows = sum(piece.shape[0] for piece in left_pieces)
     widths = [right[0][0].shape[1] // outs for right in rights for _ in range(outs)]
+    tile = min(512 if max(widths) <= 1024 else 256, depth)
+    blocks = 4 * rows * tile + (2 * len(rights)) * rows * rights[0][0][0].shape[1]
+    needed = blocks + 4 * tile * sum(widths) * (2 + len(left)) + 4 * MIB
     return pl.pallas_call(
         functools.partial(
             weight_grad_kernel,
@@ -518,17 +705,19 @@
         ),
         grid=(depth // tile,),
         in_specs=[pl.BlockSpec((piece.shape[0], tile), lambda i: (0, i)) for piece in left_pieces]
-        + [pl.BlockSpec(piece.shape, lambda i: (0, 0)) for piece in right_pieces],
+        + [
+            resident((count, piece.shape[1])) for count, piece in zip(counts, right_pieces)
+        ],
         out_specs=[pl.BlockSpec((tile, width), lambda i: (i, 0)) for width in widths],
         out_shape=[jax.ShapeDtypeStruct((depth, width), jnp.float32) for width in widths],
         name="weight_grad",
-        compiler_params=pltpu.CompilerParams(vmem_limit_bytes=44 * MIB),
+        compiler_params=pltpu.CompilerParams(vmem_limit_bytes=max(28 * MIB, needed)),
         cost_estimate=pl.CostEstimate(
             flops=2 * rows * depth * sum(widths),
             bytes_accessed=2 * rows * (depth + sum(widths)) + 4 * depth * sum(widths),
             transcendentals=0,
         ),
-    )(*left_pieces, *right_pieces)
+    )(*[in_hbm(piece) for piece in left_pieces + right_pieces])
 
 
 def build(dp_size, tensor_size):
@@ -538,17 +727,29 @@
         size = dp_size if axis == "dp" else tensor_size
         return lax.ppermute(value, axis, [(i, i ^ mask) for i in range(size)])
 
-    def tensor_gather(own):
-        near = [own] + [swap(own, "tensor", 2 * k) for k in range(1, pairs)]
+    def tensor_gather(own, relay=False):
+        near = [own]
+        for k in range(1, pairs):
+            if relay and k == 3:
+                near.append(swap(near[2], "tensor", 2))
+            else:
+                near.append(swap(own, "tensor", 2 * k))
         return near + [swap(near[k], "tensor", 1) for k in range(pairs)]
 
-    def tensor_scatter(partial_of, rows):
+    def tensor_scatter(partial_of, rows, relay=False):
         half = rows // 2
         far = partial_of(half, rows).astype(jnp.bfloat16)
         far = swap(far, "tensor", 1)
         near = partial_of(0, half) + far.astype(jnp.float32)
         count = half // pairs
         total = near[:count]
+        if relay and pairs == 4:
+            one, two, three = [near[k * count : (k + 1) * count] for k in range(1, pairs)]
+            three = swap(three.astype(jnp.bfloat16), "tensor", 2)
+            one = swap(one.astype(jnp.bfloat16), "tensor", 2)
+            two = (two + three.astype(jnp.float32)).astype(jnp.bfloat16)
+            two = swap(two, "tensor", 4)
+            return total + one.astype(jnp.float32) + two.astype(jnp.float32)
         for k in range(1, pairs):
             block = near[k * count : (k + 1) * count].astype(jnp.bfloat16)
             total = total + swap(block, "tensor", 2 * k).astype(jnp.float32)
@@ -566,40 +767,30 @@
         others = [swap(value, "tensor", 2 * k) for k in range(1, pairs)]
         return [value] + others, [order(2 * k) for k in range(1, pairs)]
 
-    def tree_sum(values):
-        while len(values) > 1:
-            values = [values[i] + values[i + 1] for i in range(0, len(values), 2)]
-        return values[0]
-
-    def dp_gather(own):
+    def dp_gather(own, cut):
+        if dp_size == 4:
+            one = swap(own, "dp", 1)
+            two = swap(own, "dp", 2)
+            top = one[:cut]
+            bottom = two[cut:]
+            top = swap(top, "dp", 2)
+            bottom = swap(bottom, "dp", 1)
+            return [[own], [one], [two], [top, bottom]]
         return [[own]] + [[swap(own, "dp", j)] for j in range(1, dp_size)]
 
     def dp_gather_shared(pieces):
         near = jnp.concatenate(pieces[:pairs], axis=0)
+        fetched = dp_gather(near, near.shape[0] // 2)[1:]
         groups = [[near] + pieces[pairs:]]
-        for j in range(1, dp_size):
-            piece = swap(near, "dp", j)
-            groups.append([piece, swap(piece, "tensor", 1)])
+        for mine in fetched:
+            groups.append(mine + [swap(piece, "tensor", 1) for piece in mine])
         return groups
 
-    def dp_sum(matrix):
-        rows = matrix.shape[0] // dp_size
-        rounded = matrix.astype(jnp.bfloat16)
-        me = lax.axis_index("dp")
-        zero = jnp.zeros_like(me)
-        own = lax.dynamic_slice_in_dim(matrix, me * rows, rows, 0)
-        others = []
-        for j in range(1, dp_size):
-            piece = lax.dynamic_slice_in_dim(rounded, (me ^ j) * rows, rows, 0)
-            others.append(swap(piece, "dp", j))
+    def dp_sum(own, others, me):
+        others = [swap(piece, "dp", j + 1) for j, piece in enumerate(others)]
         total = add_pieces(own, others)
-        result = jnp.zeros(matrix.shape, jnp.float32)
-        for j in range(dp_size):
-            piece = total if j == 0 else swap(total, "dp", j)
-            result = lax.dynamic_update_slice(
-                result, piece.astype(jnp.float32), ((me ^ j) * rows, zero)
-            )
-        return result
+        pieces = [total] + [swap(total, "dp", j) for j in range(1, dp_size)]
+        return assemble(pieces, me)
 
     def positions(rows):
         count = rows // tensor_size
@@ -642,40 +833,42 @@
         width = w_query.shape[1]
         tables = tables_of(rows)
 
-        gathered = tensor_gather(tokens)
+        gathered = tensor_gather(tokens, relay=True)
         query, keys, values, squares = project(gathered, w_query, w_key, w_value, tensor_size)
         square_parts, orders = row_sum(squares)
         attended, q_rot, k_rot, squares = attend(
             query, keys, values, square_parts, orders, q_gain, k_gain, tables, model_width
         )
-        attn_rows = tensor_scatter(lambda a, b: product(attended[a:b], w_out), rows)
+        attn_rows = tensor_scatter(lambda a, b: product(attended[a:b], w_out), rows, relay=True)
         a_inverse = row_scale(attn_rows)
         a_normed = attn_rows * a_inverse
         mixed = tokens.astype(jnp.float32) + a_normed * attn_gain
-        mixed_b = tensor_gather(mixed.astype(jnp.bfloat16))
+        mixed_b = tensor_gather(mixed.astype(jnp.bfloat16), relay=True)
         gate, up_proj, swiglu = ffn(mixed_b, w_gate, w_up)
-        ffn_rows = tensor_scatter(lambda a, b: product(swiglu[a:b], w_down), rows)
+        ffn_rows = tensor_scatter(lambda a, b: product(swiglu[a:b], w_down), rows, relay=True)
         m_inverse = row_scale(ffn_rows)
         m_normed = ffn_rows * m_inverse
         layer_out = mixed + m_normed * ffn_gain
         grad_out = cotangent.astype(jnp.float32)
         ffn_gain_part = jnp.sum(grad_out * m_normed, axis=0)
         grad_ffn = tensor_gather(
-            norm_back(grad_out * ffn_gain, m_normed, m_inverse).astype(jnp.bfloat16)
+            norm_back(grad_out * ffn_gain, m_normed, m_inverse).astype(jnp.bfloat16), relay=True
         )
         grad_gate, grad_up = ffn_back(grad_ffn, w_down, gate, up_proj)
         grad_mixed = grad_out + tensor_scatter(
             lambda a, b: times_transposed(grad_gate[a:b], w_gate)
             + times_transposed(grad_up[a:b], w_up),
             rows,
+            relay=True,
         )
         attn_gain_part = jnp.sum(grad_mixed * a_normed, axis=0)
-        grad_attn = jnp.concatenate(tensor_gather(
-            norm_back(grad_mixed * attn_gain, a_normed, a_inverse).astype(jnp.bfloat16)
-        ), axis=0)
-        grad_attended = times_transposed(grad_attn, w_out).astype(jnp.bfloat16)
+        grad_attn = tensor_gather(
+            norm_back(grad_mixed * attn_gain, a_normed, a_inverse).astype(jnp.bfloat16), relay=True
+        )
+        me = lax.axis_index("dp").astype(jnp.int32).reshape(1)
         grad_values, grad_q, grad_k, inner, gain_parts = attend_back(
-            grad_attended,
+            grad_attn,
+            w_out,
             q_rot,
             k_rot,
             values,
@@ -693,15 +886,27 @@
                 [inner, attn_gain_part.reshape(-1, lanes), ffn_gain_part.reshape(-1, lanes)]
             ),
         )
-        grad_qkv, post_gains = finish(
-            query, keys, grad_q, grad_k, grad_values, squares, inner_parts, orders, model_width
-        )
-        grad_tokens = grad_mixed + tensor_scatter(
-            lambda a, b: times_transposed(grad_qkv[a:b, :width], w_query)
-            + times_transposed(grad_qkv[a:b, width : 2 * width], w_key)
-            + times_transposed(grad_qkv[a:b, 2 * width :], w_value),
-            rows,
-        )
+        out_own, *out_others = out_grad(attended, grad_attn, me, dp_size)
+        grad_qkv = finish(
+            query,
+            keys,
+            grad_q,
+            grad_k,
+            grad_values,
+            squares,
+            inner_parts,
+            gain_parts,
+            orders,
+            model_width,
+        )
+        weights = (w_query, w_key, w_value)
+        (far,) = tokens_back(grad_qkv, weights, rows // 2, 1)
+        far = swap(far, "tensor", 1)
+        own, *others = tokens_back(
+            grad_qkv, weights, rows // 2, 0, far, tokens.shape[0]
+        )
+        others = [swap(piece, "tensor", 2 * k + 2) for k, piece in enumerate(others)]
+        grad_tokens = grad_mixed + sum([piece.astype(jnp.float32) for piece in others], own)
 
         tokens_all = dp_gather_shared(gathered)
         mixed_all = dp_gather_shared(mixed_b)
@@ -709,18 +914,21 @@
         swiglus, grad_gates, grad_ups = [[swiglu]], [[grad_gate]], [[grad_up]]
         for j in range(1, dp_size):
             gate_j, up_j, swiglu_j = ffn(mixed_all[j], w_gate, w_up)
-            grad_gate_j, grad_up_j = ffn_back(grad_ffn_all[j], w_down, gate_j, up_j)
+            grad_gate_j, grad_up_j = ffn_back(
+                grad_ffn_all[j], w_down, gate_j, up_j, *[in_hbm][: j // (dp_size - 1)]
+            )
             swiglus.append([swiglu_j])
             grad_gates.append([grad_gate_j])
             grad_ups.append([grad_up_j])
         (grad_w_down,) = weight_grad(swiglus, grad_ffn_all)
-        grad_w_gate, grad_w_up = weight_grad(mixed_all, grad_gates, grad_ups)
-        grad_w_out = dp_sum(transposed_times(attended, grad_attn))
+        (grad_w_gate,) = weight_grad(mixed_all, grad_gates)
+        (grad_w_up,) = weight_grad(mixed_all, grad_ups)
+        grad_w_out = dp_sum(out_own, out_others, me)
+        operands = dp_gather(grad_qkv, rows // 2)
         grad_w_query, grad_w_key, grad_w_value = weight_grad(
-            tokens_all, dp_gather(grad_qkv), outs=3
-        )
-        own_gains = jnp.concatenate([post_gains.reshape(-1), gain_parts.reshape(-1)])
-        gains = tree_sum([piece for group in dp_gather(own_gains) for piece in group])
+            tokens_all, operands, outs=3, extra=grad_qkv.shape[0] - rows
+        )
+        gains = sum_gains([group[-1] for group in operands], model_width, width)
         return (
             layer_out,
             grad_tokens,
@@ -731,10 +939,10 @@
             grad_w_gate,
             grad_w_up,
             grad_w_down,
-            gains[2 * model_width : 2 * model_width + width],
-            gains[2 * model_width + width :],
-            gains[:model_width],
-            gains[model_width : 2 * model_width],
+            gains[2],
+            gains[3],
+            gains[0],
+            gains[1],
         )
 
     return shards

time: 453 us -> 422 us (0.932)
  waiting for transfers between devices: 193 us -> 166 us
  Pallas kernels: 104 us -> 124 us
  starting transfers between devices: 93.7 us -> 83.8 us
  local copies, waits for them, and re-layouts: 32 us -> 26 us
  matrix products: 13.1 us -> 8.56 us
    ppermute x82 -> x86, waiting for transfers between devices: 193 us -> 166 us  [swap(): return lax.ppermute(value, axis, [(i, i ^ mask) for i in range(size)])]
    ppermute x82 -> x86, starting transfers between devices: 93.7 us -> 83.8 us  [swap(): return lax.ppermute(value, axis, [(i, i ^ mask) for i in range(size)])]
    pallas_call x1 -> x6, Pallas kernels: 4.23 us -> 12.2 us  [the longest x1 5.76 us: attend_back(): pl.pallas_call(functools.partial(attend_back_kernel, model_width, len(gra...]
    unnamed x194 -> x231, local copies, waits for them, and re-layouts: 28.6 us -> 22.3 us
    pallas_call x3 -> x4, Pallas kernels: 49.2 us -> 54 us  [weight_grad(): pl.pallas_call(functools.partial(weight_grad_kernel, [len(group) for grou...]
  transfers between devices with their start and end apart: 82 -> 86, of which waited for: 37 -> 34; matrix products, arithmetic and copies ran while one was open for 6% -> 2% of each run, Pallas kernels for 21% -> 25%
where the time goes in v1:
time: 422 us; the launch traced here: 416 us
  waiting for transfers between devices  166 us (39%)
  Pallas kernels  124 us (29%)
  starting transfers between devices  83.8 us (20%)
  local copies, waits for them, and re-layouts  26 us (6%)
  matrix products  8.56 us (2%)
  other arithmetic  4.95 us (1%)
    ppermute x86, waiting for transfers between devices, swap(): return lax.ppermute(value, axis, [(i, i ^ mask) for i in range(size)])  166 us
    ppermute x86, starting transfers between devices, swap(): return lax.ppermute(value, axis, [(i, i ^ mask) for i in range(size)])  83.8 us
    pallas_call x4, Pallas kernels, weight_grad(): pl.pallas_call(functools.partial(weight_grad_kernel, [len(group) for grou...  54 us
    pallas_call x4, Pallas kernels, ffn(): pl.pallas_call(functools.partial(ffn_kernel, len(rows)), grid=(units // t...  30 us
    unnamed x231, local copies, waits for them, and re-layouts  22.3 us
    pallas_call x4, Pallas kernels, ffn_back(): pl.pallas_call(functools.partial(ffn_back_kernel, len(grad)), grid=(units...  19.9 us
  transfers between devices with their start and end apart: 86, of which 34 were waited for; matrix products, arithmetic and copies ran while one was open for 2% of the time, Pallas kernels for 25%

profile of v1, /device:TPU:0, one launch (start us, length us, event | category | flops | bytes accessed | tf_op | source)
XLA Modules:
  0.0 416.3 jit_solution(3914356328079055649)
XLA Ops:
  0.6 4.1 collective-permute-start.1
  6.3 10.7 %collective-permute-done.1.refs_2_ = bf16[64,2048]{1,0:T(8,128)(2,1)S(1)} collective-permute-done((bf16[64,2048]{1,0:T(8,128)(2,1)}, bf16[64,2048]{1,0:T(8,128)(2,1)S(1)}, u32[]{:S(2)}, u32[]{:S(2)}) %collective-permute-start.1) | collective-permute-done | bytes 262176 | tf_op jit(solution)/shard_map/ppermute | solution.py:728
  18.4 6.0 %collective-permute-done.2.refs_3_ = bf16[64,2048]{1,0:T(8,128)(2,1)S(1)} collective-permute-done((bf16[64,2048]{1,0:T(8,128)(2,1)S(1)}, bf16[64,2048]{1,0:T(8,128)(2,1)S(1)}, u32[]{:S(2)}, u32[]{:S(2)}) %collective-permute-start.2) | collective-permute-done | bytes 262176 | tf_op jit(solution)/shard_map/ppermute | solution.py:728
  27.1 4.4 %project.1 = (f32[512,256]{1,0:T(8,128)S(1)}, f32[512,256]{1,0:T(8,128)S(1)}, bf16[512,256]{1,0:T(8,128)(2,1)S(1)}, f32[8,128]{1,0:T(8,128)S(1)}) custom-call(bf16[64,2048]{1,0:T(8,128)(2,1)} %refs_0_.3, bf16[64,2048]{1,0:T(8,128)(2,1)} %copy-done.97, bf16[64,2048]{1,0:T(8,128)(2,1)} %copy-done.93, bf16[64,2048]{1,0:T(8,128)(2,1)} %copy-done.95, ...), custom_call_target="tpu_custom_call" | custom-call | flops 1610612736 | bytes 6553600 | tf_op jit(solution)/shard_map/project/pallas_call | solution.py:575
  32.9 4.2 %collective-permute-start.10 = (f32[8,128]{1,0:T(8,128)S(1)}, f32[8,128]{1,0:T(8,128)S(1)}, u32[]{:S(2)}, u32[]{:S(2)}) collective-permute-start(f32[8,128]{1,0:T(8,128)S(1)} %add_blocks.2.refs_0_), channel_id=1, source_target_pairs={{0,6},{1,7},{2,4},{3,5},{4,2},{5,3},{6,0},{7,1},{8,14},{9,15},{10,... | collective-permute-start | bytes 12296 | tf_op jit(solution)/shard_map/ppermute | solution.py:728
  38.8 2.9 collective-permute-done.9.refs_2_
  41.7 3.4 attend.1
  45.6 2.6 collective-permute-done.11
  48.9 2.0 collective-permute-start.12
  50.9 7.2 %collective-permute-done.13 = bf16[64,2048]{1,0:T(8,128)(2,1)S(1)} collective-permute-done((bf16[64,2048]{1,0:T(8,128)(2,1)S(1)}, bf16[64,2048]{1,0:T(8,128)(2,1)S(1)}, u32[]{:S(2)}, u32[]{:S(2)}) %collective-permute-start.13) | collective-permute-done | bytes 262176 | tf_op jit(solution)/shard_map/ppermute | solution.py:728
  58.1 2.1 collective-permute-start.14
  60.2 6.9 %collective-permute-done.12 = bf16[64,2048]{1,0:T(8,128)(2,1)S(1)} collective-permute-done((bf16[64,2048]{1,0:T(8,128)(2,1)S(1)}, bf16[64,2048]{1,0:T(8,128)(2,1)S(1)}, u32[]{:S(2)}, u32[]{:S(2)}) %collective-permute-start.12) | collective-permute-done | bytes 262176 | tf_op jit(solution)/shard_map/ppermute | solution.py:728
  67.1 5.2 %collective-permute-done.14 = bf16[64,2048]{1,0:T(8,128)(2,1)S(1)} collective-permute-done((bf16[64,2048]{1,0:T(8,128)(2,1)S(1)}, bf16[64,2048]{1,0:T(8,128)(2,1)S(1)}, u32[]{:S(2)}, u32[]{:S(2)}) %collective-permute-start.14) | collective-permute-done | bytes 262176 | tf_op jit(solution)/shard_map/ppermute | solution.py:728
  72.8 1.7 collective-permute-start.15
  74.5 8.3 %collective-permute-done.16.refs_2_ = bf16[64,2048]{1,0:T(8,128)(2,1)S(1)} collective-permute-done((bf16[64,2048]{1,0:T(8,128)(2,1)S(1)}, bf16[64,2048]{1,0:T(8,128)(2,1)S(1)}, u32[]{:S(2)}, u32[]{:S(2)}) %collective-permute-start.16) | collective-permute-done | bytes 262176 | tf_op jit(solution)/shard_map/ppermute | solution.py:728
  83.3 5.8 %collective-permute-done.17.refs_3_ = bf16[64,2048]{1,0:T(8,128)(2,1)S(1)} collective-permute-done((bf16[64,2048]{1,0:T(8,128)(2,1)S(1)}, bf16[64,2048]{1,0:T(8,128)(2,1)S(1)}, u32[]{:S(2)}, u32[]{:S(2)}) %collective-permute-start.17) | collective-permute-done | bytes 262176 | tf_op jit(solution)/shard_map/ppermute | solution.py:728
  90.7 6.6 %ffn.4 = (f32[512,1024]{1,0:T(8,128)S(1)}, f32[512,1024]{1,0:T(8,128)S(1)}, bf16[512,1024]{1,0:T(8,128)(2,1)S(1)}) custom-call(bf16[64,2048]{1,0:T(8,128)(2,1)S(1)} %fusion.22.refs_0_, bf16[64,2048]{1,0:T(8,128)(2,1)S(1)} %collective-permute-done.15.refs_1_, bf16[64,2048]{1,0:T(8,128)(2,1)S(1)} %collective-permute-done.16.refs_2_, ...), custom_call_target="tpu_custom_call" | custom-call | flops 4294967296 | bytes 15728640 | tf_op jit(solution)/shard_map/ffn/pallas_call | solution.py:610
  98.8 2.5 collective-permute-done.22
  103.1 1.6 collective-permute-start.23
  104.8 7.1 %collective-permute-done.24 = bf16[64,2048]{1,0:T(8,128)(2,1)S(1)} collective-permute-done((bf16[64,2048]{1,0:T(8,128)(2,1)S(1)}, bf16[64,2048]{1,0:T(8,128)(2,1)S(1)}, u32[]{:S(2)}, u32[]{:S(2)}) %collective-permute-start.24) | collective-permute-done | bytes 262176 | tf_op jit(solution)/shard_map/ppermute | solution.py:728
  112.0 2.1 collective-permute-start.25
  114.1 6.9 %collective-permute-done.23 = bf16[64,2048]{1,0:T(8,128)(2,1)S(1)} collective-permute-done((bf16[64,2048]{1,0:T(8,128)(2,1)S(1)}, bf16[64,2048]{1,0:T(8,128)(2,1)S(1)}, u32[]{:S(2)}, u32[]{:S(2)}) %collective-permute-start.23) | collective-permute-done | bytes 262176 | tf_op jit(solution)/shard_map/ppermute | solution.py:728
  121.0 5.0 %collective-permute-done.25 = bf16[64,2048]{1,0:T(8,128)(2,1)S(1)} collective-permute-done((bf16[64,2048]{1,0:T(8,128)(2,1)S(1)}, bf16[64,2048]{1,0:T(8,128)(2,1)S(1)}, u32[]{:S(2)}, u32[]{:S(2)}) %collective-permute-start.25) | collective-permute-done | bytes 262176 | tf_op jit(solution)/shard_map/ppermute | solution.py:728
  126.8 6.0 %collective-permute-start.26 = (bf16[64,2048]{1,0:T(8,128)(2,1)S(1)}, bf16[64,2048]{1,0:T(8,128)(2,1)S(1)}, u32[]{:S(2)}, u32[]{:S(2)}) collective-permute-start(bf16[64,2048]{1,0:T(8,128)(2,1)S(1)} %fusion.6.refs_0_), channel_id=1, source_target_pairs={{0,2},{1,3},{2,0},{3,1},{4,6},{5,7},{6,4},{7,5},{8,10},{9,11},{10,... | collective-permute-start | bytes 786440 | tf_op jit(solution)/shard_map/ppermute | solution.py:728
  132.8 1.7 collective-permute-done.27.refs_2_
  134.5 3.0 collective-permute-start.28
  138.0 2.0 collective-permute-done.26.refs_1_
  140.0 2.8 collective-permute-done.28.refs_3_
  144.4 4.0 ffn_back.4
  151.3 1.6 collective-permute-start.54
  157.8 1.8 collective-permute-start.35
  160.0 5.6 %collective-permute-done.35 = bf16[64,2048]{1,0:T(8,128)(2,1)S(1)} collective-permute-done((bf16[64,2048]{1,0:T(8,128)(2,1)S(1)}, bf16[64,2048]{1,0:T(8,128)(2,1)S(1)}, u32[]{:S(2)}, u32[]{:S(2)}) %collective-permute-start.35) | collective-permute-done | bytes 262176 | tf_op jit(solution)/shard_map/ppermute | solution.py:728
  165.6 1.7 collective-permute-start.34
  167.4 10.0 %collective-permute-done.54.refs_7_ = bf16[256,2048]{1,0:T(8,128)(2,1)S(1)} collective-permute-done((bf16[256,2048]{1,0:T(8,128)(2,1)S(1)}, bf16[256,2048]{1,0:T(8,128)(2,1)S(1)}, u32[]{:S(2)}, u32[]{:S(2)}) %collective-permute-start.54) | collective-permute-done | bytes 1048608 | tf_op jit(solution)/shard_map/ppermute | solution.py:728
  177.4 3.1 collective-permute-start.36
  180.5 18.9 %collective-permute-done.72.refs_0_.refs_7_ = bf16[256,2048]{1,0:T(8,128)(2,1)} collective-permute-done((bf16[256,2048]{1,0:T(8,128)(2,1)S(1)}, bf16[256,2048]{1,0:T(8,128)(2,1)}, u32[]{:S(2)}, u32[]{:S(2)}) %collective-permute-start.72) | collective-permute-done | bytes 1048608 | tf_op jit(solution)/shard_map/ppermute | solution.py:728
  203.8 1.6 collective-permute-start.74
  207.8 6.4 %collective-permute-done.57.refs_10_ = bf16[128,2048]{1,0:T(8,128)(2,1)S(1)} collective-permute-done((bf16[128,2048]{1,0:T(8,128)(2,1)S(1)}, bf16[128,2048]{1,0:T(8,128)(2,1)S(1)}, u32[]{:S(2)}, u32[]{:S(2)}) %collective-permute-start.57) | collective-permute-done | bytes 524320 | tf_op jit(solution)/shard_map/ppermute | solution.py:728
  214.2 11.2 %collective-permute-done.75.refs_1_.refs_10_ = bf16[128,2048]{1,0:T(8,128)(2,1)S(1)} collective-permute-done((bf16[128,2048]{1,0:T(8,128)(2,1)S(1)}, bf16[128,2048]{1,0:T(8,128)(2,1)S(1)}, u32[]{:S(2)}, u32[]{:S(2)}) %collective-permute-start.75) | collective-permute-done | bytes 524320 | tf_op jit(solution)/shard_map/ppermute | solution.py:728
  226.5 3.1 collective-permute-start.38
  229.9 9.2 %collective-permute-done.80.refs_0_.refs_11_ = bf16[256,2048]{1,0:T(8,128)(2,1)S(1)} collective-permute-done((bf16[256,2048]{1,0:T(8,128)(2,1)S(1)}, bf16[256,2048]{1,0:T(8,128)(2,1)S(1)}, u32[]{:S(2)}, u32[]{:S(2)}) %collective-permute-start.80) | collective-permute-done | bytes 1048608 | tf_op jit(solution)/shard_map/ppermute | solution.py:728
  239.1 1.6 collective-permute-start.37
  243.0 3.5 collective-permute-done.78.refs_0_.refs_9_
  248.3 5.2 %collective-permute-done.39.refs_3_ = bf16[64,2048]{1,0:T(8,128)(2,1)S(1)} collective-permute-done((bf16[64,2048]{1,0:T(8,128)(2,1)S(1)}, bf16[64,2048]{1,0:T(8,128)(2,1)S(1)}, u32[]{:S(2)}, u32[]{:S(2)}) %collective-permute-start.39) | collective-permute-done | bytes 262176 | tf_op jit(solution)/shard_map/ppermute | solution.py:728
  255.2 5.8 %attend_back.1 = (bf16[512,256]{1,0:T(8,128)(2,1)S(1)}, f32[512,256]{1,0:T(8,128)S(1)}, f32[512,256]{1,0:T(8,128)S(1)}, f32[8,128]{1,0:T(8,128)S(1)}, f32[2,256]{1,0:T(2,128)S(1)}) custom-call(bf16[64,2048]{1,0:T(8,128)(2,1)S(1)} %get-tuple-element.124.refs_0_, bf16[64,2048]{1,0:T(8,128)(2,1)S(1)} %collective-permute-done.37.refs_1_, ...), custom_call_target="tpu_custom_call" | custom-call | flops 335544320 | bytes 3407872 | tf_op jit(solution)/shard_map/attend_back/pallas_call | solution.py:249
  268.9 2.2 copy-done.9
  271.1 2.2 copy-done.60
  273.3 6.6 %ffn.7 = (f32[512,1024]{1,0:T(8,128)S(1)}, f32[512,1024]{1,0:T(8,128)S(1)}, bf16[512,1024]{1,0:T(8,128)(2,1)S(1)}) custom-call(bf16[128,2048]{1,0:T(8,128)(2,1)S(1)} %copy-done.71, bf16[128,2048]{1,0:T(8,128)(2,1)S(1)} %copy-done.69, bf16[128,2048]{1,0:T(8,128)(2,1)S(1)} %copy-done.75, bf16[128,2048]{1,0:T(8,128)(2,1)S(1)} %copy-done.73, ...), custom_call_target="tpu_custom_call" | custom-call | flops 4294967296 | bytes 15728640 | tf_op jit(solution)/shard_map/ffn/pallas_call | solution.py:610
  282.7 8.8 %ffn.5 = (f32[512,1024]{1,0:T(8,128)S(1)}, f32[512,1024]{1,0:T(8,128)S(1)}, bf16[512,1024]{1,0:T(8,128)(2,1)S(1)}) custom-call(bf16[256,2048]{1,0:T(8,128)(2,1)} %collective-permute-done.70.refs_0_.refs_5_, bf16[256,2048]{1,0:T(8,128)(2,1)} %collective-permute-done.71.refs_1_.refs_6_, bf16[2048,1024]{1,0:T(8,128)(2,1)S(1)} %copy-done.9, ...), custom_call_target="tpu_custom_call" | custom-call | flops 4294967296 | bytes 15728640 | tf_op jit(solution)/shard_map/ffn/pallas_call | solution.py:610
  292.4 3.6 collective-permute-start.47
  298.6 8.0 %ffn.6 = (f32[512,1024]{1,0:T(8,128)S(1)}, f32[512,1024]{1,0:T(8,128)S(1)}, bf16[512,1024]{1,0:T(8,128)(2,1)S(1)}) custom-call(bf16[256,2048]{1,0:T(8,128)(2,1)} %collective-permute-done.72.refs_0_.refs_7_, bf16[256,2048]{1,0:T(8,128)(2,1)} %collective-permute-done.73.refs_1_.refs_8_, bf16[2048,1024]{1,0:T(8,128)(2,1)S(1)} %copy-done.10, ...), custom_call_target="tpu_custom_call" | custom-call | flops 4294967296 | bytes 15728640 | tf_op jit(solution)/shard_map/ffn/pallas_call | solution.py:610
  306.7 3.6 collective-permute-start.45
  310.3 4.9 %ffn_back.5 = (bf16[512,1024]{1,0:T(8,128)(2,1)S(1)}, bf16[512,1024]{1,0:T(8,128)(2,1)S(1)}) custom-call(bf16[256,2048]{1,0:T(8,128)(2,1)S(1)} %collective-permute-done.78.refs_0_.refs_9_, bf16[256,2048]{1,0:T(8,128)(2,1)} %collective-permute-done.79.refs_1_.refs_10_, bf16[1024,2048]{1,0:T(8,128)(2,1)S(1)} %copy-done.1, ...), custom_call_target="tpu_custom_call" | custom-call | flops 2147483648 | bytes 12582912 | tf_op jit(solution)/shard_map/ffn_back/pallas_call | solution.py:644
  318.3 5.0 %ffn_back.6 = (bf16[512,1024]{1,0:T(8,128)(2,1)S(1)}, bf16[512,1024]{1,0:T(8,128)(2,1)S(1)}) custom-call(bf16[256,2048]{1,0:T(8,128)(2,1)S(1)} %collective-permute-done.80.refs_0_.refs_11_, bf16[256,2048]{1,0:T(8,128)(2,1)} %collective-permute-done.81.refs_1_.refs_12_, bf16[1024,2048]{1,0:T(8,128)(2,1)S(1)} %copy-done.1, ...), custom_call_target="tpu_custom_call" | custom-call | flops 2147483648 | bytes 12582912 | tf_op jit(solution)/shard_map/ffn_back/pallas_call | solution.py:644
  326.0 1.7 tokens_back.2
  330.1 1.8 collective-permute-start.69
  331.8 14.9 %weight_grad.7 = f32[1024,2048]{1,0:T(8,128)} custom-call(bf16[512,1024]{1,0:T(8,128)(2,1)} %copy-done.49, bf16[512,1024]{1,0:T(8,128)(2,1)} %copy-done.81, bf16[512,1024]{1,0:T(8,128)(2,1)} %copy-done.82, bf16[512,1024]{1,0:T(8,128)(2,1)} %copy-done.80, bf16[256,2048]{1,0:T(8,128)(2,1)} %copy-done.88, bf16[64,2048]{1,0:T(8,128)(2,1)} %copy-done.50, ...), custom_call_target="tpu_custom_call" | custom-call | flops 8589934592 | bytes 20971520 | tf_op jit(solution)/shard_map/weight_grad/pallas_call | solution.py:698
  348.9 6.0 %ffn_back.7 = (bf16[512,1024]{1,0:T(8,128)(2,1)S(1)}, bf16[512,1024]{1,0:T(8,128)(2,1)S(1)}) custom-call(bf16[128,2048]{1,0:T(8,128)(2,1)S(1)} %copy-done.38, bf16[128,2048]{1,0:T(8,128)(2,1)S(1)} %copy-done.36, bf16[128,2048]{1,0:T(8,128)(2,1)S(1)} %copy-done.42, bf16[128,2048]{1,0:T(8,128)(2,1)S(1)} %copy-done.40, bf16[1024,2048]{1,0:T(8,128)(2,1)} %refs_4_.3, ...), custom_call_target="tpu_custom_call" | custom-call | flops 2147483648 | bytes 12582912 | tf_op jit(solution)/shard_map/ffn_back/pallas_call | solution.py:644
  359.2 14.2 %weight_grad.5 = f32[2048,1024]{1,0:T(8,128)} custom-call(bf16[256,2048]{1,0:T(8,128)(2,1)} %copy-done.87, bf16[64,2048]{1,0:T(8,128)(2,1)} %copy-done.76, bf16[64,2048]{1,0:T(8,128)(2,1)} %copy-done.78, bf16[64,2048]{1,0:T(8,128)(2,1)} %copy-done.77, bf16[64,2048]{1,0:T(8,128)(2,1)} %copy-done.79, ...), custom_call_target="tpu_custom_call" | custom-call | flops 8589934592 | bytes 20971520 | tf_op jit(solution)/shard_map/weight_grad/pallas_call | solution.py:698
  375.9 13.9 %weight_grad.6 = f32[2048,1024]{1,0:T(8,128)} custom-call(bf16[256,2048]{1,0:T(8,128)(2,1)} %copy-done.87, bf16[64,2048]{1,0:T(8,128)(2,1)} %copy-done.76, bf16[64,2048]{1,0:T(8,128)(2,1)} %copy-done.78, bf16[64,2048]{1,0:T(8,128)(2,1)} %copy-done.77, bf16[64,2048]{1,0:T(8,128)(2,1)} %copy-done.79, ...), custom_call_target="tpu_custom_call" | custom-call | flops 8589934592 | bytes 20971520 | tf_op jit(solution)/shard_map/weight_grad/pallas_call | solution.py:698
  391.3 1.8 tokens_back.3
  393.7 2.6 collective-permute-start.50
  399.4 10.9 %weight_grad.4 = (f32[2048,256]{1,0:T(8,128)}, f32[2048,256]{1,0:T(8,128)}, f32[2048,256]{1,0:T(8,128)}) custom-call(bf16[256,2048]{1,0:T(8,128)(2,1)} %copy-done.101, bf16[64,2048]{1,0:T(8,128)(2,1)} %copy-done.110, bf16[64,2048]{1,0:T(8,128)(2,1)} %copy-done.112, bf16[64,2048]{1,0:T(8,128)(2,1)} %copy-done.111, bf16[64,2048]{1,0:T(8,128)(2,1)} %copy-done.113, ...), custom_call_target="tpu_custom_call" | custom-call | flops 6442450944 | bytes 17825792 | tf_op jit(solution)/shard_map/weight_grad/pallas_call | solution.py:698
  412.0 3.1 collective-permute-done.50
  (406 shorter events, 78.5 us)
Async XLA Ops:
  0.6 16.4 %collective-permute-start.1 = (bf16[64,2048]{1,0:T(8,128)(2,1)}, bf16[64,2048]{1,0:T(8,128)(2,1)S(1)}, u32[]{:S(2)}, u32[]{:S(2)}) collective-permute-start(bf16[64,2048]{1,0:T(8,128)(2,1)} %refs_0_.3), channel_id=1, source_target_pairs={{0,4},{1,5},{2,6},{3,7},{4,0},{5,1},{6,2},{7,3},{8,12},{9,13},{10,... | collective-permute-start | bytes 786440 | tf_op jit(solution)/shard_map/ppermute | solution.py:728
  4.8 13.6 %collective-permute-start = (bf16[64,2048]{1,0:T(8,128)(2,1)}, bf16[64,2048]{1,0:T(8,128)(2,1)S(1)}, u32[]{:S(2)}, u32[]{:S(2)}) collective-permute-start(bf16[64,2048]{1,0:T(8,128)(2,1)} %refs_0_.3), channel_id=1, source_target_pairs={{0,2},{1,3},{2,0},{3,1},{4,6},{5,7},{6,4},{7,5},{8,10},{9,11},{10,... | collective-permute-start | bytes 786440 | tf_op jit(solution)/shard_map/ppermute | solution.py:728
  17.0 7.4 %collective-permute-start.2 = (bf16[64,2048]{1,0:T(8,128)(2,1)S(1)}, bf16[64,2048]{1,0:T(8,128)(2,1)S(1)}, u32[]{:S(2)}, u32[]{:S(2)}) collective-permute-start(bf16[64,2048]{1,0:T(8,128)(2,1)S(1)} %collective-permute-done.1.refs_2_), channel_id=1, source_target_pairs={{0,2},{1,3},{2,0},{3,1},{4,6},{5,7},{6,4},{7,5},{8,10},{9,11},{10,... | collective-permute-start | bytes 786440 | tf_op jit(solution)/shard_map/ppermute | solution.py:728
  17.7 7.7 %collective-permute-start.3 = (bf16[64,2048]{1,0:T(8,128)(2,1)}, bf16[64,2048]{1,0:T(8,128)(2,1)S(1)}, u32[]{:S(2)}, u32[]{:S(2)}) collective-permute-start(bf16[64,2048]{1,0:T(8,128)(2,1)} %refs_0_.3), channel_id=1, source_target_pairs={{0,1},{1,0},{2,3},{3,2},{4,5},{5,4},{6,7},{7,6},{8,9},{9,8},{10,11... | collective-permute-start | bytes 786440 | tf_op jit(solution)/shard_map/ppermute | solution.py:728
  17.8 7.7 %collective-permute-start.5 = (bf16[64,2048]{1,0:T(8,128)(2,1)S(1)}, bf16[64,2048]{1,0:T(8,128)(2,1)S(1)}, u32[]{:S(2)}, u32[]{:S(2)}) collective-permute-start(bf16[64,2048]{1,0:T(8,128)(2,1)S(1)} %collective-permute-done.1.refs_2_), channel_id=1, source_target_pairs={{0,1},{1,0},{2,3},{3,2},{4,5},{5,4},{6,7},{7,6},{8,9},{9,8},{10,11... | collective-permute-start | bytes 786440 | tf_op jit(solution)/shard_map/ppermute | solution.py:728
  18.3 7.2 %collective-permute-start.4 = (bf16[64,2048]{1,0:T(8,128)(2,1)S(1)}, bf16[64,2048]{1,0:T(8,128)(2,1)S(1)}, u32[]{:S(2)}, u32[]{:S(2)}) collective-permute-start(bf16[64,2048]{1,0:T(8,128)(2,1)S(1)} %collective-permute-done.refs_1_), channel_id=1, source_target_pairs={{0,1},{1,0},{2,3},{3,2},{4,5},{5,4},{6,7},{7,6},{8,9},{9,8},{10,11... | collective-permute-start | bytes 786440 | tf_op jit(solution)/shard_map/ppermute | solution.py:728
  48.8 9.2 %collective-permute-start.13 = (bf16[64,2048]{1,0:T(8,128)(2,1)S(1)}, bf16[64,2048]{1,0:T(8,128)(2,1)S(1)}, u32[]{:S(2)}, u32[]{:S(2)}) collective-permute-start(bf16[64,2048]{1,0:T(8,128)(2,1)S(1)} %get-tuple-element.123), channel_id=1, source_target_pairs={{0,2},{1,3},{2,0},{3,1},{4,6},{5,7},{6,4},{7,5},{8,10},{9,11},{10,... | collective-permute-start | bytes 786440 | tf_op jit(solution)/shard_map/ppermute | solution.py:728
  48.9 18.2 %collective-permute-start.12 = (bf16[64,2048]{1,0:T(8,128)(2,1)S(1)}, bf16[64,2048]{1,0:T(8,128)(2,1)S(1)}, u32[]{:S(2)}, u32[]{:S(2)}) collective-permute-start(bf16[64,2048]{1,0:T(8,128)(2,1)S(1)} %get-tuple-element.122), channel_id=1, source_target_pairs={{0,2},{1,3},{2,0},{3,1},{4,6},{5,7},{6,4},{7,5},{8,10},{9,11},{10,... | collective-permute-start | bytes 786440 | tf_op jit(solution)/shard_map/ppermute | solution.py:728
  58.1 14.2 %collective-permute-start.14 = (bf16[64,2048]{1,0:T(8,128)(2,1)S(1)}, bf16[64,2048]{1,0:T(8,128)(2,1)S(1)}, u32[]{:S(2)}, u32[]{:S(2)}) collective-permute-start(bf16[64,2048]{1,0:T(8,128)(2,1)S(1)} %fusion.12), channel_id=1, source_target_pairs={{0,4},{1,5},{2,6},{3,7},{4,0},{5,1},{6,2},{7,3},{8,12},{9,13},{10,... | collective-permute-start | bytes 786440 | tf_op jit(solution)/shard_map/ppermute | solution.py:728
  72.7 10.0 %collective-permute-start.16 = (bf16[64,2048]{1,0:T(8,128)(2,1)S(1)}, bf16[64,2048]{1,0:T(8,128)(2,1)S(1)}, u32[]{:S(2)}, u32[]{:S(2)}) collective-permute-start(bf16[64,2048]{1,0:T(8,128)(2,1)S(1)} %fusion.22.refs_0_), channel_id=1, source_target_pairs={{0,4},{1,5},{2,6},{3,7},{4,0},{5,1},{6,2},{7,3},{8,12},{9,13},{10,... | collective-permute-start | bytes 786440 | tf_op jit(solution)/shard_map/ppermute | solution.py:728
  72.8 10.5 %collective-permute-start.15 = (bf16[64,2048]{1,0:T(8,128)(2,1)S(1)}, bf16[64,2048]{1,0:T(8,128)(2,1)S(1)}, u32[]{:S(2)}, u32[]{:S(2)}) collective-permute-start(bf16[64,2048]{1,0:T(8,128)(2,1)S(1)} %fusion.22.refs_0_), channel_id=1, source_target_pairs={{0,2},{1,3},{2,0},{3,1},{4,6},{5,7},{6,4},{7,5},{8,10},{9,11},{10,... | collective-permute-start | bytes 786440 | tf_op jit(solution)/shard_map/ppermute | solution.py:728
  102.7 9.2 %collective-permute-start.24 = (bf16[64,2048]{1,0:T(8,128)(2,1)S(1)}, bf16[64,2048]{1,0:T(8,128)(2,1)S(1)}, u32[]{:S(2)}, u32[]{:S(2)}) collective-permute-start(bf16[64,2048]{1,0:T(8,128)(2,1)S(1)} %get-tuple-element.121), channel_id=1, source_target_pairs={{0,2},{1,3},{2,0},{3,1},{4,6},{5,7},{6,4},{7,5},{8,10},{9,11},{10,... | collective-permute-start | bytes 786440 | tf_op jit(solution)/shard_map/ppermute | solution.py:728
  103.1 17.8 %collective-permute-start.23 = (bf16[64,2048]{1,0:T(8,128)(2,1)S(1)}, bf16[64,2048]{1,0:T(8,128)(2,1)S(1)}, u32[]{:S(2)}, u32[]{:S(2)}) collective-permute-start(bf16[64,2048]{1,0:T(8,128)(2,1)S(1)} %get-tuple-element.120), channel_id=1, source_target_pairs={{0,2},{1,3},{2,0},{3,1},{4,6},{5,7},{6,4},{7,5},{8,10},{9,11},{10,... | collective-permute-start | bytes 786440 | tf_op jit(solution)/shard_map/ppermute | solution.py:728
  112.0 14.0 %collective-permute-start.25 = (bf16[64,2048]{1,0:T(8,128)(2,1)S(1)}, bf16[64,2048]{1,0:T(8,128)(2,1)S(1)}, u32[]{:S(2)}, u32[]{:S(2)}) collective-permute-start(bf16[64,2048]{1,0:T(8,128)(2,1)S(1)} %fusion.10), channel_id=1, source_target_pairs={{0,4},{1,5},{2,6},{3,7},{4,0},{5,1},{6,2},{7,3},{8,12},{9,13},{10,... | collective-permute-start | bytes 786440 | tf_op jit(solution)/shard_map/ppermute | solution.py:728
  126.7 7.8 %collective-permute-start.27 = (bf16[64,2048]{1,0:T(8,128)(2,1)S(1)}, bf16[64,2048]{1,0:T(8,128)(2,1)S(1)}, u32[]{:S(2)}, u32[]{:S(2)}) collective-permute-start(bf16[64,2048]{1,0:T(8,128)(2,1)S(1)} %fusion.6.refs_0_), channel_id=1, source_target_pairs={{0,4},{1,5},{2,6},{3,7},{4,0},{5,1},{6,2},{7,3},{8,12},{9,13},{10,... | collective-permute-start | bytes 786440 | tf_op jit(solution)/shard_map/ppermute | solution.py:728
  126.8 13.3 %collective-permute-start.26 = (bf16[64,2048]{1,0:T(8,128)(2,1)S(1)}, bf16[64,2048]{1,0:T(8,128)(2,1)S(1)}, u32[]{:S(2)}, u32[]{:S(2)}) collective-permute-start(bf16[64,2048]{1,0:T(8,128)(2,1)S(1)} %fusion.6.refs_0_), channel_id=1, source_target_pairs={{0,2},{1,3},{2,0},{3,1},{4,6},{5,7},{6,4},{7,5},{8,10},{9,11},{10,... | collective-permute-start | bytes 786440 | tf_op jit(solution)/shard_map/ppermute | solution.py:728
  134.5 8.4 %collective-permute-start.28 = (bf16[64,2048]{1,0:T(8,128)(2,1)S(1)}, bf16[64,2048]{1,0:T(8,128)(2,1)S(1)}, u32[]{:S(2)}, u32[]{:S(2)}) collective-permute-start(bf16[64,2048]{1,0:T(8,128)(2,1)S(1)} %collective-permute-done.27.refs_2_), channel_id=1, source_target_pairs={{0,2},{1,3},{2,0},{3,1},{4,6},{5,7},{6,4},{7,5},{8,10},{9,11},{10,... | collective-permute-start | bytes 786440 | tf_op jit(solution)/shard_map/ppermute | solution.py:728
  151.3 26.1 %collective-permute-start.54 = (bf16[256,2048]{1,0:T(8,128)(2,1)S(1)}, bf16[256,2048]{1,0:T(8,128)(2,1)S(1)}, u32[]{:S(2)}, u32[]{:S(2)}) collective-permute-start(bf16[256,2048]{1,0:T(8,128)(2,1)S(1)} %constant_dynamic-update-slice_fusion.refs_0_), channel_id=1, source_target_pairs={{0,16},{8,24},{16,0},{24,8},{1,17},{9,25},{17,1},{25,9},{2,18},{10... | collective-permute-start | bytes 3145736 | tf_op jit(solution)/shard_map/ppermute | solution.py:728
  153.0 46.4 %collective-permute-start.72 = (bf16[256,2048]{1,0:T(8,128)(2,1)S(1)}, bf16[256,2048]{1,0:T(8,128)(2,1)}, u32[]{:S(2)}, u32[]{:S(2)}) collective-permute-start(bf16[256,2048]{1,0:T(8,128)(2,1)S(1)} %pad_maximum_fusion.refs_0_), channel_id=1, source_target_pairs={{0,16},{8,24},{16,0},{24,8},{1,17},{9,25},{17,1},{25,9},{2,18},{10... | collective-permute-start | bytes 3145736 | tf_op jit(solution)/shard_map/ppermute | solution.py:728
  153.6 48.4 %collective-permute-start.70 = (bf16[256,2048]{1,0:T(8,128)(2,1)S(1)}, bf16[256,2048]{1,0:T(8,128)(2,1)}, u32[]{:S(2)}, u32[]{:S(2)}) collective-permute-start(bf16[256,2048]{1,0:T(8,128)(2,1)S(1)} %pad_maximum_fusion.refs_0_), channel_id=1, source_target_pairs={{0,8},{8,0},{16,24},{24,16},{1,9},{9,1},{17,25},{25,17},{2,10},{10... | collective-permute-start | bytes 3145736 | tf_op jit(solution)/shard_map/ppermute | solution.py:728
  157.8 7.8 %collective-permute-start.35 = (bf16[64,2048]{1,0:T(8,128)(2,1)S(1)}, bf16[64,2048]{1,0:T(8,128)(2,1)S(1)}, u32[]{:S(2)}, u32[]{:S(2)}) collective-permute-start(bf16[64,2048]{1,0:T(8,128)(2,1)S(1)} %get-tuple-element.119), channel_id=1, source_target_pairs={{0,2},{1,3},{2,0},{3,1},{4,6},{5,7},{6,4},{7,5},{8,10},{9,11},{10,... | collective-permute-start | bytes 786440 | tf_op jit(solution)/shard_map/ppermute | solution.py:728
  159.6 46.6 %collective-permute-start.52 = (bf16[256,2048]{1,0:T(8,128)(2,1)S(1)}, bf16[256,2048]{1,0:T(8,128)(2,1)S(1)}, u32[]{:S(2)}, u32[]{:S(2)}) collective-permute-start(bf16[256,2048]{1,0:T(8,128)(2,1)S(1)} %constant_dynamic-update-slice_fusion.refs_0_), channel_id=1, source_target_pairs={{0,8},{8,0},{16,24},{24,16},{1,9},{9,1},{17,25},{25,17},{2,10},{10... | collective-permute-start | bytes 3145736 | tf_op jit(solution)/shard_map/ppermute | solution.py:728
  165.6 38.2 %collective-permute-start.34 = (bf16[64,2048]{1,0:T(8,128)(2,1)S(1)}, bf16[64,2048]{1,0:T(8,128)(2,1)S(1)}, u32[]{:S(2)}, u32[]{:S(2)}) collective-permute-start(bf16[64,2048]{1,0:T(8,128)(2,1)S(1)} %get-tuple-element.118), channel_id=1, source_target_pairs={{0,2},{1,3},{2,0},{3,1},{4,6},{5,7},{6,4},{7,5},{8,10},{9,11},{10,... | collective-permute-start | bytes 786440 | tf_op jit(solution)/shard_map/ppermute | solution.py:728
  177.4 28.0 %collective-permute-start.36 = (bf16[64,2048]{1,0:T(8,128)(2,1)S(1)}, bf16[64,2048]{1,0:T(8,128)(2,1)S(1)}, u32[]{:S(2)}, u32[]{:S(2)}) collective-permute-start(bf16[64,2048]{1,0:T(8,128)(2,1)S(1)} %fusion.8), channel_id=1, source_target_pairs={{0,4},{1,5},{2,6},{3,7},{4,0},{5,1},{6,2},{7,3},{8,12},{9,13},{10,... | collective-permute-start | bytes 786440 | tf_op jit(solution)/shard_map/ppermute | solution.py:728
  199.4 14.8 %collective-permute-start.57 = (bf16[128,2048]{1,0:T(8,128)(2,1)S(1)}, bf16[128,2048]{1,0:T(8,128)(2,1)S(1)}, u32[]{:S(2)}, u32[]{:S(2)}) collective-permute-start(bf16[128,2048]{1,0:T(8,128)(2,1)S(1)} %slice.131), channel_id=1, source_target_pairs={{0,8},{8,0},{16,24},{24,16},{1,9},{9,1},{17,25},{25,17},{2,10},{10... | collective-permute-start | bytes 1572872 | tf_op jit(solution)/shard_map/ppermute | solution.py:728
  202.0 23.4 %collective-permute-start.75 = (bf16[128,2048]{1,0:T(8,128)(2,1)S(1)}, bf16[128,2048]{1,0:T(8,128)(2,1)S(1)}, u32[]{:S(2)}, u32[]{:S(2)}) collective-permute-start(bf16[128,2048]{1,0:T(8,128)(2,1)S(1)} %slice.135), channel_id=1, source_target_pairs={{0,8},{8,0},{16,24},{24,16},{1,9},{9,1},{17,25},{25,17},{2,10},{10... | collective-permute-start | bytes 1572872 | tf_op jit(solution)/shard_map/ppermute | solution.py:728
  203.8 22.7 %collective-permute-start.74 = (bf16[128,2048]{1,0:T(8,128)(2,1)S(1)}, bf16[128,2048]{1,0:T(8,128)(2,1)S(1)}, u32[]{:S(2)}, u32[]{:S(2)}) collective-permute-start(bf16[128,2048]{1,0:T(8,128)(2,1)S(1)} %slice.134), channel_id=1, source_target_pairs={{0,16},{8,24},{16,0},{24,8},{1,17},{9,25},{17,1},{25,9},{2,18},{10... | collective-permute-start | bytes 1572872 | tf_op jit(solution)/shard_map/ppermute | solution.py:728
  205.4 33.7 %collective-permute-start.80 = (bf16[256,2048]{1,0:T(8,128)(2,1)S(1)}, bf16[256,2048]{1,0:T(8,128)(2,1)S(1)}, u32[]{:S(2)}, u32[]{:S(2)}) collective-permute-start(bf16[256,2048]{1,0:T(8,128)(2,1)S(1)} %pad_maximum_fusion.1.refs_4_), channel_id=1, source_target_pairs={{0,16},{8,24},{16,0},{24,8},{1,17},{9,25},{17,1},{25,9},{2,18},{10... | collective-permute-start | bytes 3145736 | tf_op jit(solution)/shard_map/ppermute | solution.py:728
  206.2 40.2 %collective-permute-start.78 = (bf16[256,2048]{1,0:T(8,128)(2,1)S(1)}, bf16[256,2048]{1,0:T(8,128)(2,1)S(1)}, u32[]{:S(2)}, u32[]{:S(2)}) collective-permute-start(bf16[256,2048]{1,0:T(8,128)(2,1)S(1)} %pad_maximum_fusion.1.refs_4_), channel_id=1, source_target_pairs={{0,8},{8,0},{16,24},{24,16},{1,9},{9,1},{17,25},{25,17},{2,10},{10... | collective-permute-start | bytes 3145736 | tf_op jit(solution)/shard_map/ppermute | solution.py:728
  214.2 51.6 %collective-permute-start.71 = (bf16[256,2048]{1,0:T(8,128)(2,1)}, bf16[256,2048]{1,0:T(8,128)(2,1)}, u32[]{:S(2)}, u32[]{:S(2)}) collective-permute-start(bf16[256,2048]{1,0:T(8,128)(2,1)} %collective-permute-done.70.refs_0_.refs_5_), channel_id=1, source_target_pairs={{0,1},{1,0},{2,3},{3,2},{4,5},{5,4},{6,7},{7,6},{8,9},{9,8},{10,11... | collective-permute-start | bytes 3145736 | tf_op jit(solution)/shard_map/ppermute | solution.py:728
  226.5 15.8 %collective-permute-start.38 = (bf16[64,2048]{1,0:T(8,128)(2,1)S(1)}, bf16[64,2048]{1,0:T(8,128)(2,1)S(1)}, u32[]{:S(2)}, u32[]{:S(2)}) collective-permute-start(bf16[64,2048]{1,0:T(8,128)(2,1)S(1)} %get-tuple-element.124.refs_0_), channel_id=1, source_target_pairs={{0,4},{1,5},{2,6},{3,7},{4,0},{5,1},{6,2},{7,3},{8,12},{9,13},{10,... | collective-permute-start | bytes 786440 | tf_op jit(solution)/shard_map/ppermute | solution.py:728
  229.7 16.8 %collective-permute-start.40 = (bf16[64,2048]{1,0:T(8,128)(2,1)S(1)}, bf16[64,2048]{1,0:T(8,128)(2,1)S(1)}, u32[]{:S(2)}, u32[]{:S(2)}) collective-permute-start(bf16[64,2048]{1,0:T(8,128)(2,1)S(1)} %get-tuple-element.124.refs_0_), channel_id=1, source_target_pairs={{0,1},{1,0},{2,3},{3,2},{4,5},{5,4},{6,7},{7,6},{8,9},{9,8},{10,11... | collective-permute-start | bytes 786440 | tf_op jit(solution)/shard_map/ppermute | solution.py:728
  239.1 9.2 %collective-permute-start.37 = (bf16[64,2048]{1,0:T(8,128)(2,1)S(1)}, bf16[64,2048]{1,0:T(8,128)(2,1)S(1)}, u32[]{:S(2)}, u32[]{:S(2)}) collective-permute-start(bf16[64,2048]{1,0:T(8,128)(2,1)S(1)} %get-tuple-element.124.refs_0_), channel_id=1, source_target_pairs={{0,2},{1,3},{2,0},{3,1},{4,6},{5,7},{6,4},{7,5},{8,10},{9,11},{10,... | collective-permute-start | bytes 786440 | tf_op jit(solution)/shard_map/ppermute | solution.py:728
  242.4 11.1 %collective-permute-start.39 = (bf16[64,2048]{1,0:T(8,128)(2,1)S(1)}, bf16[64,2048]{1,0:T(8,128)(2,1)S(1)}, u32[]{:S(2)}, u32[]{:S(2)}) collective-permute-start(bf16[64,2048]{1,0:T(8,128)(2,1)S(1)} %collective-permute-done.38.refs_2_), channel_id=1, source_target_pairs={{0,2},{1,3},{2,0},{3,1},{4,6},{5,7},{6,4},{7,5},{8,10},{9,11},{10,... | collective-permute-start | bytes 786440 | tf_op jit(solution)/shard_map/ppermute | solution.py:728
  246.5 16.9 %collective-permute-start.76 = (bf16[128,2048]{1,0:T(8,128)(2,1)S(1)}, bf16[128,2048]{1,0:T(8,128)(2,1)S(1)}, u32[]{:S(2)}, u32[]{:S(2)}) collective-permute-start(bf16[128,2048]{1,0:T(8,128)(2,1)S(1)} %collective-permute-done.74.refs_0_.refs_9_), channel_id=1, source_target_pairs={{0,1},{1,0},{2,3},{3,2},{4,5},{5,4},{6,7},{7,6},{8,9},{9,8},{10,11... | collective-permute-start | bytes 1572872 | tf_op jit(solution)/shard_map/ppermute | solution.py:728
  246.5 7.0 %collective-permute-start.42 = (bf16[64,2048]{1,0:T(8,128)(2,1)S(1)}, bf16[64,2048]{1,0:T(8,128)(2,1)S(1)}, u32[]{:S(2)}, u32[]{:S(2)}) collective-permute-start(bf16[64,2048]{1,0:T(8,128)(2,1)S(1)} %collective-permute-done.38.refs_2_), channel_id=1, source_target_pairs={{0,1},{1,0},{2,3},{3,2},{4,5},{5,4},{6,7},{7,6},{8,9},{9,8},{10,11... | collective-permute-start | bytes 786440 | tf_op jit(solution)/shard_map/ppermute | solution.py:728
  253.5 38.9 %collective-permute-start.73 = (bf16[256,2048]{1,0:T(8,128)(2,1)}, bf16[256,2048]{1,0:T(8,128)(2,1)}, u32[]{:S(2)}, u32[]{:S(2)}) collective-permute-start(bf16[256,2048]{1,0:T(8,128)(2,1)} %collective-permute-done.72.refs_0_.refs_7_), channel_id=1, source_target_pairs={{0,1},{1,0},{2,3},{3,2},{4,5},{5,4},{6,7},{7,6},{8,9},{9,8},{10,11... | collective-permute-start | bytes 3145736 | tf_op jit(solution)/shard_map/ppermute | solution.py:728
  254.0 43.5 %collective-permute-start.81 = (bf16[256,2048]{1,0:T(8,128)(2,1)S(1)}, bf16[256,2048]{1,0:T(8,128)(2,1)}, u32[]{:S(2)}, u32[]{:S(2)}) collective-permute-start(bf16[256,2048]{1,0:T(8,128)(2,1)S(1)} %collective-permute-done.80.refs_0_.refs_11_), channel_id=1, source_target_pairs={{0,1},{1,0},{2,3},{3,2},{4,5},{5,4},{6,7},{7,6},{8,9},{9,8},{10,11... | collective-permute-start | bytes 3145736 | tf_op jit(solution)/shard_map/ppermute | solution.py:728
  255.0 43.0 %collective-permute-start.79 = (bf16[256,2048]{1,0:T(8,128)(2,1)S(1)}, bf16[256,2048]{1,0:T(8,128)(2,1)}, u32[]{:S(2)}, u32[]{:S(2)}) collective-permute-start(bf16[256,2048]{1,0:T(8,128)(2,1)S(1)} %collective-permute-done.78.refs_0_.refs_9_), channel_id=1, source_target_pairs={{0,1},{1,0},{2,3},{3,2},{4,5},{5,4},{6,7},{7,6},{8,9},{9,8},{10,11... | collective-permute-start | bytes 3145736 | tf_op jit(solution)/shard_map/ppermute | solution.py:728
  265.8 31.1 %collective-permute-start.83 = (bf16[128,2048]{1,0:T(8,128)(2,1)S(1)}, bf16[128,2048]{1,0:T(8,128)(2,1)S(1)}, u32[]{:S(2)}, u32[]{:S(2)}) collective-permute-start(bf16[128,2048]{1,0:T(8,128)(2,1)S(1)} %slice.137), channel_id=1, source_target_pairs={{0,8},{8,0},{16,24},{24,16},{1,9},{9,1},{17,25},{25,17},{2,10},{10... | collective-permute-start | bytes 1572872 | tf_op jit(solution)/shard_map/ppermute | solution.py:728
  267.4 30.2 %collective-permute-start.82 = (bf16[128,2048]{1,0:T(8,128)(2,1)S(1)}, bf16[128,2048]{1,0:T(8,128)(2,1)S(1)}, u32[]{:S(2)}, u32[]{:S(2)}) collective-permute-start(bf16[128,2048]{1,0:T(8,128)(2,1)S(1)} %slice.136), channel_id=1, source_target_pairs={{0,16},{8,24},{16,0},{24,8},{1,17},{9,25},{17,1},{25,9},{2,18},{10... | collective-permute-start | bytes 1572872 | tf_op jit(solution)/shard_map/ppermute | solution.py:728
  296.9 31.7 %collective-permute-start.56 = (bf16[128,2048]{1,0:T(8,128)(2,1)S(1)}, bf16[128,2048]{1,0:T(8,128)(2,1)S(1)}, u32[]{:S(2)}, u32[]{:S(2)}) collective-permute-start(bf16[128,2048]{1,0:T(8,128)(2,1)S(1)} %slice.130), channel_id=1, source_target_pairs={{0,16},{8,24},{16,0},{24,8},{1,17},{9,25},{17,1},{25,9},{2,18},{10... | collective-permute-start | bytes 1572872 | tf_op jit(solution)/shard_map/ppermute | solution.py:728
  297.5 32.5 %collective-permute-start.85 = (bf16[128,2048]{1,0:T(8,128)(2,1)S(1)}, bf16[128,2048]{1,0:T(8,128)(2,1)S(1)}, u32[]{:S(2)}, u32[]{:S(2)}) collective-permute-start(bf16[128,2048]{1,0:T(8,128)(2,1)S(1)} %collective-permute-done.83.refs_1_.refs_14_), channel_id=1, source_target_pairs={{0,1},{1,0},{2,3},{3,2},{4,5},{5,4},{6,7},{7,6},{8,9},{9,8},{10,11... | collective-permute-start | bytes 1572872 | tf_op jit(solution)/shard_map/ppermute | solution.py:728
  297.5 32.5 %collective-permute-start.84 = (bf16[128,2048]{1,0:T(8,128)(2,1)S(1)}, bf16[128,2048]{1,0:T(8,128)(2,1)S(1)}, u32[]{:S(2)}, u32[]{:S(2)}) collective-permute-start(bf16[128,2048]{1,0:T(8,128)(2,1)S(1)} %collective-permute-done.82.refs_0_.refs_13_), channel_id=1, source_target_pairs={{0,1},{1,0},{2,3},{3,2},{4,5},{5,4},{6,7},{7,6},{8,9},{9,8},{10,11... | collective-permute-start | bytes 1572872 | tf_op jit(solution)/shard_map/ppermute | solution.py:728
  298.0 18.8 %collective-permute-start.64 = (bf16[64,2048]{1,0:T(8,128)(2,1)S(1)}, bf16[64,2048]{1,0:T(8,128)(2,1)S(1)}, u32[]{:S(2)}, u32[]{:S(2)}) collective-permute-start(bf16[64,2048]{1,0:T(8,128)(2,1)S(1)} %get-tuple-element.87), channel_id=1, source_target_pairs={{0,8},{8,0},{16,24},{24,16},{1,9},{9,1},{17,25},{25,17},{2,10},{10... | collective-permute-start | bytes 786440 | tf_op jit(solution)/shard_map/ppermute | solution.py:728
  298.6 8.1 %collective-permute-start.46 = (f32[40,128]{1,0:T(8,128)S(1)}, f32[40,128]{1,0:T(8,128)S(1)}, u32[]{:S(2)}, u32[]{:S(2)}) collective-permute-start(f32[40,128]{1,0:T(8,128)S(1)} %add_blocks.3.refs_0_), channel_id=1, source_target_pairs={{0,4},{1,5},{2,6},{3,7},{4,0},{5,1},{6,2},{7,3},{8,12},{9,13},{10,... | collective-permute-start | bytes 61448 | tf_op jit(solution)/shard_map/ppermute | solution.py:728
  306.7 9.6 %collective-permute-start.45 = (f32[40,128]{1,0:T(8,128)S(1)}, f32[40,128]{1,0:T(8,128)S(1)}, u32[]{:S(2)}, u32[]{:S(2)}) collective-permute-start(f32[40,128]{1,0:T(8,128)S(1)} %add_blocks.3.refs_0_), channel_id=1, source_target_pairs={{0,2},{1,3},{2,0},{3,1},{4,6},{5,7},{6,4},{7,5},{8,10},{9,11},{10,... | collective-permute-start | bytes 61448 | tf_op jit(solution)/shard_map/ppermute | solution.py:728
  316.3 11.7 %collective-permute-start.65 = (bf16[64,2048]{1,0:T(8,128)(2,1)S(1)}, bf16[64,2048]{1,0:T(8,128)(2,1)S(1)}, u32[]{:S(2)}, u32[]{:S(2)}) collective-permute-start(bf16[64,2048]{1,0:T(8,128)(2,1)S(1)} %get-tuple-element.88), channel_id=1, source_target_pairs={{0,16},{8,24},{16,0},{24,8},{1,17},{9,25},{17,1},{25,9},{2,18},{10... | collective-permute-start | bytes 786440 | tf_op jit(solution)/shard_map/ppermute | solution.py:728
  316.8 11.2 %collective-permute-start.66 = (bf16[64,2048]{1,0:T(8,128)(2,1)S(1)}, bf16[64,2048]{1,0:T(8,128)(2,1)S(1)}, u32[]{:S(2)}, u32[]{:S(2)}) collective-permute-start(bf16[64,2048]{1,0:T(8,128)(2,1)S(1)} %get-tuple-element.89), channel_id=1, source_target_pairs={{0,24},{8,16},{16,8},{24,0},{1,25},{9,17},{17,9},{25,1},{2,26},{10... | collective-permute-start | bytes 786440 | tf_op jit(solution)/shard_map/ppermute | solution.py:728
  328.0 28.8 %collective-permute-start.59 = (bf16[128,2048]{1,0:T(8,128)(2,1)S(1)}, bf16[128,2048]{1,0:T(8,128)(2,1)S(1)}, u32[]{:S(2)}, u32[]{:S(2)}) collective-permute-start(bf16[128,2048]{1,0:T(8,128)(2,1)S(1)} %copy-done.105), channel_id=1, source_target_pairs={{0,1},{1,0},{2,3},{3,2},{4,5},{5,4},{6,7},{7,6},{8,9},{9,8},{10,11... | collective-permute-start | bytes 1572872 | tf_op jit(solution)/shard_map/ppermute | solution.py:728
  328.0 29.4 %collective-permute-start.61 = (bf16[528,768]{1,0:T(8,128)(2,1)S(1)}, bf16[528,768]{1,0:T(8,128)(2,1)S(1)}, u32[]{:S(2)}, u32[]{:S(2)}) collective-permute-start(bf16[528,768]{1,0:T(8,128)(2,1)S(1)} %finish.1.grad_ref.refs_13_.refs_0_), channel_id=1, source_target_pairs={{0,16},{8,24},{16,0},{24,8},{1,17},{9,25},{17,1},{25,9},{2,18},{10... | collective-permute-start | bytes 2433032 | tf_op jit(solution)/shard_map/ppermute | solution.py:728
  328.7 29.4 %collective-permute-start.60 = (bf16[528,768]{1,0:T(8,128)(2,1)S(1)}, bf16[528,768]{1,0:T(8,128)(2,1)S(1)}, u32[]{:S(2)}, u32[]{:S(2)}) collective-permute-start(bf16[528,768]{1,0:T(8,128)(2,1)S(1)} %finish.1.grad_ref.refs_13_.refs_0_), channel_id=1, source_target_pairs={{0,8},{8,0},{16,24},{24,16},{1,9},{9,1},{17,25},{25,17},{2,10},{10... | collective-permute-start | bytes 2433032 | tf_op jit(solution)/shard_map/ppermute | solution.py:728
  330.0 44.5 %collective-permute-start.48 = (bf16[256,2048]{1,0:T(8,128)(2,1)S(1)}, bf16[256,2048]{1,0:T(8,128)(2,1)S(1)}, u32[]{:S(2)}, u32[]{:S(2)}) collective-permute-start(bf16[256,2048]{1,0:T(8,128)(2,1)S(1)} %tokens_back.2), channel_id=1, source_target_pairs={{0,1},{1,0},{2,3},{3,2},{4,5},{5,4},{6,7},{7,6},{8,9},{9,8},{10,11... | collective-permute-start | bytes 3145736 | tf_op jit(solution)/shard_map/ppermute | solution.py:728
  330.1 26.9 %collective-permute-start.69 = (bf16[64,2048]{1,0:T(8,128)(2,1)S(1)}, bf16[64,2048]{1,0:T(8,128)(2,1)S(1)}, u32[]{:S(2)}, u32[]{:S(2)}) collective-permute-start(bf16[64,2048]{1,0:T(8,128)(2,1)S(1)} %add_pieces.1.refs_0_), channel_id=1, source_target_pairs={{0,24},{8,16},{16,8},{24,0},{1,25},{9,17},{17,9},{25,1},{2,26},{10... | collective-permute-start | bytes 786440 | tf_op jit(solution)/shard_map/ppermute | solution.py:728
  356.8 36.3 %collective-permute-start.55 = (bf16[256,2048]{1,0:T(8,128)(2,1)S(1)}, bf16[256,2048]{1,0:T(8,128)(2,1)S(1)}, u32[]{:S(2)}, u32[]{:S(2)}) collective-permute-start(bf16[256,2048]{1,0:T(8,128)(2,1)S(1)} %copy-done.90), channel_id=1, source_target_pairs={{0,1},{1,0},{2,3},{3,2},{4,5},{5,4},{6,7},{7,6},{8,9},{9,8},{10,11... | collective-permute-start | bytes 3145736 | tf_op jit(solution)/shard_map/ppermute | solution.py:728
  357.0 39.3 %collective-permute-start.53 = (bf16[256,2048]{1,0:T(8,128)(2,1)S(1)}, bf16[256,2048]{1,0:T(8,128)(2,1)S(1)}, u32[]{:S(2)}, u32[]{:S(2)}) collective-permute-start(bf16[256,2048]{1,0:T(8,128)(2,1)S(1)} %copy-done.92), channel_id=1, source_target_pairs={{0,1},{1,0},{2,3},{3,2},{4,5},{5,4},{6,7},{7,6},{8,9},{9,8},{10,11... | collective-permute-start | bytes 3145736 | tf_op jit(solution)/shard_map/ppermute | solution.py:728
  357.4 16.1 %collective-permute-start.68 = (bf16[64,2048]{1,0:T(8,128)(2,1)S(1)}, bf16[64,2048]{1,0:T(8,128)(2,1)S(1)}, u32[]{:S(2)}, u32[]{:S(2)}) collective-permute-start(bf16[64,2048]{1,0:T(8,128)(2,1)S(1)} %add_pieces.1.refs_0_), channel_id=1, source_target_pairs={{0,16},{8,24},{16,0},{24,8},{1,17},{9,25},{17,1},{25,9},{2,18},{10... | collective-permute-start | bytes 786440 | tf_op jit(solution)/shard_map/ppermute | solution.py:728
  358.1 15.5 %collective-permute-start.67 = (bf16[64,2048]{1,0:T(8,128)(2,1)S(1)}, bf16[64,2048]{1,0:T(8,128)(2,1)S(1)}, u32[]{:S(2)}, u32[]{:S(2)}) collective-permute-start(bf16[64,2048]{1,0:T(8,128)(2,1)S(1)} %add_pieces.1.refs_0_), channel_id=1, source_target_pairs={{0,8},{8,0},{16,24},{24,16},{1,9},{9,1},{17,25},{25,17},{2,10},{10... | collective-permute-start | bytes 786440 | tf_op jit(solution)/shard_map/ppermute | solution.py:728
  373.5 20.2 %collective-permute-start.58 = (bf16[128,2048]{1,0:T(8,128)(2,1)S(1)}, bf16[128,2048]{1,0:T(8,128)(2,1)S(1)}, u32[]{:S(2)}, u32[]{:S(2)}) collective-permute-start(bf16[128,2048]{1,0:T(8,128)(2,1)S(1)} %collective-permute-done.56.refs_9_), channel_id=1, source_target_pairs={{0,1},{1,0},{2,3},{3,2},{4,5},{5,4},{6,7},{7,6},{8,9},{9,8},{10,11... | collective-permute-start | bytes 1572872 | tf_op jit(solution)/shard_map/ppermute | solution.py:728
  373.6 24.1 %collective-permute-start.63 = (bf16[272,768]{1,0:T(8,128)(2,1)S(1)}, bf16[272,768]{1,0:T(8,128)(2,1)S(1)}, u32[]{:S(2)}, u32[]{:S(2)}) collective-permute-start(bf16[272,768]{1,0:T(8,128)(2,1)S(1)} %slice.133), channel_id=1, source_target_pairs={{0,8},{8,0},{16,24},{24,16},{1,9},{9,1},{17,25},{25,17},{2,10},{10... | collective-permute-start | bytes 1253384 | tf_op jit(solution)/shard_map/ppermute | solution.py:728
  374.6 23.2 %collective-permute-start.62 = (bf16[256,768]{1,0:T(8,128)(2,1)S(1)}, bf16[256,768]{1,0:T(8,128)(2,1)S(1)}, u32[]{:S(2)}, u32[]{:S(2)}) collective-permute-start(bf16[256,768]{1,0:T(8,128)(2,1)S(1)} %slice.132), channel_id=1, source_target_pairs={{0,16},{8,24},{16,0},{24,8},{1,17},{9,25},{17,1},{25,9},{2,18},{10... | collective-permute-start | bytes 1179656 | tf_op jit(solution)/shard_map/ppermute | solution.py:728
  393.2 18.8 %collective-permute-start.49 = (bf16[64,2048]{1,0:T(8,128)(2,1)S(1)}, bf16[64,2048]{1,0:T(8,128)(2,1)S(1)}, u32[]{:S(2)}, u32[]{:S(2)}) collective-permute-start(bf16[64,2048]{1,0:T(8,128)(2,1)S(1)} %get-tuple-element.80), channel_id=1, source_target_pairs={{0,2},{1,3},{2,0},{3,1},{4,6},{5,7},{6,4},{7,5},{8,10},{9,11},{10,... | collective-permute-start | bytes 786440 | tf_op jit(solution)/shard_map/ppermute | solution.py:728
  393.7 21.3 %collective-permute-start.50 = (bf16[64,2048]{1,0:T(8,128)(2,1)S(1)}, bf16[64,2048]{1,0:T(8,128)(2,1)S(1)}, u32[]{:S(2)}, u32[]{:S(2)}) collective-permute-start(bf16[64,2048]{1,0:T(8,128)(2,1)S(1)} %get-tuple-element.81), channel_id=1, source_target_pairs={{0,4},{1,5},{2,6},{3,7},{4,0},{5,1},{6,2},{7,3},{8,12},{9,13},{10,... | collective-permute-start | bytes 786440 | tf_op jit(solution)/shard_map/ppermute | solution.py:728
  396.4 18.7 %collective-permute-start.51 = (bf16[64,2048]{1,0:T(8,128)(2,1)S(1)}, bf16[64,2048]{1,0:T(8,128)(2,1)S(1)}, u32[]{:S(2)}, u32[]{:S(2)}) collective-permute-start(bf16[64,2048]{1,0:T(8,128)(2,1)S(1)} %get-tuple-element.82), channel_id=1, source_target_pairs={{0,6},{1,7},{2,4},{3,5},{4,2},{5,3},{6,0},{7,1},{8,14},{9,15},{10,... | collective-permute-start | bytes 786440 | tf_op jit(solution)/shard_map/ppermute | solution.py:728
  (136 other events, 1500.0 us)

commit v2 on v1

--- a/solution.py
+++ b/solution.py
@@ -125,10 +125,8 @@
         blocks = sequence_blocks(squares_ref, s, chunk, count)
         q_inv = inverse_column(squares_ref, 0, blocks, count, model_width)
         k_inv = inverse_column(squares_ref, 1, blocks, count, model_width)
-
-        @pl.loop(0, width // HD)
-        def _(h):
-            lanes = pl.ds(pl.multiple_of(h * HD, HD), HD)
+        for h in range(width // HD):
+            lanes = slice(h * HD, (h + 1) * HD)
             q = sequence_rows(query_ref, s, chunk, half, lanes) * q_inv * q_gain_ref[:, lanes]
             k = sequence_rows(keys_ref, s, chunk, half, lanes) * k_inv * k_gain_ref[:, lanes]
             q = (q * cos + pltpu.roll(q, HD // 2, 1) * sin).astype(jnp.bfloat16)
@@ -595,8 +593,8 @@
     w_gate_ref, w_up_ref, gate_ref, up_ref, swiglu_ref = refs[pieces:]
     gate = product(rows, w_gate_ref[...])
     up = product(rows, w_up_ref[...])
-    gate_ref[...] = gate
-    up_ref[...] = up
+    gate_ref[...] = gate.astype(jnp.bfloat16)
+    up_ref[...] = up.astype(jnp.bfloat16)
     swiglu_ref[...] = (gate * jax.nn.sigmoid(gate) * up).astype(jnp.bfloat16)
 
 
@@ -606,7 +604,7 @@
     tile = min(256, units)
     weight = pl.BlockSpec((depth, tile), lambda j: (0, j))
     out = pl.BlockSpec((count, tile), lambda j: (0, j))
-    wide = jax.ShapeDtypeStruct((count, units), jnp.float32)
+    wide = jax.ShapeDtypeStruct((count, units), jnp.bfloat16)
     return pl.pallas_call(
         functools.partial(ffn_kernel, len(rows)),
         grid=(units // tile,),
@@ -628,9 +626,9 @@
     grad = joined(refs[:pieces])
     w_down_ref, gate_ref, up_ref, grad_gate_ref, grad_up_ref = refs[pieces:]
     grad_swiglu = times_transposed(grad, w_down_ref[...])
-    gate = gate_ref[...]
+    gate = gate_ref[...].astype(jnp.float32)
     sig = jax.nn.sigmoid(gate)
-    grad_gate = grad_swiglu * up_ref[...] * sig * (1.0 + gate * (1.0 - sig))
+    grad_gate = grad_swiglu * up_ref[...].astype(jnp.float32) * sig * (1.0 + gate * (1.0 - sig))
     grad_gate_ref[...] = grad_gate.astype(jnp.bfloat16)
     grad_up_ref[...] = (grad_swiglu * (gate * sig)).astype(jnp.bfloat16)
 
@@ -717,7 +715,7 @@
             bytes_accessed=2 * rows * (depth + sum(widths)) + 4 * depth * sum(widths),
             transcendentals=0,
         ),
-    )(*[in_hbm(piece) for piece in left_pieces + right_pieces])
+    )(*[in_hbm(piece) for piece in left_pieces], *right_pieces)
 
 
 def build(dp_size, tensor_size):

time: 422 us -> 415 us (0.983)
  waiting for transfers between devices: 166 us -> 200 us
  starting transfers between devices: 83.8 us -> 56.3 us
  local copies, waits for them, and re-layouts: 26 us -> 16.9 us
  Pallas kernels: 124 us -> 118 us
    ppermute x86, waiting for transfers between devices: 166 us -> 200 us  [swap(): return lax.ppermute(value, axis, [(i, i ^ mask) for i in range(size)])]
    ppermute x86, starting transfers between devices: 83.8 us -> 56.3 us  [swap(): return lax.ppermute(value, axis, [(i, i ^ mask) for i in range(size)])]
    unnamed x231 -> x195, local copies, waits for them, and re-layouts: 22.3 us -> 13.2 us
    pallas_call x4, Pallas kernels: 54 us -> 48.7 us  [weight_grad(): pl.pallas_call(functools.partial(weight_grad_kernel, [len(group) for grou...]
  transfers between devices with their start and end apart: 86 -> 86, of which waited for: 34 -> 37; matrix products, arithmetic and copies ran while one was open for 2% -> 2% of each run, Pallas kernels for 25% -> 25%
where the time goes in v2:
time: 415 us; the launch traced here: 407 us
  waiting for transfers between devices  200 us (48%)
  Pallas kernels  118 us (28%)
  starting transfers between devices  56.3 us (14%)
  local copies, waits for them, and re-layouts  16.9 us (4%)
  matrix products  8.64 us (2%)
  other arithmetic  5.06 us (1%)
    ppermute x86, waiting for transfers between devices, swap(): return lax.ppermute(value, axis, [(i, i ^ mask) for i in range(size)])  200 us
    ppermute x86, starting transfers between devices, swap(): return lax.ppermute(value, axis, [(i, i ^ mask) for i in range(size)])  56.3 us
    pallas_call x4, Pallas kernels, weight_grad(): pl.pallas_call(functools.partial(weight_grad_kernel, [len(group) for grou...  48.7 us
    pallas_call x4, Pallas kernels, ffn(): pl.pallas_call(functools.partial(ffn_kernel, len(rows)), grid=(units // t...  29.9 us
    pallas_call x4, Pallas kernels, ffn_back(): pl.pallas_call(functools.partial(ffn_back_kernel, len(grad)), grid=(units...  19.8 us
    unnamed x195, local copies, waits for them, and re-layouts  13.2 us
  transfers between devices with their start and end apart: 86, of which 37 were waited for; matrix products, arithmetic and copies ran while one was open for 2% of the time, Pallas kernels for 25%

profile of v2, /device:TPU:0, one launch (start us, length us, event | category | flops | bytes accessed | tf_op | source)
XLA Modules:
  0.0 407.3 jit_solution(3367913025972302447)
XLA Ops:
  0.6 4.1 %collective-permute-start.1 = (bf16[64,2048]{1,0:T(8,128)(2,1)}, bf16[64,2048]{1,0:T(8,128)(2,1)S(1)}, u32[]{:S(2)}, u32[]{:S(2)}) collective-permute-start(bf16[64,2048]{1,0:T(8,128)(2,1)} %refs_0_.3), channel_id=1, source_target_pairs={{0,4},{1,5},{2,6},{3,7},{4,0},{5,1},{6,2},{7,3},{8,12},{9,13},{10,... | collective-permute-start | bytes 786440 | tf_op jit(solution)/shard_map/ppermute | solution.py:726
  4.8 1.6 collective-permute-start
  6.3 10.7 %collective-permute-done.1.refs_2_ = bf16[64,2048]{1,0:T(8,128)(2,1)S(1)} collective-permute-done((bf16[64,2048]{1,0:T(8,128)(2,1)}, bf16[64,2048]{1,0:T(8,128)(2,1)S(1)}, u32[]{:S(2)}, u32[]{:S(2)}) %collective-permute-start.1) | collective-permute-done | bytes 262176 | tf_op jit(solution)/shard_map/ppermute | solution.py:726
  18.4 6.0 %collective-permute-done.2.refs_3_ = bf16[64,2048]{1,0:T(8,128)(2,1)S(1)} collective-permute-done((bf16[64,2048]{1,0:T(8,128)(2,1)S(1)}, bf16[64,2048]{1,0:T(8,128)(2,1)S(1)}, u32[]{:S(2)}, u32[]{:S(2)}) %collective-permute-start.2) | collective-permute-done | bytes 262176 | tf_op jit(solution)/shard_map/ppermute | solution.py:726
  27.1 4.4 %project.1 = (f32[512,256]{1,0:T(8,128)S(1)}, f32[512,256]{1,0:T(8,128)S(1)}, bf16[512,256]{1,0:T(8,128)(2,1)S(1)}, f32[8,128]{1,0:T(8,128)S(1)}) custom-call(bf16[64,2048]{1,0:T(8,128)(2,1)} %refs_0_.3, bf16[64,2048]{1,0:T(8,128)(2,1)} %copy-done.80, bf16[64,2048]{1,0:T(8,128)(2,1)} %copy-done.76, bf16[64,2048]{1,0:T(8,128)(2,1)} %copy-done.78, ...), custom_call_target="tpu_custom_call" | custom-call | flops 1610612736 | bytes 6553600 | tf_op jit(solution)/shard_map/project/pallas_call | solution.py:573
  32.9 4.2 %collective-permute-start.10 = (f32[8,128]{1,0:T(8,128)S(1)}, f32[8,128]{1,0:T(8,128)S(1)}, u32[]{:S(2)}, u32[]{:S(2)}) collective-permute-start(f32[8,128]{1,0:T(8,128)S(1)} %add_blocks.2.refs_0_), channel_id=1, source_target_pairs={{0,6},{1,7},{2,4},{3,5},{4,2},{5,3},{6,0},{7,1},{8,14},{9,15},{10,... | collective-permute-start | bytes 12296 | tf_op jit(solution)/shard_map/ppermute | solution.py:726
  38.7 2.1 collective-permute-done.8.refs_1_
  41.6 1.9 attend.1
  44.1 2.6 collective-permute-done.11
  47.3 2.1 collective-permute-start.13
  49.5 7.1 %collective-permute-done.13 = bf16[64,2048]{1,0:T(8,128)(2,1)S(1)} collective-permute-done((bf16[64,2048]{1,0:T(8,128)(2,1)S(1)}, bf16[64,2048]{1,0:T(8,128)(2,1)S(1)}, u32[]{:S(2)}, u32[]{:S(2)}) %collective-permute-start.13) | collective-permute-done | bytes 262176 | tf_op jit(solution)/shard_map/ppermute | solution.py:726
  57.3 6.6 %collective-permute-done.12 = bf16[64,2048]{1,0:T(8,128)(2,1)S(1)} collective-permute-done((bf16[64,2048]{1,0:T(8,128)(2,1)S(1)}, bf16[64,2048]{1,0:T(8,128)(2,1)S(1)}, u32[]{:S(2)}, u32[]{:S(2)}) %collective-permute-start.12) | collective-permute-done | bytes 262176 | tf_op jit(solution)/shard_map/ppermute | solution.py:726
  63.9 9.8 %collective-permute-done.14 = bf16[64,2048]{1,0:T(8,128)(2,1)S(1)} collective-permute-done((bf16[64,2048]{1,0:T(8,128)(2,1)S(1)}, bf16[64,2048]{1,0:T(8,128)(2,1)S(1)}, u32[]{:S(2)}, u32[]{:S(2)}) %collective-permute-start.14) | collective-permute-done | bytes 262176 | tf_op jit(solution)/shard_map/ppermute | solution.py:726
  74.3 8.0 %collective-permute-done.16.refs_2_ = bf16[64,2048]{1,0:T(8,128)(2,1)S(1)} collective-permute-done((bf16[64,2048]{1,0:T(8,128)(2,1)S(1)}, bf16[64,2048]{1,0:T(8,128)(2,1)S(1)}, u32[]{:S(2)}, u32[]{:S(2)}) %collective-permute-start.16) | collective-permute-done | bytes 262176 | tf_op jit(solution)/shard_map/ppermute | solution.py:726
  82.8 2.5 collective-permute-done.15.refs_1_
  85.3 4.1 %collective-permute-done.17.refs_3_ = bf16[64,2048]{1,0:T(8,128)(2,1)S(1)} collective-permute-done((bf16[64,2048]{1,0:T(8,128)(2,1)S(1)}, bf16[64,2048]{1,0:T(8,128)(2,1)S(1)}, u32[]{:S(2)}, u32[]{:S(2)}) %collective-permute-start.17) | collective-permute-done | bytes 262176 | tf_op jit(solution)/shard_map/ppermute | solution.py:726
  90.9 7.1 %ffn.4 = (bf16[512,1024]{1,0:T(8,128)(2,1)S(1)}, bf16[512,1024]{1,0:T(8,128)(2,1)S(1)}, bf16[512,1024]{1,0:T(8,128)(2,1)S(1)}) custom-call(bf16[64,2048]{1,0:T(8,128)(2,1)S(1)} %fusion.22.refs_0_, bf16[64,2048]{1,0:T(8,128)(2,1)S(1)} %collective-permute-done.15.refs_1_, bf16[64,2048]{1,0:T(8,128)(2,1)S(1)} %collective-permute-done.16.refs_2_, ...), custom_call_target="tpu_custom_call" | custom-call | flops 4294967296 | bytes 15728640 | tf_op jit(solution)/shard_map/ffn/pallas_call | solution.py:608
  99.5 2.5 collective-permute-done.22
  103.5 2.0 collective-permute-start.23
  105.6 7.2 %collective-permute-done.24 = bf16[64,2048]{1,0:T(8,128)(2,1)S(1)} collective-permute-done((bf16[64,2048]{1,0:T(8,128)(2,1)S(1)}, bf16[64,2048]{1,0:T(8,128)(2,1)S(1)}, u32[]{:S(2)}, u32[]{:S(2)}) %collective-permute-start.24) | collective-permute-done | bytes 262176 | tf_op jit(solution)/shard_map/ppermute | solution.py:726
  112.9 6.2 %collective-permute-done.23 = bf16[64,2048]{1,0:T(8,128)(2,1)S(1)} collective-permute-done((bf16[64,2048]{1,0:T(8,128)(2,1)S(1)}, bf16[64,2048]{1,0:T(8,128)(2,1)S(1)}, u32[]{:S(2)}, u32[]{:S(2)}) %collective-permute-start.23) | collective-permute-done | bytes 262176 | tf_op jit(solution)/shard_map/ppermute | solution.py:726
  119.1 9.8 %collective-permute-done.25 = bf16[64,2048]{1,0:T(8,128)(2,1)S(1)} collective-permute-done((bf16[64,2048]{1,0:T(8,128)(2,1)S(1)}, bf16[64,2048]{1,0:T(8,128)(2,1)S(1)}, u32[]{:S(2)}, u32[]{:S(2)}) %collective-permute-start.25) | collective-permute-done | bytes 262176 | tf_op jit(solution)/shard_map/ppermute | solution.py:726
  129.8 7.5 %collective-permute-done.27.refs_2_ = bf16[64,2048]{1,0:T(8,128)(2,1)S(1)} collective-permute-done((bf16[64,2048]{1,0:T(8,128)(2,1)S(1)}, bf16[64,2048]{1,0:T(8,128)(2,1)S(1)}, u32[]{:S(2)}, u32[]{:S(2)}) %collective-permute-start.27) | collective-permute-done | bytes 262176 | tf_op jit(solution)/shard_map/ppermute | solution.py:726
  137.9 4.1 %collective-permute-done.26.refs_1_ = bf16[64,2048]{1,0:T(8,128)(2,1)S(1)} collective-permute-done((bf16[64,2048]{1,0:T(8,128)(2,1)S(1)}, bf16[64,2048]{1,0:T(8,128)(2,1)S(1)}, u32[]{:S(2)}, u32[]{:S(2)}) %collective-permute-start.26) | collective-permute-done | bytes 262176 | tf_op jit(solution)/shard_map/ppermute | solution.py:726
  142.0 3.3 collective-permute-done.28.refs_3_
  146.8 4.0 ffn_back.4
  153.8 1.5 collective-permute-start.52
  161.0 7.1 %collective-permute-done.35 = bf16[64,2048]{1,0:T(8,128)(2,1)S(1)} collective-permute-done((bf16[64,2048]{1,0:T(8,128)(2,1)S(1)}, bf16[64,2048]{1,0:T(8,128)(2,1)S(1)}, u32[]{:S(2)}, u32[]{:S(2)}) %collective-permute-start.35) | collective-permute-done | bytes 262176 | tf_op jit(solution)/shard_map/ppermute | solution.py:726
  168.4 11.5 %collective-permute-done.52.refs_5_ = bf16[256,2048]{1,0:T(8,128)(2,1)S(1)} collective-permute-done((bf16[256,2048]{1,0:T(8,128)(2,1)S(1)}, bf16[256,2048]{1,0:T(8,128)(2,1)S(1)}, u32[]{:S(2)}, u32[]{:S(2)}) %collective-permute-start.52) | collective-permute-done | bytes 1048608 | tf_op jit(solution)/shard_map/ppermute | solution.py:726
  179.9 21.9 %collective-permute-done.70.refs_0_.refs_5_ = bf16[256,2048]{1,0:T(8,128)(2,1)} collective-permute-done((bf16[256,2048]{1,0:T(8,128)(2,1)S(1)}, bf16[256,2048]{1,0:T(8,128)(2,1)}, u32[]{:S(2)}, u32[]{:S(2)}) %collective-permute-start.70) | collective-permute-done | bytes 1048608 | tf_op jit(solution)/shard_map/ppermute | solution.py:726
  206.3 1.5 collective-permute-start.75
  208.8 1.6 collective-permute-start.80
  210.3 6.3 %collective-permute-done.56.refs_9_ = bf16[128,2048]{1,0:T(8,128)(2,1)S(1)} collective-permute-done((bf16[128,2048]{1,0:T(8,128)(2,1)S(1)}, bf16[128,2048]{1,0:T(8,128)(2,1)S(1)}, u32[]{:S(2)}, u32[]{:S(2)}) %collective-permute-start.56) | collective-permute-done | bytes 524320 | tf_op jit(solution)/shard_map/ppermute | solution.py:726
  216.7 11.2 %collective-permute-done.74.refs_0_.refs_9_ = bf16[128,2048]{1,0:T(8,128)(2,1)S(1)} collective-permute-done((bf16[128,2048]{1,0:T(8,128)(2,1)S(1)}, bf16[128,2048]{1,0:T(8,128)(2,1)S(1)}, u32[]{:S(2)}, u32[]{:S(2)}) %collective-permute-start.74) | collective-permute-done | bytes 524320 | tf_op jit(solution)/shard_map/ppermute | solution.py:726
  229.8 11.8 %collective-permute-done.78.refs_0_.refs_9_ = bf16[256,2048]{1,0:T(8,128)(2,1)S(1)} collective-permute-done((bf16[256,2048]{1,0:T(8,128)(2,1)S(1)}, bf16[256,2048]{1,0:T(8,128)(2,1)S(1)}, u32[]{:S(2)}, u32[]{:S(2)}) %collective-permute-start.78) | collective-permute-done | bytes 1048608 | tf_op jit(solution)/shard_map/ppermute | solution.py:726
  241.6 2.0 collective-permute-done.38.refs_2_
  243.6 5.3 %collective-permute-done.80.refs_0_.refs_11_ = bf16[256,2048]{1,0:T(8,128)(2,1)S(1)} collective-permute-done((bf16[256,2048]{1,0:T(8,128)(2,1)S(1)}, bf16[256,2048]{1,0:T(8,128)(2,1)S(1)}, u32[]{:S(2)}, u32[]{:S(2)}) %collective-permute-start.80) | collective-permute-done | bytes 1048608 | tf_op jit(solution)/shard_map/ppermute | solution.py:726
  249.6 2.3 collective-permute-done.39.refs_3_
  253.5 5.8 %attend_back.1 = (bf16[512,256]{1,0:T(8,128)(2,1)S(1)}, f32[512,256]{1,0:T(8,128)S(1)}, f32[512,256]{1,0:T(8,128)S(1)}, f32[8,128]{1,0:T(8,128)S(1)}, f32[2,256]{1,0:T(2,128)S(1)}) custom-call(bf16[64,2048]{1,0:T(8,128)(2,1)S(1)} %get-tuple-element.124.refs_0_, bf16[64,2048]{1,0:T(8,128)(2,1)S(1)} %collective-permute-done.37.refs_1_, ...), custom_call_target="tpu_custom_call" | custom-call | flops 335544320 | bytes 3407872 | tf_op jit(solution)/shard_map/attend_back/pallas_call | solution.py:247
  264.3 1.6 collective-permute-start.82
  267.3 2.2 copy-done.7
  269.5 2.2 copy-done.49
  271.7 6.6 %ffn.7 = (bf16[512,1024]{1,0:T(8,128)(2,1)S(1)}, bf16[512,1024]{1,0:T(8,128)(2,1)S(1)}, bf16[512,1024]{1,0:T(8,128)(2,1)S(1)}) custom-call(bf16[128,2048]{1,0:T(8,128)(2,1)S(1)} %copy-done.53, bf16[128,2048]{1,0:T(8,128)(2,1)S(1)} %copy-done.55, bf16[128,2048]{1,0:T(8,128)(2,1)S(1)} %copy-done.57, bf16[128,2048]{1,0:T(8,128)(2,1)S(1)} %copy-done.59, ...), custom_call_target="tpu_custom_call" | custom-call | flops 4294967296 | bytes 15728640 | tf_op jit(solution)/shard_map/ffn/pallas_call | solution.py:608
  281.3 8.3 %ffn.6 = (bf16[512,1024]{1,0:T(8,128)(2,1)S(1)}, bf16[512,1024]{1,0:T(8,128)(2,1)S(1)}, bf16[512,1024]{1,0:T(8,128)(2,1)S(1)}) custom-call(bf16[256,2048]{1,0:T(8,128)(2,1)} %collective-permute-done.72.refs_0_.refs_7_, bf16[256,2048]{1,0:T(8,128)(2,1)} %collective-permute-done.73.refs_1_.refs_8_, bf16[2048,1024]{1,0:T(8,128)(2,1)S(1)} %copy-done.7, ...), custom_call_target="tpu_custom_call" | custom-call | flops 4294967296 | bytes 15728640 | tf_op jit(solution)/shard_map/ffn/pallas_call | solution.py:608
  294.0 7.8 %ffn.5 = (bf16[512,1024]{1,0:T(8,128)(2,1)S(1)}, bf16[512,1024]{1,0:T(8,128)(2,1)S(1)}, bf16[512,1024]{1,0:T(8,128)(2,1)S(1)}) custom-call(bf16[256,2048]{1,0:T(8,128)(2,1)} %collective-permute-done.70.refs_0_.refs_5_, bf16[256,2048]{1,0:T(8,128)(2,1)} %collective-permute-done.71.refs_1_.refs_6_, bf16[2048,1024]{1,0:T(8,128)(2,1)S(1)} %copy-done.8, ...), custom_call_target="tpu_custom_call" | custom-call | flops 4294967296 | bytes 15728640 | tf_op jit(solution)/shard_map/ffn/pallas_call | solution.py:608
  301.9 3.8 collective-permute-start.47
  305.6 5.0 %ffn_back.6 = (bf16[512,1024]{1,0:T(8,128)(2,1)S(1)}, bf16[512,1024]{1,0:T(8,128)(2,1)S(1)}) custom-call(bf16[256,2048]{1,0:T(8,128)(2,1)S(1)} %collective-permute-done.80.refs_0_.refs_11_, bf16[256,2048]{1,0:T(8,128)(2,1)} %collective-permute-done.81.refs_1_.refs_12_, bf16[1024,2048]{1,0:T(8,128)(2,1)S(1)} %copy-done.1, ...), custom_call_target="tpu_custom_call" | custom-call | flops 2147483648 | bytes 12582912 | tf_op jit(solution)/shard_map/ffn_back/pallas_call | solution.py:642
  311.2 1.5 collective-permute-start.66
  312.7 5.1 %ffn_back.5 = (bf16[512,1024]{1,0:T(8,128)(2,1)S(1)}, bf16[512,1024]{1,0:T(8,128)(2,1)S(1)}) custom-call(bf16[256,2048]{1,0:T(8,128)(2,1)S(1)} %collective-permute-done.78.refs_0_.refs_9_, bf16[256,2048]{1,0:T(8,128)(2,1)} %collective-permute-done.79.refs_1_.refs_10_, bf16[1024,2048]{1,0:T(8,128)(2,1)S(1)} %copy-done.1, ...), custom_call_target="tpu_custom_call" | custom-call | flops 2147483648 | bytes 12582912 | tf_op jit(solution)/shard_map/ffn_back/pallas_call | solution.py:642
  319.7 1.7 tokens_back.2
  321.4 2.4 collective-permute-done.65.refs_2_
  325.2 1.5 collective-permute-start.67
  326.7 13.1 %weight_grad.7 = f32[1024,2048]{1,0:T(8,128)} custom-call(bf16[512,1024]{1,0:T(8,128)(2,1)} %copy-done.33, bf16[512,1024]{1,0:T(8,128)(2,1)} %copy-done.66, bf16[512,1024]{1,0:T(8,128)(2,1)} %copy-done.65, bf16[512,1024]{1,0:T(8,128)(2,1)} %copy-done.64, bf16[256,2048]{1,0:T(8,128)(2,1)S(1)} %copy-done.10, bf16[64,2048]{1,0:T(8,128)(2,1)S(1)} %copy-done.35, ...), custom_call_target="tpu_custom_call" | custom-call | flops 8589934592 | bytes 20971520 | tf_op jit(solution)/shard_map/weight_grad/pallas_call | solution.py:696
  339.8 5.7 %ffn_back.7 = (bf16[512,1024]{1,0:T(8,128)(2,1)S(1)}, bf16[512,1024]{1,0:T(8,128)(2,1)S(1)}) custom-call(bf16[128,2048]{1,0:T(8,128)(2,1)S(1)} %collective-permute-done.82.refs_0_.refs_13_, bf16[128,2048]{1,0:T(8,128)(2,1)S(1)} %collective-permute-done.83.refs_1_.refs_14_, bf16[128,2048]{1,0:T(8,128)(2,1)S(1)} %collective-permute-done.84.refs_2_.refs_15_, ...), custom_call_target="tpu_custom_call" | custom-call | flops 2147483648 | bytes 12582912 | tf_op jit(solution)/shard_map/ffn_back/pallas_call | solution.py:642
  345.8 4.6 %collective-permute-done.67.refs_1_ = bf16[64,2048]{1,0:T(8,128)(2,1)S(1)} collective-permute-done((bf16[64,2048]{1,0:T(8,128)(2,1)S(1)}, bf16[64,2048]{1,0:T(8,128)(2,1)S(1)}, u32[]{:S(2)}, u32[]{:S(2)}) %collective-permute-start.67) | collective-permute-done | bytes 262176 | tf_op jit(solution)/shard_map/ppermute | solution.py:726
  350.4 1.6 collective-permute-start.68
  352.5 13.0 %weight_grad.6 = f32[2048,1024]{1,0:T(8,128)} custom-call(bf16[256,2048]{1,0:T(8,128)(2,1)} %copy-done.71, bf16[64,2048]{1,0:T(8,128)(2,1)} %copy-done.60, bf16[64,2048]{1,0:T(8,128)(2,1)} %copy-done.62, bf16[64,2048]{1,0:T(8,128)(2,1)} %copy-done.61, bf16[64,2048]{1,0:T(8,128)(2,1)} %copy-done.63, ...), custom_call_target="tpu_custom_call" | custom-call | flops 8589934592 | bytes 20971520 | tf_op jit(solution)/shard_map/weight_grad/pallas_call | solution.py:696
  365.6 1.5 collective-permute-start.63
  367.2 1.5 collective-permute-start.62
  368.7 12.6 %weight_grad.5 = f32[2048,1024]{1,0:T(8,128)} custom-call(bf16[256,2048]{1,0:T(8,128)(2,1)} %copy-done.71, bf16[64,2048]{1,0:T(8,128)(2,1)} %copy-done.60, bf16[64,2048]{1,0:T(8,128)(2,1)} %copy-done.62, bf16[64,2048]{1,0:T(8,128)(2,1)} %copy-done.61, bf16[64,2048]{1,0:T(8,128)(2,1)} %copy-done.63, ...), custom_call_target="tpu_custom_call" | custom-call | flops 8589934592 | bytes 20971520 | tf_op jit(solution)/shard_map/weight_grad/pallas_call | solution.py:696
  382.8 1.8 tokens_back.3
  385.8 3.3 collective-permute-start.51
  389.1 10.0 %weight_grad.4 = (f32[2048,256]{1,0:T(8,128)}, f32[2048,256]{1,0:T(8,128)}, f32[2048,256]{1,0:T(8,128)}) custom-call(bf16[256,2048]{1,0:T(8,128)(2,1)} %copy-done.84, bf16[64,2048]{1,0:T(8,128)(2,1)} %copy-done.92, bf16[64,2048]{1,0:T(8,128)(2,1)} %copy-done.94, bf16[64,2048]{1,0:T(8,128)(2,1)} %copy-done.93, bf16[64,2048]{1,0:T(8,128)(2,1)} %copy-done.95, ...), custom_call_target="tpu_custom_call" | custom-call | flops 6442450944 | bytes 17825792 | tf_op jit(solution)/shard_map/weight_grad/pallas_call | solution.py:696
  399.7 6.4 %collective-permute-done.50 = bf16[64,2048]{1,0:T(8,128)(2,1)S(1)} collective-permute-done((bf16[64,2048]{1,0:T(8,128)(2,1)S(1)}, bf16[64,2048]{1,0:T(8,128)(2,1)S(1)}, u32[]{:S(2)}, u32[]{:S(2)}) %collective-permute-start.50) | collective-permute-done | bytes 262176 | tf_op jit(solution)/shard_map/ppermute | solution.py:726
  (370 shorter events, 58.6 us)
Async XLA Ops:
  0.6 16.4 %collective-permute-start.1 = (bf16[64,2048]{1,0:T(8,128)(2,1)}, bf16[64,2048]{1,0:T(8,128)(2,1)S(1)}, u32[]{:S(2)}, u32[]{:S(2)}) collective-permute-start(bf16[64,2048]{1,0:T(8,128)(2,1)} %refs_0_.3), channel_id=1, source_target_pairs={{0,4},{1,5},{2,6},{3,7},{4,0},{5,1},{6,2},{7,3},{8,12},{9,13},{10,... | collective-permute-start | bytes 786440 | tf_op jit(solution)/shard_map/ppermute | solution.py:726
  4.8 13.6 %collective-permute-start = (bf16[64,2048]{1,0:T(8,128)(2,1)}, bf16[64,2048]{1,0:T(8,128)(2,1)S(1)}, u32[]{:S(2)}, u32[]{:S(2)}) collective-permute-start(bf16[64,2048]{1,0:T(8,128)(2,1)} %refs_0_.3), channel_id=1, source_target_pairs={{0,2},{1,3},{2,0},{3,1},{4,6},{5,7},{6,4},{7,5},{8,10},{9,11},{10,... | collective-permute-start | bytes 786440 | tf_op jit(solution)/shard_map/ppermute | solution.py:726
  17.0 7.4 %collective-permute-start.2 = (bf16[64,2048]{1,0:T(8,128)(2,1)S(1)}, bf16[64,2048]{1,0:T(8,128)(2,1)S(1)}, u32[]{:S(2)}, u32[]{:S(2)}) collective-permute-start(bf16[64,2048]{1,0:T(8,128)(2,1)S(1)} %collective-permute-done.1.refs_2_), channel_id=1, source_target_pairs={{0,2},{1,3},{2,0},{3,1},{4,6},{5,7},{6,4},{7,5},{8,10},{9,11},{10,... | collective-permute-start | bytes 786440 | tf_op jit(solution)/shard_map/ppermute | solution.py:726
  17.7 7.7 %collective-permute-start.3 = (bf16[64,2048]{1,0:T(8,128)(2,1)}, bf16[64,2048]{1,0:T(8,128)(2,1)S(1)}, u32[]{:S(2)}, u32[]{:S(2)}) collective-permute-start(bf16[64,2048]{1,0:T(8,128)(2,1)} %refs_0_.3), channel_id=1, source_target_pairs={{0,1},{1,0},{2,3},{3,2},{4,5},{5,4},{6,7},{7,6},{8,9},{9,8},{10,11... | collective-permute-start | bytes 786440 | tf_op jit(solution)/shard_map/ppermute | solution.py:726
  17.8 7.7 %collective-permute-start.5 = (bf16[64,2048]{1,0:T(8,128)(2,1)S(1)}, bf16[64,2048]{1,0:T(8,128)(2,1)S(1)}, u32[]{:S(2)}, u32[]{:S(2)}) collective-permute-start(bf16[64,2048]{1,0:T(8,128)(2,1)S(1)} %collective-permute-done.1.refs_2_), channel_id=1, source_target_pairs={{0,1},{1,0},{2,3},{3,2},{4,5},{5,4},{6,7},{7,6},{8,9},{9,8},{10,11... | collective-permute-start | bytes 786440 | tf_op jit(solution)/shard_map/ppermute | solution.py:726
  47.3 9.2 %collective-permute-start.13 = (bf16[64,2048]{1,0:T(8,128)(2,1)S(1)}, bf16[64,2048]{1,0:T(8,128)(2,1)S(1)}, u32[]{:S(2)}, u32[]{:S(2)}) collective-permute-start(bf16[64,2048]{1,0:T(8,128)(2,1)S(1)} %get-tuple-element.123), channel_id=1, source_target_pairs={{0,2},{1,3},{2,0},{3,1},{4,6},{5,7},{6,4},{7,5},{8,10},{9,11},{10,... | collective-permute-start | bytes 786440 | tf_op jit(solution)/shard_map/ppermute | solution.py:726
  49.4 14.5 %collective-permute-start.12 = (bf16[64,2048]{1,0:T(8,128)(2,1)S(1)}, bf16[64,2048]{1,0:T(8,128)(2,1)S(1)}, u32[]{:S(2)}, u32[]{:S(2)}) collective-permute-start(bf16[64,2048]{1,0:T(8,128)(2,1)S(1)} %get-tuple-element.122), channel_id=1, source_target_pairs={{0,2},{1,3},{2,0},{3,1},{4,6},{5,7},{6,4},{7,5},{8,10},{9,11},{10,... | collective-permute-start | bytes 786440 | tf_op jit(solution)/shard_map/ppermute | solution.py:726
  56.6 17.1 %collective-permute-start.14 = (bf16[64,2048]{1,0:T(8,128)(2,1)S(1)}, bf16[64,2048]{1,0:T(8,128)(2,1)S(1)}, u32[]{:S(2)}, u32[]{:S(2)}) collective-permute-start(bf16[64,2048]{1,0:T(8,128)(2,1)S(1)} %fusion.12), channel_id=1, source_target_pairs={{0,4},{1,5},{2,6},{3,7},{4,0},{5,1},{6,2},{7,3},{8,12},{9,13},{10,... | collective-permute-start | bytes 786440 | tf_op jit(solution)/shard_map/ppermute | solution.py:726
  74.2 8.1 %collective-permute-start.16 = (bf16[64,2048]{1,0:T(8,128)(2,1)S(1)}, bf16[64,2048]{1,0:T(8,128)(2,1)S(1)}, u32[]{:S(2)}, u32[]{:S(2)}) collective-permute-start(bf16[64,2048]{1,0:T(8,128)(2,1)S(1)} %fusion.22.refs_0_), channel_id=1, source_target_pairs={{0,4},{1,5},{2,6},{3,7},{4,0},{5,1},{6,2},{7,3},{8,12},{9,13},{10,... | collective-permute-start | bytes 786440 | tf_op jit(solution)/shard_map/ppermute | solution.py:726
  74.2 11.0 %collective-permute-start.15 = (bf16[64,2048]{1,0:T(8,128)(2,1)S(1)}, bf16[64,2048]{1,0:T(8,128)(2,1)S(1)}, u32[]{:S(2)}, u32[]{:S(2)}) collective-permute-start(bf16[64,2048]{1,0:T(8,128)(2,1)S(1)} %fusion.22.refs_0_), channel_id=1, source_target_pairs={{0,2},{1,3},{2,0},{3,1},{4,6},{5,7},{6,4},{7,5},{8,10},{9,11},{10,... | collective-permute-start | bytes 786440 | tf_op jit(solution)/shard_map/ppermute | solution.py:726
  103.5 9.2 %collective-permute-start.24 = (bf16[64,2048]{1,0:T(8,128)(2,1)S(1)}, bf16[64,2048]{1,0:T(8,128)(2,1)S(1)}, u32[]{:S(2)}, u32[]{:S(2)}) collective-permute-start(bf16[64,2048]{1,0:T(8,128)(2,1)S(1)} %get-tuple-element.121), channel_id=1, source_target_pairs={{0,2},{1,3},{2,0},{3,1},{4,6},{5,7},{6,4},{7,5},{8,10},{9,11},{10,... | collective-permute-start | bytes 786440 | tf_op jit(solution)/shard_map/ppermute | solution.py:726
  103.5 15.5 %collective-permute-start.23 = (bf16[64,2048]{1,0:T(8,128)(2,1)S(1)}, bf16[64,2048]{1,0:T(8,128)(2,1)S(1)}, u32[]{:S(2)}, u32[]{:S(2)}) collective-permute-start(bf16[64,2048]{1,0:T(8,128)(2,1)S(1)} %get-tuple-element.120), channel_id=1, source_target_pairs={{0,2},{1,3},{2,0},{3,1},{4,6},{5,7},{6,4},{7,5},{8,10},{9,11},{10,... | collective-permute-start | bytes 786440 | tf_op jit(solution)/shard_map/ppermute | solution.py:726
  112.8 16.2 %collective-permute-start.25 = (bf16[64,2048]{1,0:T(8,128)(2,1)S(1)}, bf16[64,2048]{1,0:T(8,128)(2,1)S(1)}, u32[]{:S(2)}, u32[]{:S(2)}) collective-permute-start(bf16[64,2048]{1,0:T(8,128)(2,1)S(1)} %fusion.10), channel_id=1, source_target_pairs={{0,4},{1,5},{2,6},{3,7},{4,0},{5,1},{6,2},{7,3},{8,12},{9,13},{10,... | collective-permute-start | bytes 786440 | tf_op jit(solution)/shard_map/ppermute | solution.py:726
  129.6 7.7 %collective-permute-start.27 = (bf16[64,2048]{1,0:T(8,128)(2,1)S(1)}, bf16[64,2048]{1,0:T(8,128)(2,1)S(1)}, u32[]{:S(2)}, u32[]{:S(2)}) collective-permute-start(bf16[64,2048]{1,0:T(8,128)(2,1)S(1)} %fusion.6.refs_0_), channel_id=1, source_target_pairs={{0,4},{1,5},{2,6},{3,7},{4,0},{5,1},{6,2},{7,3},{8,12},{9,13},{10,... | collective-permute-start | bytes 786440 | tf_op jit(solution)/shard_map/ppermute | solution.py:726
  129.7 12.2 %collective-permute-start.26 = (bf16[64,2048]{1,0:T(8,128)(2,1)S(1)}, bf16[64,2048]{1,0:T(8,128)(2,1)S(1)}, u32[]{:S(2)}, u32[]{:S(2)}) collective-permute-start(bf16[64,2048]{1,0:T(8,128)(2,1)S(1)} %fusion.6.refs_0_), channel_id=1, source_target_pairs={{0,2},{1,3},{2,0},{3,1},{4,6},{5,7},{6,4},{7,5},{8,10},{9,11},{10,... | collective-permute-start | bytes 786440 | tf_op jit(solution)/shard_map/ppermute | solution.py:726
  137.3 7.9 %collective-permute-start.28 = (bf16[64,2048]{1,0:T(8,128)(2,1)S(1)}, bf16[64,2048]{1,0:T(8,128)(2,1)S(1)}, u32[]{:S(2)}, u32[]{:S(2)}) collective-permute-start(bf16[64,2048]{1,0:T(8,128)(2,1)S(1)} %collective-permute-done.27.refs_2_), channel_id=1, source_target_pairs={{0,2},{1,3},{2,0},{3,1},{4,6},{5,7},{6,4},{7,5},{8,10},{9,11},{10,... | collective-permute-start | bytes 786440 | tf_op jit(solution)/shard_map/ppermute | solution.py:726
  137.3 8.0 %collective-permute-start.29 = (bf16[64,2048]{1,0:T(8,128)(2,1)S(1)}, bf16[64,2048]{1,0:T(8,128)(2,1)S(1)}, u32[]{:S(2)}, u32[]{:S(2)}) collective-permute-start(bf16[64,2048]{1,0:T(8,128)(2,1)S(1)} %fusion.6.refs_0_), channel_id=1, source_target_pairs={{0,1},{1,0},{2,3},{3,2},{4,5},{5,4},{6,7},{7,6},{8,9},{9,8},{10,11... | collective-permute-start | bytes 786440 | tf_op jit(solution)/shard_map/ppermute | solution.py:726
  137.4 8.0 %collective-permute-start.31 = (bf16[64,2048]{1,0:T(8,128)(2,1)S(1)}, bf16[64,2048]{1,0:T(8,128)(2,1)S(1)}, u32[]{:S(2)}, u32[]{:S(2)}) collective-permute-start(bf16[64,2048]{1,0:T(8,128)(2,1)S(1)} %collective-permute-done.27.refs_2_), channel_id=1, source_target_pairs={{0,1},{1,0},{2,3},{3,2},{4,5},{5,4},{6,7},{7,6},{8,9},{9,8},{10,11... | collective-permute-start | bytes 786440 | tf_op jit(solution)/shard_map/ppermute | solution.py:726
  153.8 26.1 %collective-permute-start.52 = (bf16[256,2048]{1,0:T(8,128)(2,1)S(1)}, bf16[256,2048]{1,0:T(8,128)(2,1)S(1)}, u32[]{:S(2)}, u32[]{:S(2)}) collective-permute-start(bf16[256,2048]{1,0:T(8,128)(2,1)S(1)} %constant_dynamic-update-slice_fusion.refs_0_), channel_id=1, source_target_pairs={{0,8},{8,0},{16,24},{24,16},{1,9},{9,1},{17,25},{25,17},{2,10},{10... | collective-permute-start | bytes 3145736 | tf_op jit(solution)/shard_map/ppermute | solution.py:726
  155.4 46.5 %collective-permute-start.70 = (bf16[256,2048]{1,0:T(8,128)(2,1)S(1)}, bf16[256,2048]{1,0:T(8,128)(2,1)}, u32[]{:S(2)}, u32[]{:S(2)}) collective-permute-start(bf16[256,2048]{1,0:T(8,128)(2,1)S(1)} %pad_maximum_fusion.refs_0_), channel_id=1, source_target_pairs={{0,8},{8,0},{16,24},{24,16},{1,9},{9,1},{17,25},{25,17},{2,10},{10... | collective-permute-start | bytes 3145736 | tf_op jit(solution)/shard_map/ppermute | solution.py:726
  156.1 48.4 %collective-permute-start.72 = (bf16[256,2048]{1,0:T(8,128)(2,1)S(1)}, bf16[256,2048]{1,0:T(8,128)(2,1)}, u32[]{:S(2)}, u32[]{:S(2)}) collective-permute-start(bf16[256,2048]{1,0:T(8,128)(2,1)S(1)} %pad_maximum_fusion.refs_0_), channel_id=1, source_target_pairs={{0,16},{8,24},{16,0},{24,8},{1,17},{9,25},{17,1},{25,9},{2,18},{10... | collective-permute-start | bytes 3145736 | tf_op jit(solution)/shard_map/ppermute | solution.py:726
  160.3 7.8 %collective-permute-start.35 = (bf16[64,2048]{1,0:T(8,128)(2,1)S(1)}, bf16[64,2048]{1,0:T(8,128)(2,1)S(1)}, u32[]{:S(2)}, u32[]{:S(2)}) collective-permute-start(bf16[64,2048]{1,0:T(8,128)(2,1)S(1)} %get-tuple-element.119), channel_id=1, source_target_pairs={{0,2},{1,3},{2,0},{3,1},{4,6},{5,7},{6,4},{7,5},{8,10},{9,11},{10,... | collective-permute-start | bytes 786440 | tf_op jit(solution)/shard_map/ppermute | solution.py:726
  160.4 48.4 %collective-permute-start.54 = (bf16[256,2048]{1,0:T(8,128)(2,1)S(1)}, bf16[256,2048]{1,0:T(8,128)(2,1)S(1)}, u32[]{:S(2)}, u32[]{:S(2)}) collective-permute-start(bf16[256,2048]{1,0:T(8,128)(2,1)S(1)} %constant_dynamic-update-slice_fusion.refs_0_), channel_id=1, source_target_pairs={{0,16},{8,24},{16,0},{24,8},{1,17},{9,25},{17,1},{25,9},{2,18},{10... | collective-permute-start | bytes 3145736 | tf_op jit(solution)/shard_map/ppermute | solution.py:726
  168.1 38.2 %collective-permute-start.34 = (bf16[64,2048]{1,0:T(8,128)(2,1)S(1)}, bf16[64,2048]{1,0:T(8,128)(2,1)S(1)}, u32[]{:S(2)}, u32[]{:S(2)}) collective-permute-start(bf16[64,2048]{1,0:T(8,128)(2,1)S(1)} %get-tuple-element.118), channel_id=1, source_target_pairs={{0,2},{1,3},{2,0},{3,1},{4,6},{5,7},{6,4},{7,5},{8,10},{9,11},{10,... | collective-permute-start | bytes 786440 | tf_op jit(solution)/shard_map/ppermute | solution.py:726
  179.9 27.9 %collective-permute-start.36 = (bf16[64,2048]{1,0:T(8,128)(2,1)S(1)}, bf16[64,2048]{1,0:T(8,128)(2,1)S(1)}, u32[]{:S(2)}, u32[]{:S(2)}) collective-permute-start(bf16[64,2048]{1,0:T(8,128)(2,1)S(1)} %fusion.8), channel_id=1, source_target_pairs={{0,4},{1,5},{2,6},{3,7},{4,0},{5,1},{6,2},{7,3},{8,12},{9,13},{10,... | collective-permute-start | bytes 786440 | tf_op jit(solution)/shard_map/ppermute | solution.py:726
  201.9 14.8 %collective-permute-start.56 = (bf16[128,2048]{1,0:T(8,128)(2,1)S(1)}, bf16[128,2048]{1,0:T(8,128)(2,1)S(1)}, u32[]{:S(2)}, u32[]{:S(2)}) collective-permute-start(bf16[128,2048]{1,0:T(8,128)(2,1)S(1)} %slice.130), channel_id=1, source_target_pairs={{0,16},{8,24},{16,0},{24,8},{1,17},{9,25},{17,1},{25,9},{2,18},{10... | collective-permute-start | bytes 1572872 | tf_op jit(solution)/shard_map/ppermute | solution.py:726
  204.5 23.4 %collective-permute-start.74 = (bf16[128,2048]{1,0:T(8,128)(2,1)S(1)}, bf16[128,2048]{1,0:T(8,128)(2,1)S(1)}, u32[]{:S(2)}, u32[]{:S(2)}) collective-permute-start(bf16[128,2048]{1,0:T(8,128)(2,1)S(1)} %slice.134), channel_id=1, source_target_pairs={{0,16},{8,24},{16,0},{24,8},{1,17},{9,25},{17,1},{25,9},{2,18},{10... | collective-permute-start | bytes 1572872 | tf_op jit(solution)/shard_map/ppermute | solution.py:726
  206.3 22.7 %collective-permute-start.75 = (bf16[128,2048]{1,0:T(8,128)(2,1)S(1)}, bf16[128,2048]{1,0:T(8,128)(2,1)S(1)}, u32[]{:S(2)}, u32[]{:S(2)}) collective-permute-start(bf16[128,2048]{1,0:T(8,128)(2,1)S(1)} %slice.135), channel_id=1, source_target_pairs={{0,8},{8,0},{16,24},{24,16},{1,9},{9,1},{17,25},{25,17},{2,10},{10... | collective-permute-start | bytes 1572872 | tf_op jit(solution)/shard_map/ppermute | solution.py:726
  207.8 33.8 %collective-permute-start.78 = (bf16[256,2048]{1,0:T(8,128)(2,1)S(1)}, bf16[256,2048]{1,0:T(8,128)(2,1)S(1)}, u32[]{:S(2)}, u32[]{:S(2)}) collective-permute-start(bf16[256,2048]{1,0:T(8,128)(2,1)S(1)} %pad_maximum_fusion.1.refs_4_), channel_id=1, source_target_pairs={{0,8},{8,0},{16,24},{24,16},{1,9},{9,1},{17,25},{25,17},{2,10},{10... | collective-permute-start | bytes 3145736 | tf_op jit(solution)/shard_map/ppermute | solution.py:726
  208.8 40.2 %collective-permute-start.80 = (bf16[256,2048]{1,0:T(8,128)(2,1)S(1)}, bf16[256,2048]{1,0:T(8,128)(2,1)S(1)}, u32[]{:S(2)}, u32[]{:S(2)}) collective-permute-start(bf16[256,2048]{1,0:T(8,128)(2,1)S(1)} %pad_maximum_fusion.1.refs_4_), channel_id=1, source_target_pairs={{0,16},{8,24},{16,0},{24,8},{1,17},{9,25},{17,1},{25,9},{2,18},{10... | collective-permute-start | bytes 3145736 | tf_op jit(solution)/shard_map/ppermute | solution.py:726
  216.7 47.6 %collective-permute-start.73 = (bf16[256,2048]{1,0:T(8,128)(2,1)}, bf16[256,2048]{1,0:T(8,128)(2,1)}, u32[]{:S(2)}, u32[]{:S(2)}) collective-permute-start(bf16[256,2048]{1,0:T(8,128)(2,1)} %collective-permute-done.72.refs_0_.refs_7_), channel_id=1, source_target_pairs={{0,1},{1,0},{2,3},{3,2},{4,5},{5,4},{6,7},{7,6},{8,9},{9,8},{10,11... | collective-permute-start | bytes 3145736 | tf_op jit(solution)/shard_map/ppermute | solution.py:726
  229.1 14.6 %collective-permute-start.38 = (bf16[64,2048]{1,0:T(8,128)(2,1)S(1)}, bf16[64,2048]{1,0:T(8,128)(2,1)S(1)}, u32[]{:S(2)}, u32[]{:S(2)}) collective-permute-start(bf16[64,2048]{1,0:T(8,128)(2,1)S(1)} %get-tuple-element.124.refs_0_), channel_id=1, source_target_pairs={{0,4},{1,5},{2,6},{3,7},{4,0},{5,1},{6,2},{7,3},{8,12},{9,13},{10,... | collective-permute-start | bytes 786440 | tf_op jit(solution)/shard_map/ppermute | solution.py:726
  229.8 19.1 %collective-permute-start.37 = (bf16[64,2048]{1,0:T(8,128)(2,1)S(1)}, bf16[64,2048]{1,0:T(8,128)(2,1)S(1)}, u32[]{:S(2)}, u32[]{:S(2)}) collective-permute-start(bf16[64,2048]{1,0:T(8,128)(2,1)S(1)} %get-tuple-element.124.refs_0_), channel_id=1, source_target_pairs={{0,2},{1,3},{2,0},{3,1},{4,6},{5,7},{6,4},{7,5},{8,10},{9,11},{10,... | collective-permute-start | bytes 786440 | tf_op jit(solution)/shard_map/ppermute | solution.py:726
  241.6 7.8 %collective-permute-start.40 = (bf16[64,2048]{1,0:T(8,128)(2,1)S(1)}, bf16[64,2048]{1,0:T(8,128)(2,1)S(1)}, u32[]{:S(2)}, u32[]{:S(2)}) collective-permute-start(bf16[64,2048]{1,0:T(8,128)(2,1)S(1)} %get-tuple-element.124.refs_0_), channel_id=1, source_target_pairs={{0,1},{1,0},{2,3},{3,2},{4,5},{5,4},{6,7},{7,6},{8,9},{9,8},{10,11... | collective-permute-start | bytes 786440 | tf_op jit(solution)/shard_map/ppermute | solution.py:726
  243.6 8.2 %collective-permute-start.39 = (bf16[64,2048]{1,0:T(8,128)(2,1)S(1)}, bf16[64,2048]{1,0:T(8,128)(2,1)S(1)}, u32[]{:S(2)}, u32[]{:S(2)}) collective-permute-start(bf16[64,2048]{1,0:T(8,128)(2,1)S(1)} %collective-permute-done.38.refs_2_), channel_id=1, source_target_pairs={{0,2},{1,3},{2,0},{3,1},{4,6},{5,7},{6,4},{7,5},{8,10},{9,11},{10,... | collective-permute-start | bytes 786440 | tf_op jit(solution)/shard_map/ppermute | solution.py:726
  249.0 12.8 %collective-permute-start.77 = (bf16[128,2048]{1,0:T(8,128)(2,1)S(1)}, bf16[128,2048]{1,0:T(8,128)(2,1)S(1)}, u32[]{:S(2)}, u32[]{:S(2)}) collective-permute-start(bf16[128,2048]{1,0:T(8,128)(2,1)S(1)} %collective-permute-done.75.refs_1_.refs_10_), channel_id=1, source_target_pairs={{0,1},{1,0},{2,3},{3,2},{4,5},{5,4},{6,7},{7,6},{8,9},{9,8},{10,11... | collective-permute-start | bytes 1572872 | tf_op jit(solution)/shard_map/ppermute | solution.py:726
  251.9 37.8 %collective-permute-start.71 = (bf16[256,2048]{1,0:T(8,128)(2,1)}, bf16[256,2048]{1,0:T(8,128)(2,1)}, u32[]{:S(2)}, u32[]{:S(2)}) collective-permute-start(bf16[256,2048]{1,0:T(8,128)(2,1)} %collective-permute-done.70.refs_0_.refs_5_), channel_id=1, source_target_pairs={{0,1},{1,0},{2,3},{3,2},{4,5},{5,4},{6,7},{7,6},{8,9},{9,8},{10,11... | collective-permute-start | bytes 3145736 | tf_op jit(solution)/shard_map/ppermute | solution.py:726
  252.4 39.2 %collective-permute-start.79 = (bf16[256,2048]{1,0:T(8,128)(2,1)S(1)}, bf16[256,2048]{1,0:T(8,128)(2,1)}, u32[]{:S(2)}, u32[]{:S(2)}) collective-permute-start(bf16[256,2048]{1,0:T(8,128)(2,1)S(1)} %collective-permute-done.78.refs_0_.refs_9_), channel_id=1, source_target_pairs={{0,1},{1,0},{2,3},{3,2},{4,5},{5,4},{6,7},{7,6},{8,9},{9,8},{10,11... | collective-permute-start | bytes 3145736 | tf_op jit(solution)/shard_map/ppermute | solution.py:726
  253.4 38.7 %collective-permute-start.81 = (bf16[256,2048]{1,0:T(8,128)(2,1)S(1)}, bf16[256,2048]{1,0:T(8,128)(2,1)}, u32[]{:S(2)}, u32[]{:S(2)}) collective-permute-start(bf16[256,2048]{1,0:T(8,128)(2,1)S(1)} %collective-permute-done.80.refs_0_.refs_11_), channel_id=1, source_target_pairs={{0,1},{1,0},{2,3},{3,2},{4,5},{5,4},{6,7},{7,6},{8,9},{9,8},{10,11... | collective-permute-start | bytes 3145736 | tf_op jit(solution)/shard_map/ppermute | solution.py:726
  264.3 26.7 %collective-permute-start.82 = (bf16[128,2048]{1,0:T(8,128)(2,1)S(1)}, bf16[128,2048]{1,0:T(8,128)(2,1)S(1)}, u32[]{:S(2)}, u32[]{:S(2)}) collective-permute-start(bf16[128,2048]{1,0:T(8,128)(2,1)S(1)} %slice.136), channel_id=1, source_target_pairs={{0,16},{8,24},{16,0},{24,8},{1,17},{9,25},{17,1},{25,9},{2,18},{10... | collective-permute-start | bytes 1572872 | tf_op jit(solution)/shard_map/ppermute | solution.py:726
  265.9 25.7 %collective-permute-start.83 = (bf16[128,2048]{1,0:T(8,128)(2,1)S(1)}, bf16[128,2048]{1,0:T(8,128)(2,1)S(1)}, u32[]{:S(2)}, u32[]{:S(2)}) collective-permute-start(bf16[128,2048]{1,0:T(8,128)(2,1)S(1)} %slice.137), channel_id=1, source_target_pairs={{0,8},{8,0},{16,24},{24,16},{1,9},{9,1},{17,25},{25,17},{2,10},{10... | collective-permute-start | bytes 1572872 | tf_op jit(solution)/shard_map/ppermute | solution.py:726
  291.0 33.5 %collective-permute-start.57 = (bf16[128,2048]{1,0:T(8,128)(2,1)S(1)}, bf16[128,2048]{1,0:T(8,128)(2,1)S(1)}, u32[]{:S(2)}, u32[]{:S(2)}) collective-permute-start(bf16[128,2048]{1,0:T(8,128)(2,1)S(1)} %slice.131), channel_id=1, source_target_pairs={{0,8},{8,0},{16,24},{24,16},{1,9},{9,1},{17,25},{25,17},{2,10},{10... | collective-permute-start | bytes 1572872 | tf_op jit(solution)/shard_map/ppermute | solution.py:726
  291.6 33.6 %collective-permute-start.84 = (bf16[128,2048]{1,0:T(8,128)(2,1)S(1)}, bf16[128,2048]{1,0:T(8,128)(2,1)S(1)}, u32[]{:S(2)}, u32[]{:S(2)}) collective-permute-start(bf16[128,2048]{1,0:T(8,128)(2,1)S(1)} %collective-permute-done.82.refs_0_.refs_13_), channel_id=1, source_target_pairs={{0,1},{1,0},{2,3},{3,2},{4,5},{5,4},{6,7},{7,6},{8,9},{9,8},{10,11... | collective-permute-start | bytes 1572872 | tf_op jit(solution)/shard_map/ppermute | solution.py:726
  291.6 33.6 %collective-permute-start.85 = (bf16[128,2048]{1,0:T(8,128)(2,1)S(1)}, bf16[128,2048]{1,0:T(8,128)(2,1)S(1)}, u32[]{:S(2)}, u32[]{:S(2)}) collective-permute-start(bf16[128,2048]{1,0:T(8,128)(2,1)S(1)} %collective-permute-done.83.refs_1_.refs_14_), channel_id=1, source_target_pairs={{0,1},{1,0},{2,3},{3,2},{4,5},{5,4},{6,7},{7,6},{8,9},{9,8},{10,11... | collective-permute-start | bytes 1572872 | tf_op jit(solution)/shard_map/ppermute | solution.py:726
  292.1 19.1 %collective-permute-start.64 = (bf16[64,2048]{1,0:T(8,128)(2,1)S(1)}, bf16[64,2048]{1,0:T(8,128)(2,1)S(1)}, u32[]{:S(2)}, u32[]{:S(2)}) collective-permute-start(bf16[64,2048]{1,0:T(8,128)(2,1)S(1)} %get-tuple-element.87), channel_id=1, source_target_pairs={{0,8},{8,0},{16,24},{24,16},{1,9},{9,1},{17,25},{25,17},{2,10},{10... | collective-permute-start | bytes 786440 | tf_op jit(solution)/shard_map/ppermute | solution.py:726
  293.6 8.3 %collective-permute-start.46 = (f32[40,128]{1,0:T(8,128)S(1)}, f32[40,128]{1,0:T(8,128)S(1)}, u32[]{:S(2)}, u32[]{:S(2)}) collective-permute-start(f32[40,128]{1,0:T(8,128)S(1)} %add_blocks.3.refs_0_), channel_id=1, source_target_pairs={{0,4},{1,5},{2,6},{3,7},{4,0},{5,1},{6,2},{7,3},{8,12},{9,13},{10,... | collective-permute-start | bytes 61448 | tf_op jit(solution)/shard_map/ppermute | solution.py:726
  301.9 8.8 %collective-permute-start.47 = (f32[40,128]{1,0:T(8,128)S(1)}, f32[40,128]{1,0:T(8,128)S(1)}, u32[]{:S(2)}, u32[]{:S(2)}) collective-permute-start(f32[40,128]{1,0:T(8,128)S(1)} %add_blocks.3.refs_0_), channel_id=1, source_target_pairs={{0,6},{1,7},{2,4},{3,5},{4,2},{5,3},{6,0},{7,1},{8,14},{9,15},{10,... | collective-permute-start | bytes 61448 | tf_op jit(solution)/shard_map/ppermute | solution.py:726
  310.7 13.1 %collective-permute-start.65 = (bf16[64,2048]{1,0:T(8,128)(2,1)S(1)}, bf16[64,2048]{1,0:T(8,128)(2,1)S(1)}, u32[]{:S(2)}, u32[]{:S(2)}) collective-permute-start(bf16[64,2048]{1,0:T(8,128)(2,1)S(1)} %get-tuple-element.88), channel_id=1, source_target_pairs={{0,16},{8,24},{16,0},{24,8},{1,17},{9,25},{17,1},{25,9},{2,18},{10... | collective-permute-start | bytes 786440 | tf_op jit(solution)/shard_map/ppermute | solution.py:726
  311.2 12.6 %collective-permute-start.66 = (bf16[64,2048]{1,0:T(8,128)(2,1)S(1)}, bf16[64,2048]{1,0:T(8,128)(2,1)S(1)}, u32[]{:S(2)}, u32[]{:S(2)}) collective-permute-start(bf16[64,2048]{1,0:T(8,128)(2,1)S(1)} %get-tuple-element.89), channel_id=1, source_target_pairs={{0,24},{8,16},{16,8},{24,0},{1,25},{9,17},{17,9},{25,1},{2,26},{10... | collective-permute-start | bytes 786440 | tf_op jit(solution)/shard_map/ppermute | solution.py:726
  323.8 21.7 %collective-permute-start.58 = (bf16[128,2048]{1,0:T(8,128)(2,1)S(1)}, bf16[128,2048]{1,0:T(8,128)(2,1)S(1)}, u32[]{:S(2)}, u32[]{:S(2)}) collective-permute-start(bf16[128,2048]{1,0:T(8,128)(2,1)S(1)} %copy-done.88), channel_id=1, source_target_pairs={{0,1},{1,0},{2,3},{3,2},{4,5},{5,4},{6,7},{7,6},{8,9},{9,8},{10,11... | collective-permute-start | bytes 1572872 | tf_op jit(solution)/shard_map/ppermute | solution.py:726
  323.8 26.6 %collective-permute-start.61 = (bf16[528,768]{1,0:T(8,128)(2,1)S(1)}, bf16[528,768]{1,0:T(8,128)(2,1)S(1)}, u32[]{:S(2)}, u32[]{:S(2)}) collective-permute-start(bf16[528,768]{1,0:T(8,128)(2,1)S(1)} %finish.1.grad_ref.refs_13_.refs_0_), channel_id=1, source_target_pairs={{0,16},{8,24},{16,0},{24,8},{1,17},{9,25},{17,1},{25,9},{2,18},{10... | collective-permute-start | bytes 2433032 | tf_op jit(solution)/shard_map/ppermute | solution.py:726
  324.5 27.4 %collective-permute-start.60 = (bf16[528,768]{1,0:T(8,128)(2,1)S(1)}, bf16[528,768]{1,0:T(8,128)(2,1)S(1)}, u32[]{:S(2)}, u32[]{:S(2)}) collective-permute-start(bf16[528,768]{1,0:T(8,128)(2,1)S(1)} %finish.1.grad_ref.refs_13_.refs_0_), channel_id=1, source_target_pairs={{0,8},{8,0},{16,24},{24,16},{1,9},{9,1},{17,25},{25,17},{2,10},{10... | collective-permute-start | bytes 2433032 | tf_op jit(solution)/shard_map/ppermute | solution.py:726
  325.2 42.0 %collective-permute-start.48 = (bf16[256,2048]{1,0:T(8,128)(2,1)S(1)}, bf16[256,2048]{1,0:T(8,128)(2,1)S(1)}, u32[]{:S(2)}, u32[]{:S(2)}) collective-permute-start(bf16[256,2048]{1,0:T(8,128)(2,1)S(1)} %tokens_back.2), channel_id=1, source_target_pairs={{0,1},{1,0},{2,3},{3,2},{4,5},{5,4},{6,7},{7,6},{8,9},{9,8},{10,11... | collective-permute-start | bytes 3145736 | tf_op jit(solution)/shard_map/ppermute | solution.py:726
  325.2 25.2 %collective-permute-start.67 = (bf16[64,2048]{1,0:T(8,128)(2,1)S(1)}, bf16[64,2048]{1,0:T(8,128)(2,1)S(1)}, u32[]{:S(2)}, u32[]{:S(2)}) collective-permute-start(bf16[64,2048]{1,0:T(8,128)(2,1)S(1)} %add_pieces.1.refs_0_), channel_id=1, source_target_pairs={{0,8},{8,0},{16,24},{24,16},{1,9},{9,1},{17,25},{25,17},{2,10},{10... | collective-permute-start | bytes 786440 | tf_op jit(solution)/shard_map/ppermute | solution.py:726
  345.5 39.2 %collective-permute-start.53 = (bf16[256,2048]{1,0:T(8,128)(2,1)S(1)}, bf16[256,2048]{1,0:T(8,128)(2,1)S(1)}, u32[]{:S(2)}, u32[]{:S(2)}) collective-permute-start(bf16[256,2048]{1,0:T(8,128)(2,1)S(1)} %copy-done.73), channel_id=1, source_target_pairs={{0,1},{1,0},{2,3},{3,2},{4,5},{5,4},{6,7},{7,6},{8,9},{9,8},{10,11... | collective-permute-start | bytes 3145736 | tf_op jit(solution)/shard_map/ppermute | solution.py:726
  350.3 35.4 %collective-permute-start.55 = (bf16[256,2048]{1,0:T(8,128)(2,1)S(1)}, bf16[256,2048]{1,0:T(8,128)(2,1)S(1)}, u32[]{:S(2)}, u32[]{:S(2)}) collective-permute-start(bf16[256,2048]{1,0:T(8,128)(2,1)S(1)} %copy-done.75), channel_id=1, source_target_pairs={{0,1},{1,0},{2,3},{3,2},{4,5},{5,4},{6,7},{7,6},{8,9},{9,8},{10,11... | collective-permute-start | bytes 3145736 | tf_op jit(solution)/shard_map/ppermute | solution.py:726
  350.4 15.2 %collective-permute-start.68 = (bf16[64,2048]{1,0:T(8,128)(2,1)S(1)}, bf16[64,2048]{1,0:T(8,128)(2,1)S(1)}, u32[]{:S(2)}, u32[]{:S(2)}) collective-permute-start(bf16[64,2048]{1,0:T(8,128)(2,1)S(1)} %add_pieces.1.refs_0_), channel_id=1, source_target_pairs={{0,16},{8,24},{16,0},{24,8},{1,17},{9,25},{17,1},{25,9},{2,18},{10... | collective-permute-start | bytes 786440 | tf_op jit(solution)/shard_map/ppermute | solution.py:726
  351.9 13.7 %collective-permute-start.69 = (bf16[64,2048]{1,0:T(8,128)(2,1)S(1)}, bf16[64,2048]{1,0:T(8,128)(2,1)S(1)}, u32[]{:S(2)}, u32[]{:S(2)}) collective-permute-start(bf16[64,2048]{1,0:T(8,128)(2,1)S(1)} %add_pieces.1.refs_0_), channel_id=1, source_target_pairs={{0,24},{8,16},{16,8},{24,0},{1,25},{9,17},{17,9},{25,1},{2,26},{10... | collective-permute-start | bytes 786440 | tf_op jit(solution)/shard_map/ppermute | solution.py:726
  365.5 19.1 %collective-permute-start.59 = (bf16[128,2048]{1,0:T(8,128)(2,1)S(1)}, bf16[128,2048]{1,0:T(8,128)(2,1)S(1)}, u32[]{:S(2)}, u32[]{:S(2)}) collective-permute-start(bf16[128,2048]{1,0:T(8,128)(2,1)S(1)} %collective-permute-done.57.refs_10_), channel_id=1, source_target_pairs={{0,1},{1,0},{2,3},{3,2},{4,5},{5,4},{6,7},{7,6},{8,9},{9,8},{10,11... | collective-permute-start | bytes 1572872 | tf_op jit(solution)/shard_map/ppermute | solution.py:726
  365.6 23.5 %collective-permute-start.63 = (bf16[272,768]{1,0:T(8,128)(2,1)S(1)}, bf16[272,768]{1,0:T(8,128)(2,1)S(1)}, u32[]{:S(2)}, u32[]{:S(2)}) collective-permute-start(bf16[272,768]{1,0:T(8,128)(2,1)S(1)} %slice.133), channel_id=1, source_target_pairs={{0,8},{8,0},{16,24},{24,16},{1,9},{9,1},{17,25},{25,17},{2,10},{10... | collective-permute-start | bytes 1253384 | tf_op jit(solution)/shard_map/ppermute | solution.py:726
  367.2 21.9 %collective-permute-start.62 = (bf16[256,768]{1,0:T(8,128)(2,1)S(1)}, bf16[256,768]{1,0:T(8,128)(2,1)S(1)}, u32[]{:S(2)}, u32[]{:S(2)}) collective-permute-start(bf16[256,768]{1,0:T(8,128)(2,1)S(1)} %slice.132), channel_id=1, source_target_pairs={{0,16},{8,24},{16,0},{24,8},{1,17},{9,25},{17,1},{25,9},{2,18},{10... | collective-permute-start | bytes 1179656 | tf_op jit(solution)/shard_map/ppermute | solution.py:726
  384.6 15.1 %collective-permute-start.49 = (bf16[64,2048]{1,0:T(8,128)(2,1)S(1)}, bf16[64,2048]{1,0:T(8,128)(2,1)S(1)}, u32[]{:S(2)}, u32[]{:S(2)}) collective-permute-start(bf16[64,2048]{1,0:T(8,128)(2,1)S(1)} %get-tuple-element.80), channel_id=1, source_target_pairs={{0,2},{1,3},{2,0},{3,1},{4,6},{5,7},{6,4},{7,5},{8,10},{9,11},{10,... | collective-permute-start | bytes 786440 | tf_op jit(solution)/shard_map/ppermute | solution.py:726
  384.7 21.4 %collective-permute-start.50 = (bf16[64,2048]{1,0:T(8,128)(2,1)S(1)}, bf16[64,2048]{1,0:T(8,128)(2,1)S(1)}, u32[]{:S(2)}, u32[]{:S(2)}) collective-permute-start(bf16[64,2048]{1,0:T(8,128)(2,1)S(1)} %get-tuple-element.81), channel_id=1, source_target_pairs={{0,4},{1,5},{2,6},{3,7},{4,0},{5,1},{6,2},{7,3},{8,12},{9,13},{10,... | collective-permute-start | bytes 786440 | tf_op jit(solution)/shard_map/ppermute | solution.py:726
  385.8 20.3 %collective-permute-start.51 = (bf16[64,2048]{1,0:T(8,128)(2,1)S(1)}, bf16[64,2048]{1,0:T(8,128)(2,1)S(1)}, u32[]{:S(2)}, u32[]{:S(2)}) collective-permute-start(bf16[64,2048]{1,0:T(8,128)(2,1)S(1)} %get-tuple-element.82), channel_id=1, source_target_pairs={{0,6},{1,7},{2,4},{3,5},{4,2},{5,3},{6,0},{7,1},{8,14},{9,15},{10,... | collective-permute-start | bytes 786440 | tf_op jit(solution)/shard_map/ppermute | solution.py:726
  (118 other events, 1143.3 us)

commit v3 on v2

--- a/solution.py
+++ b/solution.py
@@ -431,6 +431,55 @@
     )(*arrays, *weights)
 
 
+def partial_kernel(terms, multiply, count, *refs):
+    total = multiply(refs[0][...], refs[terms][...])
+    for i in range(1, terms):
+        total = total + multiply(refs[i][...], refs[terms + i][...])
+    outs = refs[2 * terms :]
+    if count is None:
+        outs[0][...] = total.astype(jnp.bfloat16)
+        return
+    total = total + outs[0][...].astype(jnp.float32)
+    for k, ref in enumerate(outs[1:]):
+        ref[...] = total[k * count : (k + 1) * count].astype(ref.dtype)
+
+
+def partial_rows(lefts, rights, multiply, part, far=None, kinds=(jnp.bfloat16,)):
+    half = lefts[0].shape[0] // 2
+    transposed = multiply is times_transposed
+    depth = rights[0].shape[0 if transposed else 1]
+    tile = min(512, depth)
+    if transposed:
+        right_specs = [pl.BlockSpec((tile, r.shape[1]), lambda j: (j, 0)) for r in rights]
+    else:
+        right_specs = [pl.BlockSpec((r.shape[0], tile), lambda j: (0, j)) for r in rights]
+    count = None if far is None else half // len(kinds)
+    size = count or half
+    specs = [
+        pl.BlockSpec((half, left.shape[1]), lambda j: (part, 0), pipeline_mode=pl.Buffered(1))
+        for left in lefts
+    ] + right_specs
+    arrays = [*lefts, *rights]
+    if far is not None:
+        specs.append(pl.BlockSpec((half, tile), lambda j: (0, j)))
+        arrays.append(far)
+    terms = sum(left.shape[1] for left in lefts)
+    return pl.pallas_call(
+        functools.partial(partial_kernel, len(lefts), multiply, count),
+        grid=(depth // tile,),
+        in_specs=specs,
+        out_specs=[pl.BlockSpec((size, tile), lambda j: (0, j)) for _ in kinds],
+        out_shape=[jax.ShapeDtypeStruct((size, depth), kind) for kind in kinds],
+        name="partial_rows",
+        compiler_params=pltpu.CompilerParams(vmem_limit_bytes=14 * MIB),
+        cost_estimate=pl.CostEstimate(
+            flops=2 * half * depth * terms,
+            bytes_accessed=2 * terms * (half + depth) + 6 * half * depth,
+            transcendentals=0,
+        ),
+    )(*arrays)
+
+
 def out_grad_kernel(pieces, *refs):
     attended_ref, me_ref = refs[pieces : pieces + 2]
     own_ref, others, grad_ref = refs[pieces + 2], refs[pieces + 3 : -1], refs[-1]
@@ -460,7 +509,7 @@
             bytes_accessed=2 * attended.shape[0] * (width + depth) + 3 * width * depth,
             transcendentals=0,
         ),
-    )(*grad_attn, attended, me)
+    )(*[in_hbm(piece) for piece in grad_attn], attended, me)
 
 
 def assemble_kernel(*refs):
@@ -690,7 +739,7 @@
             counts += [piece.shape[0] for piece in group[:-1]] + [group[-1].shape[0] - extra]
     rows = sum(piece.shape[0] for piece in left_pieces)
     widths = [right[0][0].shape[1] // outs for right in rights for _ in range(outs)]
-    tile = min(512 if max(widths) <= 1024 else 256, depth)
+    tile = min(256, depth)
     blocks = 4 * rows * tile + (2 * len(rights)) * rows * rights[0][0][0].shape[1]
     needed = blocks + 4 * tile * sum(widths) * (2 + len(left)) + 4 * MIB
     return pl.pallas_call(
@@ -751,6 +800,23 @@
         for k in range(1, pairs):
             block = near[k * count : (k + 1) * count].astype(jnp.bfloat16)
             total = total + swap(block, "tensor", 2 * k).astype(jnp.float32)
+        return total
+
+    def product_scatter(lefts, rights, multiply):
+        (far,) = partial_rows(lefts, rights, multiply, 1)
+        far = swap(far, "tensor", 1)
+        relay = pairs == 4
+        kinds = [jnp.float32] + [jnp.bfloat16] * (pairs - 1)
+        if relay:
+            kinds[2] = jnp.float32
+        total, *blocks = partial_rows(lefts, rights, multiply, 0, far, tuple(kinds))
+        if relay:
+            three = swap(blocks[2], "tensor", 2).astype(jnp.float32)
+            one = swap(blocks[0], "tensor", 2).astype(jnp.float32)
+            two = swap((blocks[1] + three).astype(jnp.bfloat16), "tensor", 4)
+            return total + one + two.astype(jnp.float32)
+        for k, block in enumerate(blocks):
+            total = total + swap(block, "tensor", 2 * k + 2).astype(jnp.float32)
         return total
 
     def row_sum(value):
@@ -853,11 +919,8 @@
             norm_back(grad_out * ffn_gain, m_normed, m_inverse).astype(jnp.bfloat16), relay=True
         )
         grad_gate, grad_up = ffn_back(grad_ffn, w_down, gate, up_proj)
-        grad_mixed = grad_out + tensor_scatter(
-            lambda a, b: times_transposed(grad_gate[a:b], w_gate)
-            + times_transposed(grad_up[a:b], w_up),
-            rows,
-            relay=True,
+        grad_mixed = grad_out + product_scatter(
+            [grad_gate, grad_up], [w_gate, w_up], times_transposed
         )
         attn_gain_part = jnp.sum(grad_mixed * a_normed, axis=0)
         grad_attn = tensor_gather(

time: 415 us -> 416 us (level); the launches traced: 407 us -> 413 us
  Pallas kernels: 118 us -> 130 us
  matrix products: 8.64 us -> 3.4 us
    pallas_call x0 -> x2, Pallas kernels: none -> 6.25 us  [partial_rows(): pl.pallas_call(functools.partial(partial_kernel, len(lefts), multiply, co...]
    dot_general x4 -> x0, matrix products: 5.21 us -> none  [times_transposed(): lax.dot_general(left, right, (((1,), (1,)), ((), ())), preferred_element_...]
    pallas_call x4, Pallas kernels: 48.7 us -> 52.9 us  [weight_grad(): pl.pallas_call(functools.partial(weight_grad_kernel, [len(group) for grou...]
    unnamed x195 -> x175, local copies, waits for them, and re-layouts: 13.2 us -> 13.9 us
  transfers between devices with their start and end apart: 86 -> 86, of which waited for: 37 -> 37; matrix products, arithmetic and copies ran while one was open for 2% -> 2% of each run, Pallas kernels for 25% -> 27%
where the time goes in v3:
time: 416 us; the launch traced here: 413 us
  waiting for transfers between devices  197 us (47%)
  Pallas kernels  130 us (31%)
  starting transfers between devices  56.3 us (14%)
  local copies, waits for them, and re-layouts  19.6 us (5%)
  other arithmetic  5.02 us (1%)
    ppermute x86, waiting for transfers between devices, swap(): return lax.ppermute(value, axis, [(i, i ^ mask) for i in range(size)])  197 us
    ppermute x86, starting transfers between devices, swap(): return lax.ppermute(value, axis, [(i, i ^ mask) for i in range(size)])  56.3 us
    pallas_call x4, Pallas kernels, weight_grad(): pl.pallas_call(functools.partial(weight_grad_kernel, [len(group) for grou...  52.9 us
    pallas_call x4, Pallas kernels, ffn(): pl.pallas_call(functools.partial(ffn_kernel, len(rows)), grid=(units // t...  29.2 us
    pallas_call x4, Pallas kernels, ffn_back(): pl.pallas_call(functools.partial(ffn_back_kernel, len(grad)), grid=(units...  20.5 us
    unnamed x175, local copies, waits for them, and re-layouts  13.9 us
  transfers between devices with their start and end apart: 86, of which 37 were waited for; matrix products, arithmetic and copies ran while one was open for 2% of the time, Pallas kernels for 27%

profile of v3, /device:TPU:0, one launch (start us, length us, event | category | flops | bytes accessed | tf_op | source)
XLA Modules:
  0.0 412.6 jit_solution(3586331214285226346)
XLA Ops:
  0.6 4.1 %collective-permute-start.1 = (bf16[64,2048]{1,0:T(8,128)(2,1)}, bf16[64,2048]{1,0:T(8,128)(2,1)S(1)}, u32[]{:S(2)}, u32[]{:S(2)}) collective-permute-start(bf16[64,2048]{1,0:T(8,128)(2,1)} %refs_0_.3), channel_id=1, source_target_pairs={{0,4},{1,5},{2,6},{3,7},{4,0},{5,1},{6,2},{7,3},{8,12},{9,13},{10,... | collective-permute-start | bytes 786440 | tf_op jit(solution)/shard_map/ppermute | solution.py:775
  4.8 1.6 collective-permute-start
  6.4 10.7 %collective-permute-done.1.refs_2_ = bf16[64,2048]{1,0:T(8,128)(2,1)S(1)} collective-permute-done((bf16[64,2048]{1,0:T(8,128)(2,1)}, bf16[64,2048]{1,0:T(8,128)(2,1)S(1)}, u32[]{:S(2)}, u32[]{:S(2)}) %collective-permute-start.1) | collective-permute-done | bytes 262176 | tf_op jit(solution)/shard_map/ppermute | solution.py:775
  18.4 6.0 %collective-permute-done.2.refs_3_ = bf16[64,2048]{1,0:T(8,128)(2,1)S(1)} collective-permute-done((bf16[64,2048]{1,0:T(8,128)(2,1)S(1)}, bf16[64,2048]{1,0:T(8,128)(2,1)S(1)}, u32[]{:S(2)}, u32[]{:S(2)}) %collective-permute-start.2) | collective-permute-done | bytes 262176 | tf_op jit(solution)/shard_map/ppermute | solution.py:775
  27.1 4.4 %project.1 = (f32[512,256]{1,0:T(8,128)S(1)}, f32[512,256]{1,0:T(8,128)S(1)}, bf16[512,256]{1,0:T(8,128)(2,1)S(1)}, f32[8,128]{1,0:T(8,128)S(1)}) custom-call(bf16[64,2048]{1,0:T(8,128)(2,1)} %refs_0_.3, bf16[64,2048]{1,0:T(8,128)(2,1)} %copy-done.68, bf16[64,2048]{1,0:T(8,128)(2,1)} %copy-done.66, bf16[64,2048]{1,0:T(8,128)(2,1)} %copy-done.70, ...), custom_call_target="tpu_custom_call" | custom-call | flops 1610612736 | bytes 6553600 | tf_op jit(solution)/shard_map/project/pallas_call | solution.py:622
  32.9 4.2 %collective-permute-start.10 = (f32[8,128]{1,0:T(8,128)S(1)}, f32[8,128]{1,0:T(8,128)S(1)}, u32[]{:S(2)}, u32[]{:S(2)}) collective-permute-start(f32[8,128]{1,0:T(8,128)S(1)} %add_blocks.2.refs_0_), channel_id=1, source_target_pairs={{0,6},{1,7},{2,4},{3,5},{4,2},{5,3},{6,0},{7,1},{8,14},{9,15},{10,... | collective-permute-start | bytes 12296 | tf_op jit(solution)/shard_map/ppermute | solution.py:775
  38.7 2.1 collective-permute-done.8.refs_1_
  41.6 1.9 attend.1
  44.1 2.6 collective-permute-done.11
  47.3 2.1 collective-permute-start.13
  49.5 7.1 %collective-permute-done.13 = bf16[64,2048]{1,0:T(8,128)(2,1)S(1)} collective-permute-done((bf16[64,2048]{1,0:T(8,128)(2,1)S(1)}, bf16[64,2048]{1,0:T(8,128)(2,1)S(1)}, u32[]{:S(2)}, u32[]{:S(2)}) %collective-permute-start.13) | collective-permute-done | bytes 262176 | tf_op jit(solution)/shard_map/ppermute | solution.py:775
  57.3 6.6 %collective-permute-done.12 = bf16[64,2048]{1,0:T(8,128)(2,1)S(1)} collective-permute-done((bf16[64,2048]{1,0:T(8,128)(2,1)S(1)}, bf16[64,2048]{1,0:T(8,128)(2,1)S(1)}, u32[]{:S(2)}, u32[]{:S(2)}) %collective-permute-start.12) | collective-permute-done | bytes 262176 | tf_op jit(solution)/shard_map/ppermute | solution.py:775
  63.9 9.8 %collective-permute-done.14 = bf16[64,2048]{1,0:T(8,128)(2,1)S(1)} collective-permute-done((bf16[64,2048]{1,0:T(8,128)(2,1)S(1)}, bf16[64,2048]{1,0:T(8,128)(2,1)S(1)}, u32[]{:S(2)}, u32[]{:S(2)}) %collective-permute-start.14) | collective-permute-done | bytes 262176 | tf_op jit(solution)/shard_map/ppermute | solution.py:775
  74.3 8.0 %collective-permute-done.16.refs_2_ = bf16[64,2048]{1,0:T(8,128)(2,1)S(1)} collective-permute-done((bf16[64,2048]{1,0:T(8,128)(2,1)S(1)}, bf16[64,2048]{1,0:T(8,128)(2,1)S(1)}, u32[]{:S(2)}, u32[]{:S(2)}) %collective-permute-start.16) | collective-permute-done | bytes 262176 | tf_op jit(solution)/shard_map/ppermute | solution.py:775
  82.8 2.5 collective-permute-done.15.refs_1_
  85.2 4.1 %collective-permute-done.17.refs_3_ = bf16[64,2048]{1,0:T(8,128)(2,1)S(1)} collective-permute-done((bf16[64,2048]{1,0:T(8,128)(2,1)S(1)}, bf16[64,2048]{1,0:T(8,128)(2,1)S(1)}, u32[]{:S(2)}, u32[]{:S(2)}) %collective-permute-start.17) | collective-permute-done | bytes 262176 | tf_op jit(solution)/shard_map/ppermute | solution.py:775
  90.9 6.7 %ffn.4 = (bf16[512,1024]{1,0:T(8,128)(2,1)S(1)}, bf16[512,1024]{1,0:T(8,128)(2,1)S(1)}, bf16[512,1024]{1,0:T(8,128)(2,1)S(1)}) custom-call(bf16[64,2048]{1,0:T(8,128)(2,1)S(1)} %fusion.12.refs_0_, bf16[64,2048]{1,0:T(8,128)(2,1)S(1)} %collective-permute-done.15.refs_1_, bf16[64,2048]{1,0:T(8,128)(2,1)S(1)} %collective-permute-done.16.refs_2_, ...), custom_call_target="tpu_custom_call" | custom-call | flops 4294967296 | bytes 15728640 | tf_op jit(solution)/shard_map/ffn/pallas_call | solution.py:657
  99.1 2.6 collective-permute-done.22
  103.1 2.0 collective-permute-start.23
  105.1 7.2 %collective-permute-done.24 = bf16[64,2048]{1,0:T(8,128)(2,1)S(1)} collective-permute-done((bf16[64,2048]{1,0:T(8,128)(2,1)S(1)}, bf16[64,2048]{1,0:T(8,128)(2,1)S(1)}, u32[]{:S(2)}, u32[]{:S(2)}) %collective-permute-start.24) | collective-permute-done | bytes 262176 | tf_op jit(solution)/shard_map/ppermute | solution.py:775
  112.4 6.3 %collective-permute-done.23 = bf16[64,2048]{1,0:T(8,128)(2,1)S(1)} collective-permute-done((bf16[64,2048]{1,0:T(8,128)(2,1)S(1)}, bf16[64,2048]{1,0:T(8,128)(2,1)S(1)}, u32[]{:S(2)}, u32[]{:S(2)}) %collective-permute-start.23) | collective-permute-done | bytes 262176 | tf_op jit(solution)/shard_map/ppermute | solution.py:775
  118.7 9.8 %collective-permute-done.25 = bf16[64,2048]{1,0:T(8,128)(2,1)S(1)} collective-permute-done((bf16[64,2048]{1,0:T(8,128)(2,1)S(1)}, bf16[64,2048]{1,0:T(8,128)(2,1)S(1)}, u32[]{:S(2)}, u32[]{:S(2)}) %collective-permute-start.25) | collective-permute-done | bytes 262176 | tf_op jit(solution)/shard_map/ppermute | solution.py:775
  129.4 7.5 %collective-permute-done.27.refs_2_ = bf16[64,2048]{1,0:T(8,128)(2,1)S(1)} collective-permute-done((bf16[64,2048]{1,0:T(8,128)(2,1)S(1)}, bf16[64,2048]{1,0:T(8,128)(2,1)S(1)}, u32[]{:S(2)}, u32[]{:S(2)}) %collective-permute-start.27) | collective-permute-done | bytes 262176 | tf_op jit(solution)/shard_map/ppermute | solution.py:775
  137.4 4.1 collective-permute-done.26.refs_1_
  141.6 3.3 collective-permute-done.28.refs_3_
  146.4 3.8 ffn_back.4
  150.4 3.1 partial_rows.2
  153.8 1.6 collective-permute-start.52
  157.5 3.2 partial_rows.3
  161.4 7.1 %collective-permute-done.35 = bf16[64,2048]{1,0:T(8,128)(2,1)S(1)} collective-permute-done((bf16[64,2048]{1,0:T(8,128)(2,1)S(1)}, bf16[64,2048]{1,0:T(8,128)(2,1)S(1)}, u32[]{:S(2)}, u32[]{:S(2)}) %collective-permute-start.35) | collective-permute-done | bytes 262176 | tf_op jit(solution)/shard_map/ppermute | solution.py:775
  168.9 11.0 %collective-permute-done.52.refs_5_ = bf16[256,2048]{1,0:T(8,128)(2,1)S(1)} collective-permute-done((bf16[256,2048]{1,0:T(8,128)(2,1)S(1)}, bf16[256,2048]{1,0:T(8,128)(2,1)S(1)}, u32[]{:S(2)}, u32[]{:S(2)}) %collective-permute-start.52) | collective-permute-done | bytes 1048608 | tf_op jit(solution)/shard_map/ppermute | solution.py:775
  179.9 21.9 %collective-permute-done.70.refs_0_.refs_5_ = bf16[256,2048]{1,0:T(8,128)(2,1)} collective-permute-done((bf16[256,2048]{1,0:T(8,128)(2,1)S(1)}, bf16[256,2048]{1,0:T(8,128)(2,1)}, u32[]{:S(2)}, u32[]{:S(2)}) %collective-permute-start.70) | collective-permute-done | bytes 1048608 | tf_op jit(solution)/shard_map/ppermute | solution.py:775
  206.2 1.6 collective-permute-start.75
  208.7 1.6 collective-permute-start.80
  210.3 6.4 %collective-permute-done.56.refs_9_ = bf16[128,2048]{1,0:T(8,128)(2,1)S(1)} collective-permute-done((bf16[128,2048]{1,0:T(8,128)(2,1)S(1)}, bf16[128,2048]{1,0:T(8,128)(2,1)S(1)}, u32[]{:S(2)}, u32[]{:S(2)}) %collective-permute-start.56) | collective-permute-done | bytes 524320 | tf_op jit(solution)/shard_map/ppermute | solution.py:775
  216.6 11.2 %collective-permute-done.74.refs_0_.refs_9_ = bf16[128,2048]{1,0:T(8,128)(2,1)S(1)} collective-permute-done((bf16[128,2048]{1,0:T(8,128)(2,1)S(1)}, bf16[128,2048]{1,0:T(8,128)(2,1)S(1)}, u32[]{:S(2)}, u32[]{:S(2)}) %collective-permute-start.74) | collective-permute-done | bytes 524320 | tf_op jit(solution)/shard_map/ppermute | solution.py:775
  230.6 11.1 %collective-permute-done.78.refs_0_.refs_9_ = bf16[256,2048]{1,0:T(8,128)(2,1)} collective-permute-done((bf16[256,2048]{1,0:T(8,128)(2,1)S(1)}, bf16[256,2048]{1,0:T(8,128)(2,1)}, u32[]{:S(2)}, u32[]{:S(2)}) %collective-permute-start.78) | collective-permute-done | bytes 1048608 | tf_op jit(solution)/shard_map/ppermute | solution.py:775
  241.7 1.9 collective-permute-done.38.refs_2_
  243.5 5.5 %collective-permute-done.80.refs_0_.refs_11_ = bf16[256,2048]{1,0:T(8,128)(2,1)} collective-permute-done((bf16[256,2048]{1,0:T(8,128)(2,1)S(1)}, bf16[256,2048]{1,0:T(8,128)(2,1)}, u32[]{:S(2)}, u32[]{:S(2)}) %collective-permute-start.80) | collective-permute-done | bytes 1048608 | tf_op jit(solution)/shard_map/ppermute | solution.py:775
  249.7 2.1 collective-permute-done.39.refs_3_
  253.4 6.0 %attend_back.1 = (bf16[512,256]{1,0:T(8,128)(2,1)S(1)}, f32[512,256]{1,0:T(8,128)S(1)}, f32[512,256]{1,0:T(8,128)S(1)}, f32[8,128]{1,0:T(8,128)S(1)}, f32[2,256]{1,0:T(2,128)S(1)}) custom-call(bf16[64,2048]{1,0:T(8,128)(2,1)S(1)} %get-tuple-element.130.refs_0_, bf16[64,2048]{1,0:T(8,128)(2,1)S(1)} %collective-permute-done.37.refs_1_, ...), custom_call_target="tpu_custom_call" | custom-call | flops 335544320 | bytes 3407872 | tf_op jit(solution)/shard_map/attend_back/pallas_call | solution.py:247
  266.4 1.6 collective-permute-start.82
  269.5 2.2 copy-done.3
  271.7 2.2 copy-done.6
  273.9 6.6 %ffn.7 = (bf16[512,1024]{1,0:T(8,128)(2,1)S(1)}, bf16[512,1024]{1,0:T(8,128)(2,1)S(1)}, bf16[512,1024]{1,0:T(8,128)(2,1)S(1)}) custom-call(bf16[128,2048]{1,0:T(8,128)(2,1)S(1)} %copy-done.43, bf16[128,2048]{1,0:T(8,128)(2,1)S(1)} %copy-done.45, bf16[128,2048]{1,0:T(8,128)(2,1)S(1)} %copy-done.47, bf16[128,2048]{1,0:T(8,128)(2,1)S(1)} %copy-done.49, ...), custom_call_target="tpu_custom_call" | custom-call | flops 4294967296 | bytes 15728640 | tf_op jit(solution)/shard_map/ffn/pallas_call | solution.py:657
  283.4 8.0 %ffn.6 = (bf16[512,1024]{1,0:T(8,128)(2,1)S(1)}, bf16[512,1024]{1,0:T(8,128)(2,1)S(1)}, bf16[512,1024]{1,0:T(8,128)(2,1)S(1)}) custom-call(bf16[256,2048]{1,0:T(8,128)(2,1)} %collective-permute-done.72.refs_0_.refs_7_, bf16[256,2048]{1,0:T(8,128)(2,1)} %collective-permute-done.73.refs_1_.refs_8_, bf16[2048,1024]{1,0:T(8,128)(2,1)S(1)} %copy-done.3, ...), custom_call_target="tpu_custom_call" | custom-call | flops 4294967296 | bytes 15728640 | tf_op jit(solution)/shard_map/ffn/pallas_call | solution.py:657
  291.8 2.3 out_grad.1
  297.2 7.8 %ffn.5 = (bf16[512,1024]{1,0:T(8,128)(2,1)S(1)}, bf16[512,1024]{1,0:T(8,128)(2,1)S(1)}, bf16[512,1024]{1,0:T(8,128)(2,1)S(1)}) custom-call(bf16[256,2048]{1,0:T(8,128)(2,1)} %collective-permute-done.70.refs_0_.refs_5_, bf16[256,2048]{1,0:T(8,128)(2,1)} %collective-permute-done.71.refs_1_.refs_6_, bf16[2048,1024]{1,0:T(8,128)(2,1)S(1)} %copy-done.4, ...), custom_call_target="tpu_custom_call" | custom-call | flops 4294967296 | bytes 15728640 | tf_op jit(solution)/shard_map/ffn/pallas_call | solution.py:657
  305.1 3.7 collective-permute-start.47
  308.8 5.3 %ffn_back.6 = (bf16[512,1024]{1,0:T(8,128)(2,1)S(1)}, bf16[512,1024]{1,0:T(8,128)(2,1)S(1)}) custom-call(bf16[256,2048]{1,0:T(8,128)(2,1)} %collective-permute-done.80.refs_0_.refs_11_, bf16[256,2048]{1,0:T(8,128)(2,1)} %collective-permute-done.81.refs_1_.refs_12_, bf16[1024,2048]{1,0:T(8,128)(2,1)S(1)} %copy-done.1, ...), custom_call_target="tpu_custom_call" | custom-call | flops 2147483648 | bytes 12582912 | tf_op jit(solution)/shard_map/ffn_back/pallas_call | solution.py:691
  316.2 5.4 %ffn_back.5 = (bf16[512,1024]{1,0:T(8,128)(2,1)S(1)}, bf16[512,1024]{1,0:T(8,128)(2,1)S(1)}) custom-call(bf16[256,2048]{1,0:T(8,128)(2,1)} %collective-permute-done.78.refs_0_.refs_9_, bf16[256,2048]{1,0:T(8,128)(2,1)} %collective-permute-done.79.refs_1_.refs_10_, bf16[1024,2048]{1,0:T(8,128)(2,1)S(1)} %copy-done.1, ...), custom_call_target="tpu_custom_call" | custom-call | flops 2147483648 | bytes 12582912 | tf_op jit(solution)/shard_map/ffn_back/pallas_call | solution.py:691
  323.6 1.7 tokens_back.2
  325.2 2.1 collective-permute-done.65.refs_2_
  328.7 1.6 collective-permute-start.67
  330.3 13.7 %weight_grad.7 = f32[1024,2048]{1,0:T(8,128)} custom-call(bf16[512,1024]{1,0:T(8,128)(2,1)} %copy-done.29, bf16[512,1024]{1,0:T(8,128)(2,1)} %copy-done.56, bf16[512,1024]{1,0:T(8,128)(2,1)} %copy-done.55, bf16[512,1024]{1,0:T(8,128)(2,1)} %copy-done.54, bf16[256,2048]{1,0:T(8,128)(2,1)S(1)} %copy-done.13, bf16[64,2048]{1,0:T(8,128)(2,1)S(1)} %copy-done.31, ...), custom_call_target="tpu_custom_call" | custom-call | flops 8589934592 | bytes 20971520 | tf_op jit(solution)/shard_map/weight_grad/pallas_call | solution.py:745
  344.0 5.9 %ffn_back.7 = (bf16[512,1024]{1,0:T(8,128)(2,1)S(1)}, bf16[512,1024]{1,0:T(8,128)(2,1)S(1)}) custom-call(bf16[128,2048]{1,0:T(8,128)(2,1)S(1)} %collective-permute-done.82.refs_0_.refs_13_, bf16[128,2048]{1,0:T(8,128)(2,1)S(1)} %collective-permute-done.83.refs_1_.refs_14_, bf16[128,2048]{1,0:T(8,128)(2,1)S(1)} %collective-permute-done.84.refs_2_.refs_15_, ...), custom_call_target="tpu_custom_call" | custom-call | flops 2147483648 | bytes 12582912 | tf_op jit(solution)/shard_map/ffn_back/pallas_call | solution.py:691
  350.2 3.7 collective-permute-done.67.refs_1_
  356.0 13.8 %weight_grad.6 = f32[2048,1024]{1,0:T(8,128)} custom-call(bf16[256,2048]{1,0:T(8,128)(2,1)} %copy-done.61, bf16[64,2048]{1,0:T(8,128)(2,1)} %copy-done.50, bf16[64,2048]{1,0:T(8,128)(2,1)} %copy-done.52, bf16[64,2048]{1,0:T(8,128)(2,1)} %copy-done.51, bf16[64,2048]{1,0:T(8,128)(2,1)} %copy-done.53, ...), custom_call_target="tpu_custom_call" | custom-call | flops 8589934592 | bytes 20971520 | tf_op jit(solution)/shard_map/weight_grad/pallas_call | solution.py:745
  370.0 1.6 collective-permute-start.63
  373.1 13.8 %weight_grad.5 = f32[2048,1024]{1,0:T(8,128)} custom-call(bf16[256,2048]{1,0:T(8,128)(2,1)} %copy-done.61, bf16[64,2048]{1,0:T(8,128)(2,1)} %copy-done.50, bf16[64,2048]{1,0:T(8,128)(2,1)} %copy-done.52, bf16[64,2048]{1,0:T(8,128)(2,1)} %copy-done.51, bf16[64,2048]{1,0:T(8,128)(2,1)} %copy-done.53, ...), custom_call_target="tpu_custom_call" | custom-call | flops 8589934592 | bytes 20971520 | tf_op jit(solution)/shard_map/weight_grad/pallas_call | solution.py:745
  388.4 1.8 tokens_back.3
  391.3 3.3 collective-permute-start.51
  394.7 11.5 %weight_grad.4 = (f32[2048,256]{1,0:T(8,128)}, f32[2048,256]{1,0:T(8,128)}, f32[2048,256]{1,0:T(8,128)}) custom-call(bf16[256,2048]{1,0:T(8,128)(2,1)} %copy-done.74, bf16[64,2048]{1,0:T(8,128)(2,1)} %copy-done.82, bf16[64,2048]{1,0:T(8,128)(2,1)} %copy-done.84, bf16[64,2048]{1,0:T(8,128)(2,1)} %copy-done.83, bf16[64,2048]{1,0:T(8,128)(2,1)} %copy-done.85, ...), custom_call_target="tpu_custom_call" | custom-call | flops 6442450944 | bytes 17825792 | tf_op jit(solution)/shard_map/weight_grad/pallas_call | solution.py:745
  406.9 4.8 %collective-permute-done.50 = bf16[64,2048]{1,0:T(8,128)(2,1)S(1)} collective-permute-done((bf16[64,2048]{1,0:T(8,128)(2,1)S(1)}, bf16[64,2048]{1,0:T(8,128)(2,1)S(1)}, u32[]{:S(2)}, u32[]{:S(2)}) %collective-permute-start.50) | collective-permute-done | bytes 262176 | tf_op jit(solution)/shard_map/ppermute | solution.py:775
  (347 shorter events, 59.7 us)
Async XLA Ops:
  0.6 16.4 %collective-permute-start.1 = (bf16[64,2048]{1,0:T(8,128)(2,1)}, bf16[64,2048]{1,0:T(8,128)(2,1)S(1)}, u32[]{:S(2)}, u32[]{:S(2)}) collective-permute-start(bf16[64,2048]{1,0:T(8,128)(2,1)} %refs_0_.3), channel_id=1, source_target_pairs={{0,4},{1,5},{2,6},{3,7},{4,0},{5,1},{6,2},{7,3},{8,12},{9,13},{10,... | collective-permute-start | bytes 786440 | tf_op jit(solution)/shard_map/ppermute | solution.py:775
  4.8 13.6 %collective-permute-start = (bf16[64,2048]{1,0:T(8,128)(2,1)}, bf16[64,2048]{1,0:T(8,128)(2,1)S(1)}, u32[]{:S(2)}, u32[]{:S(2)}) collective-permute-start(bf16[64,2048]{1,0:T(8,128)(2,1)} %refs_0_.3), channel_id=1, source_target_pairs={{0,2},{1,3},{2,0},{3,1},{4,6},{5,7},{6,4},{7,5},{8,10},{9,11},{10,... | collective-permute-start | bytes 786440 | tf_op jit(solution)/shard_map/ppermute | solution.py:775
  17.0 7.4 %collective-permute-start.2 = (bf16[64,2048]{1,0:T(8,128)(2,1)S(1)}, bf16[64,2048]{1,0:T(8,128)(2,1)S(1)}, u32[]{:S(2)}, u32[]{:S(2)}) collective-permute-start(bf16[64,2048]{1,0:T(8,128)(2,1)S(1)} %collective-permute-done.1.refs_2_), channel_id=1, source_target_pairs={{0,2},{1,3},{2,0},{3,1},{4,6},{5,7},{6,4},{7,5},{8,10},{9,11},{10,... | collective-permute-start | bytes 786440 | tf_op jit(solution)/shard_map/ppermute | solution.py:775
  17.7 7.7 %collective-permute-start.3 = (bf16[64,2048]{1,0:T(8,128)(2,1)}, bf16[64,2048]{1,0:T(8,128)(2,1)S(1)}, u32[]{:S(2)}, u32[]{:S(2)}) collective-permute-start(bf16[64,2048]{1,0:T(8,128)(2,1)} %refs_0_.3), channel_id=1, source_target_pairs={{0,1},{1,0},{2,3},{3,2},{4,5},{5,4},{6,7},{7,6},{8,9},{9,8},{10,11... | collective-permute-start | bytes 786440 | tf_op jit(solution)/shard_map/ppermute | solution.py:775
  17.8 7.7 %collective-permute-start.5 = (bf16[64,2048]{1,0:T(8,128)(2,1)S(1)}, bf16[64,2048]{1,0:T(8,128)(2,1)S(1)}, u32[]{:S(2)}, u32[]{:S(2)}) collective-permute-start(bf16[64,2048]{1,0:T(8,128)(2,1)S(1)} %collective-permute-done.1.refs_2_), channel_id=1, source_target_pairs={{0,1},{1,0},{2,3},{3,2},{4,5},{5,4},{6,7},{7,6},{8,9},{9,8},{10,11... | collective-permute-start | bytes 786440 | tf_op jit(solution)/shard_map/ppermute | solution.py:775
  47.3 9.2 %collective-permute-start.13 = (bf16[64,2048]{1,0:T(8,128)(2,1)S(1)}, bf16[64,2048]{1,0:T(8,128)(2,1)S(1)}, u32[]{:S(2)}, u32[]{:S(2)}) collective-permute-start(bf16[64,2048]{1,0:T(8,128)(2,1)S(1)} %get-tuple-element.129), channel_id=1, source_target_pairs={{0,2},{1,3},{2,0},{3,1},{4,6},{5,7},{6,4},{7,5},{8,10},{9,11},{10,... | collective-permute-start | bytes 786440 | tf_op jit(solution)/shard_map/ppermute | solution.py:775
  49.4 14.5 %collective-permute-start.12 = (bf16[64,2048]{1,0:T(8,128)(2,1)S(1)}, bf16[64,2048]{1,0:T(8,128)(2,1)S(1)}, u32[]{:S(2)}, u32[]{:S(2)}) collective-permute-start(bf16[64,2048]{1,0:T(8,128)(2,1)S(1)} %get-tuple-element.128), channel_id=1, source_target_pairs={{0,2},{1,3},{2,0},{3,1},{4,6},{5,7},{6,4},{7,5},{8,10},{9,11},{10,... | collective-permute-start | bytes 786440 | tf_op jit(solution)/shard_map/ppermute | solution.py:775
  56.6 17.1 %collective-permute-start.14 = (bf16[64,2048]{1,0:T(8,128)(2,1)S(1)}, bf16[64,2048]{1,0:T(8,128)(2,1)S(1)}, u32[]{:S(2)}, u32[]{:S(2)}) collective-permute-start(bf16[64,2048]{1,0:T(8,128)(2,1)S(1)} %fusion.8), channel_id=1, source_target_pairs={{0,4},{1,5},{2,6},{3,7},{4,0},{5,1},{6,2},{7,3},{8,12},{9,13},{10,... | collective-permute-start | bytes 786440 | tf_op jit(solution)/shard_map/ppermute | solution.py:775
  74.2 8.1 %collective-permute-start.16 = (bf16[64,2048]{1,0:T(8,128)(2,1)S(1)}, bf16[64,2048]{1,0:T(8,128)(2,1)S(1)}, u32[]{:S(2)}, u32[]{:S(2)}) collective-permute-start(bf16[64,2048]{1,0:T(8,128)(2,1)S(1)} %fusion.12.refs_0_), channel_id=1, source_target_pairs={{0,4},{1,5},{2,6},{3,7},{4,0},{5,1},{6,2},{7,3},{8,12},{9,13},{10,... | collective-permute-start | bytes 786440 | tf_op jit(solution)/shard_map/ppermute | solution.py:775
  74.2 11.0 %collective-permute-start.15 = (bf16[64,2048]{1,0:T(8,128)(2,1)S(1)}, bf16[64,2048]{1,0:T(8,128)(2,1)S(1)}, u32[]{:S(2)}, u32[]{:S(2)}) collective-permute-start(bf16[64,2048]{1,0:T(8,128)(2,1)S(1)} %fusion.12.refs_0_), channel_id=1, source_target_pairs={{0,2},{1,3},{2,0},{3,1},{4,6},{5,7},{6,4},{7,5},{8,10},{9,11},{10,... | collective-permute-start | bytes 786440 | tf_op jit(solution)/shard_map/ppermute | solution.py:775
  103.1 9.2 %collective-permute-start.24 = (bf16[64,2048]{1,0:T(8,128)(2,1)S(1)}, bf16[64,2048]{1,0:T(8,128)(2,1)S(1)}, u32[]{:S(2)}, u32[]{:S(2)}) collective-permute-start(bf16[64,2048]{1,0:T(8,128)(2,1)S(1)} %get-tuple-element.127), channel_id=1, source_target_pairs={{0,2},{1,3},{2,0},{3,1},{4,6},{5,7},{6,4},{7,5},{8,10},{9,11},{10,... | collective-permute-start | bytes 786440 | tf_op jit(solution)/shard_map/ppermute | solution.py:775
  103.1 15.6 %collective-permute-start.23 = (bf16[64,2048]{1,0:T(8,128)(2,1)S(1)}, bf16[64,2048]{1,0:T(8,128)(2,1)S(1)}, u32[]{:S(2)}, u32[]{:S(2)}) collective-permute-start(bf16[64,2048]{1,0:T(8,128)(2,1)S(1)} %get-tuple-element.126), channel_id=1, source_target_pairs={{0,2},{1,3},{2,0},{3,1},{4,6},{5,7},{6,4},{7,5},{8,10},{9,11},{10,... | collective-permute-start | bytes 786440 | tf_op jit(solution)/shard_map/ppermute | solution.py:775
  112.4 16.2 %collective-permute-start.25 = (bf16[64,2048]{1,0:T(8,128)(2,1)S(1)}, bf16[64,2048]{1,0:T(8,128)(2,1)S(1)}, u32[]{:S(2)}, u32[]{:S(2)}) collective-permute-start(bf16[64,2048]{1,0:T(8,128)(2,1)S(1)} %fusion.6), channel_id=1, source_target_pairs={{0,4},{1,5},{2,6},{3,7},{4,0},{5,1},{6,2},{7,3},{8,12},{9,13},{10,... | collective-permute-start | bytes 786440 | tf_op jit(solution)/shard_map/ppermute | solution.py:775
  129.2 7.7 %collective-permute-start.27 = (bf16[64,2048]{1,0:T(8,128)(2,1)S(1)}, bf16[64,2048]{1,0:T(8,128)(2,1)S(1)}, u32[]{:S(2)}, u32[]{:S(2)}) collective-permute-start(bf16[64,2048]{1,0:T(8,128)(2,1)S(1)} %fusion.4.refs_0_), channel_id=1, source_target_pairs={{0,4},{1,5},{2,6},{3,7},{4,0},{5,1},{6,2},{7,3},{8,12},{9,13},{10,... | collective-permute-start | bytes 786440 | tf_op jit(solution)/shard_map/ppermute | solution.py:775
  129.3 12.2 %collective-permute-start.26 = (bf16[64,2048]{1,0:T(8,128)(2,1)S(1)}, bf16[64,2048]{1,0:T(8,128)(2,1)S(1)}, u32[]{:S(2)}, u32[]{:S(2)}) collective-permute-start(bf16[64,2048]{1,0:T(8,128)(2,1)S(1)} %fusion.4.refs_0_), channel_id=1, source_target_pairs={{0,2},{1,3},{2,0},{3,1},{4,6},{5,7},{6,4},{7,5},{8,10},{9,11},{10,... | collective-permute-start | bytes 786440 | tf_op jit(solution)/shard_map/ppermute | solution.py:775
  136.9 8.0 %collective-permute-start.28 = (bf16[64,2048]{1,0:T(8,128)(2,1)S(1)}, bf16[64,2048]{1,0:T(8,128)(2,1)S(1)}, u32[]{:S(2)}, u32[]{:S(2)}) collective-permute-start(bf16[64,2048]{1,0:T(8,128)(2,1)S(1)} %collective-permute-done.27.refs_2_), channel_id=1, source_target_pairs={{0,2},{1,3},{2,0},{3,1},{4,6},{5,7},{6,4},{7,5},{8,10},{9,11},{10,... | collective-permute-start | bytes 786440 | tf_op jit(solution)/shard_map/ppermute | solution.py:775
  136.9 8.0 %collective-permute-start.29 = (bf16[64,2048]{1,0:T(8,128)(2,1)S(1)}, bf16[64,2048]{1,0:T(8,128)(2,1)S(1)}, u32[]{:S(2)}, u32[]{:S(2)}) collective-permute-start(bf16[64,2048]{1,0:T(8,128)(2,1)S(1)} %fusion.4.refs_0_), channel_id=1, source_target_pairs={{0,1},{1,0},{2,3},{3,2},{4,5},{5,4},{6,7},{7,6},{8,9},{9,8},{10,11... | collective-permute-start | bytes 786440 | tf_op jit(solution)/shard_map/ppermute | solution.py:775
  136.9 8.0 %collective-permute-start.31 = (bf16[64,2048]{1,0:T(8,128)(2,1)S(1)}, bf16[64,2048]{1,0:T(8,128)(2,1)S(1)}, u32[]{:S(2)}, u32[]{:S(2)}) collective-permute-start(bf16[64,2048]{1,0:T(8,128)(2,1)S(1)} %collective-permute-done.27.refs_2_), channel_id=1, source_target_pairs={{0,1},{1,0},{2,3},{3,2},{4,5},{5,4},{6,7},{7,6},{8,9},{9,8},{10,11... | collective-permute-start | bytes 786440 | tf_op jit(solution)/shard_map/ppermute | solution.py:775
  153.8 26.1 %collective-permute-start.52 = (bf16[256,2048]{1,0:T(8,128)(2,1)S(1)}, bf16[256,2048]{1,0:T(8,128)(2,1)S(1)}, u32[]{:S(2)}, u32[]{:S(2)}) collective-permute-start(bf16[256,2048]{1,0:T(8,128)(2,1)S(1)} %constant_dynamic-update-slice_fusion.refs_0_), channel_id=1, source_target_pairs={{0,8},{8,0},{16,24},{24,16},{1,9},{9,1},{17,25},{25,17},{2,10},{10... | collective-permute-start | bytes 3145736 | tf_op jit(solution)/shard_map/ppermute | solution.py:775
  155.4 46.4 %collective-permute-start.70 = (bf16[256,2048]{1,0:T(8,128)(2,1)S(1)}, bf16[256,2048]{1,0:T(8,128)(2,1)}, u32[]{:S(2)}, u32[]{:S(2)}) collective-permute-start(bf16[256,2048]{1,0:T(8,128)(2,1)S(1)} %pad_maximum_fusion.refs_0_), channel_id=1, source_target_pairs={{0,8},{8,0},{16,24},{24,16},{1,9},{9,1},{17,25},{25,17},{2,10},{10... | collective-permute-start | bytes 3145736 | tf_op jit(solution)/shard_map/ppermute | solution.py:775
  156.0 48.5 %collective-permute-start.72 = (bf16[256,2048]{1,0:T(8,128)(2,1)S(1)}, bf16[256,2048]{1,0:T(8,128)(2,1)}, u32[]{:S(2)}, u32[]{:S(2)}) collective-permute-start(bf16[256,2048]{1,0:T(8,128)(2,1)S(1)} %pad_maximum_fusion.refs_0_), channel_id=1, source_target_pairs={{0,16},{8,24},{16,0},{24,8},{1,17},{9,25},{17,1},{25,9},{2,18},{10... | collective-permute-start | bytes 3145736 | tf_op jit(solution)/shard_map/ppermute | solution.py:775
  160.7 7.8 %collective-permute-start.35 = (bf16[64,2048]{1,0:T(8,128)(2,1)S(1)}, bf16[64,2048]{1,0:T(8,128)(2,1)S(1)}, u32[]{:S(2)}, u32[]{:S(2)}) collective-permute-start(bf16[64,2048]{1,0:T(8,128)(2,1)S(1)} %get-tuple-element.78), channel_id=1, source_target_pairs={{0,2},{1,3},{2,0},{3,1},{4,6},{5,7},{6,4},{7,5},{8,10},{9,11},{10,... | collective-permute-start | bytes 786440 | tf_op jit(solution)/shard_map/ppermute | solution.py:775
  160.8 47.9 %collective-permute-start.54 = (bf16[256,2048]{1,0:T(8,128)(2,1)S(1)}, bf16[256,2048]{1,0:T(8,128)(2,1)S(1)}, u32[]{:S(2)}, u32[]{:S(2)}) collective-permute-start(bf16[256,2048]{1,0:T(8,128)(2,1)S(1)} %constant_dynamic-update-slice_fusion.refs_0_), channel_id=1, source_target_pairs={{0,16},{8,24},{16,0},{24,8},{1,17},{9,25},{17,1},{25,9},{2,18},{10... | collective-permute-start | bytes 3145736 | tf_op jit(solution)/shard_map/ppermute | solution.py:775
  168.5 37.7 %collective-permute-start.34 = (bf16[64,2048]{1,0:T(8,128)(2,1)S(1)}, bf16[64,2048]{1,0:T(8,128)(2,1)S(1)}, u32[]{:S(2)}, u32[]{:S(2)}) collective-permute-start(bf16[64,2048]{1,0:T(8,128)(2,1)S(1)} %get-tuple-element.76), channel_id=1, source_target_pairs={{0,2},{1,3},{2,0},{3,1},{4,6},{5,7},{6,4},{7,5},{8,10},{9,11},{10,... | collective-permute-start | bytes 786440 | tf_op jit(solution)/shard_map/ppermute | solution.py:775
  179.9 27.9 %collective-permute-start.36 = (bf16[64,2048]{1,0:T(8,128)(2,1)S(1)}, bf16[64,2048]{1,0:T(8,128)(2,1)S(1)}, u32[]{:S(2)}, u32[]{:S(2)}) collective-permute-start(bf16[64,2048]{1,0:T(8,128)(2,1)S(1)} %add_convert_fusion), channel_id=1, source_target_pairs={{0,4},{1,5},{2,6},{3,7},{4,0},{5,1},{6,2},{7,3},{8,12},{9,13},{10,... | collective-permute-start | bytes 786440 | tf_op jit(solution)/shard_map/ppermute | solution.py:775
  201.8 14.8 %collective-permute-start.56 = (bf16[128,2048]{1,0:T(8,128)(2,1)S(1)}, bf16[128,2048]{1,0:T(8,128)(2,1)S(1)}, u32[]{:S(2)}, u32[]{:S(2)}) collective-permute-start(bf16[128,2048]{1,0:T(8,128)(2,1)S(1)} %slice.92), channel_id=1, source_target_pairs={{0,16},{8,24},{16,0},{24,8},{1,17},{9,25},{17,1},{25,9},{2,18},{10... | collective-permute-start | bytes 1572872 | tf_op jit(solution)/shard_map/ppermute | solution.py:775
  204.5 23.4 %collective-permute-start.74 = (bf16[128,2048]{1,0:T(8,128)(2,1)S(1)}, bf16[128,2048]{1,0:T(8,128)(2,1)S(1)}, u32[]{:S(2)}, u32[]{:S(2)}) collective-permute-start(bf16[128,2048]{1,0:T(8,128)(2,1)S(1)} %slice.96), channel_id=1, source_target_pairs={{0,16},{8,24},{16,0},{24,8},{1,17},{9,25},{17,1},{25,9},{2,18},{10... | collective-permute-start | bytes 1572872 | tf_op jit(solution)/shard_map/ppermute | solution.py:775
  206.2 22.8 %collective-permute-start.75 = (bf16[128,2048]{1,0:T(8,128)(2,1)S(1)}, bf16[128,2048]{1,0:T(8,128)(2,1)S(1)}, u32[]{:S(2)}, u32[]{:S(2)}) collective-permute-start(bf16[128,2048]{1,0:T(8,128)(2,1)S(1)} %slice.97), channel_id=1, source_target_pairs={{0,8},{8,0},{16,24},{24,16},{1,9},{9,1},{17,25},{25,17},{2,10},{10... | collective-permute-start | bytes 1572872 | tf_op jit(solution)/shard_map/ppermute | solution.py:775
  207.8 33.9 %collective-permute-start.78 = (bf16[256,2048]{1,0:T(8,128)(2,1)S(1)}, bf16[256,2048]{1,0:T(8,128)(2,1)}, u32[]{:S(2)}, u32[]{:S(2)}) collective-permute-start(bf16[256,2048]{1,0:T(8,128)(2,1)S(1)} %pad_maximum_fusion.1.refs_4_), channel_id=1, source_target_pairs={{0,8},{8,0},{16,24},{24,16},{1,9},{9,1},{17,25},{25,17},{2,10},{10... | collective-permute-start | bytes 3145736 | tf_op jit(solution)/shard_map/ppermute | solution.py:775
  208.7 40.3 %collective-permute-start.80 = (bf16[256,2048]{1,0:T(8,128)(2,1)S(1)}, bf16[256,2048]{1,0:T(8,128)(2,1)}, u32[]{:S(2)}, u32[]{:S(2)}) collective-permute-start(bf16[256,2048]{1,0:T(8,128)(2,1)S(1)} %pad_maximum_fusion.1.refs_4_), channel_id=1, source_target_pairs={{0,16},{8,24},{16,0},{24,8},{1,17},{9,25},{17,1},{25,9},{2,18},{10... | collective-permute-start | bytes 3145736 | tf_op jit(solution)/shard_map/ppermute | solution.py:775
  216.6 49.8 %collective-permute-start.73 = (bf16[256,2048]{1,0:T(8,128)(2,1)}, bf16[256,2048]{1,0:T(8,128)(2,1)}, u32[]{:S(2)}, u32[]{:S(2)}) collective-permute-start(bf16[256,2048]{1,0:T(8,128)(2,1)} %collective-permute-done.72.refs_0_.refs_7_), channel_id=1, source_target_pairs={{0,1},{1,0},{2,3},{3,2},{4,5},{5,4},{6,7},{7,6},{8,9},{9,8},{10,11... | collective-permute-start | bytes 3145736 | tf_op jit(solution)/shard_map/ppermute | solution.py:775
  229.0 14.5 %collective-permute-start.38 = (bf16[64,2048]{1,0:T(8,128)(2,1)S(1)}, bf16[64,2048]{1,0:T(8,128)(2,1)S(1)}, u32[]{:S(2)}, u32[]{:S(2)}) collective-permute-start(bf16[64,2048]{1,0:T(8,128)(2,1)S(1)} %get-tuple-element.130.refs_0_), channel_id=1, source_target_pairs={{0,4},{1,5},{2,6},{3,7},{4,0},{5,1},{6,2},{7,3},{8,12},{9,13},{10,... | collective-permute-start | bytes 786440 | tf_op jit(solution)/shard_map/ppermute | solution.py:775
  230.6 18.4 %collective-permute-start.37 = (bf16[64,2048]{1,0:T(8,128)(2,1)S(1)}, bf16[64,2048]{1,0:T(8,128)(2,1)S(1)}, u32[]{:S(2)}, u32[]{:S(2)}) collective-permute-start(bf16[64,2048]{1,0:T(8,128)(2,1)S(1)} %get-tuple-element.130.refs_0_), channel_id=1, source_target_pairs={{0,2},{1,3},{2,0},{3,1},{4,6},{5,7},{6,4},{7,5},{8,10},{9,11},{10,... | collective-permute-start | bytes 786440 | tf_op jit(solution)/shard_map/ppermute | solution.py:775
  241.7 7.9 %collective-permute-start.40 = (bf16[64,2048]{1,0:T(8,128)(2,1)S(1)}, bf16[64,2048]{1,0:T(8,128)(2,1)S(1)}, u32[]{:S(2)}, u32[]{:S(2)}) collective-permute-start(bf16[64,2048]{1,0:T(8,128)(2,1)S(1)} %get-tuple-element.130.refs_0_), channel_id=1, source_target_pairs={{0,1},{1,0},{2,3},{3,2},{4,5},{5,4},{6,7},{7,6},{8,9},{9,8},{10,11... | collective-permute-start | bytes 786440 | tf_op jit(solution)/shard_map/ppermute | solution.py:775
  243.5 8.2 %collective-permute-start.39 = (bf16[64,2048]{1,0:T(8,128)(2,1)S(1)}, bf16[64,2048]{1,0:T(8,128)(2,1)S(1)}, u32[]{:S(2)}, u32[]{:S(2)}) collective-permute-start(bf16[64,2048]{1,0:T(8,128)(2,1)S(1)} %collective-permute-done.38.refs_2_), channel_id=1, source_target_pairs={{0,2},{1,3},{2,0},{3,1},{4,6},{5,7},{6,4},{7,5},{8,10},{9,11},{10,... | collective-permute-start | bytes 786440 | tf_op jit(solution)/shard_map/ppermute | solution.py:775
  249.0 12.8 %collective-permute-start.77 = (bf16[128,2048]{1,0:T(8,128)(2,1)S(1)}, bf16[128,2048]{1,0:T(8,128)(2,1)S(1)}, u32[]{:S(2)}, u32[]{:S(2)}) collective-permute-start(bf16[128,2048]{1,0:T(8,128)(2,1)S(1)} %collective-permute-done.75.refs_1_.refs_10_), channel_id=1, source_target_pairs={{0,1},{1,0},{2,3},{3,2},{4,5},{5,4},{6,7},{7,6},{8,9},{9,8},{10,11... | collective-permute-start | bytes 1572872 | tf_op jit(solution)/shard_map/ppermute | solution.py:775
  251.8 39.7 %collective-permute-start.71 = (bf16[256,2048]{1,0:T(8,128)(2,1)}, bf16[256,2048]{1,0:T(8,128)(2,1)}, u32[]{:S(2)}, u32[]{:S(2)}) collective-permute-start(bf16[256,2048]{1,0:T(8,128)(2,1)} %collective-permute-done.70.refs_0_.refs_5_), channel_id=1, source_target_pairs={{0,1},{1,0},{2,3},{3,2},{4,5},{5,4},{6,7},{7,6},{8,9},{9,8},{10,11... | collective-permute-start | bytes 3145736 | tf_op jit(solution)/shard_map/ppermute | solution.py:775
  252.3 42.5 %collective-permute-start.79 = (bf16[256,2048]{1,0:T(8,128)(2,1)}, bf16[256,2048]{1,0:T(8,128)(2,1)}, u32[]{:S(2)}, u32[]{:S(2)}) collective-permute-start(bf16[256,2048]{1,0:T(8,128)(2,1)} %collective-permute-done.78.refs_0_.refs_9_), channel_id=1, source_target_pairs={{0,1},{1,0},{2,3},{3,2},{4,5},{5,4},{6,7},{7,6},{8,9},{9,8},{10,11... | collective-permute-start | bytes 3145736 | tf_op jit(solution)/shard_map/ppermute | solution.py:775
  253.3 42.0 %collective-permute-start.81 = (bf16[256,2048]{1,0:T(8,128)(2,1)}, bf16[256,2048]{1,0:T(8,128)(2,1)}, u32[]{:S(2)}, u32[]{:S(2)}) collective-permute-start(bf16[256,2048]{1,0:T(8,128)(2,1)} %collective-permute-done.80.refs_0_.refs_11_), channel_id=1, source_target_pairs={{0,1},{1,0},{2,3},{3,2},{4,5},{5,4},{6,7},{7,6},{8,9},{9,8},{10,11... | collective-permute-start | bytes 3145736 | tf_op jit(solution)/shard_map/ppermute | solution.py:775
  266.4 27.8 %collective-permute-start.82 = (bf16[128,2048]{1,0:T(8,128)(2,1)S(1)}, bf16[128,2048]{1,0:T(8,128)(2,1)S(1)}, u32[]{:S(2)}, u32[]{:S(2)}) collective-permute-start(bf16[128,2048]{1,0:T(8,128)(2,1)S(1)} %slice.98), channel_id=1, source_target_pairs={{0,16},{8,24},{16,0},{24,8},{1,17},{9,25},{17,1},{25,9},{2,18},{10... | collective-permute-start | bytes 1572872 | tf_op jit(solution)/shard_map/ppermute | solution.py:775
  268.0 26.8 %collective-permute-start.83 = (bf16[128,2048]{1,0:T(8,128)(2,1)S(1)}, bf16[128,2048]{1,0:T(8,128)(2,1)S(1)}, u32[]{:S(2)}, u32[]{:S(2)}) collective-permute-start(bf16[128,2048]{1,0:T(8,128)(2,1)S(1)} %slice.99), channel_id=1, source_target_pairs={{0,8},{8,0},{16,24},{24,16},{1,9},{9,1},{17,25},{25,17},{2,10},{10... | collective-permute-start | bytes 1572872 | tf_op jit(solution)/shard_map/ppermute | solution.py:775
  294.2 33.9 %collective-permute-start.57 = (bf16[128,2048]{1,0:T(8,128)(2,1)S(1)}, bf16[128,2048]{1,0:T(8,128)(2,1)S(1)}, u32[]{:S(2)}, u32[]{:S(2)}) collective-permute-start(bf16[128,2048]{1,0:T(8,128)(2,1)S(1)} %slice.93), channel_id=1, source_target_pairs={{0,8},{8,0},{16,24},{24,16},{1,9},{9,1},{17,25},{25,17},{2,10},{10... | collective-permute-start | bytes 1572872 | tf_op jit(solution)/shard_map/ppermute | solution.py:775
  294.8 33.9 %collective-permute-start.84 = (bf16[128,2048]{1,0:T(8,128)(2,1)S(1)}, bf16[128,2048]{1,0:T(8,128)(2,1)S(1)}, u32[]{:S(2)}, u32[]{:S(2)}) collective-permute-start(bf16[128,2048]{1,0:T(8,128)(2,1)S(1)} %collective-permute-done.82.refs_0_.refs_13_), channel_id=1, source_target_pairs={{0,1},{1,0},{2,3},{3,2},{4,5},{5,4},{6,7},{7,6},{8,9},{9,8},{10,11... | collective-permute-start | bytes 1572872 | tf_op jit(solution)/shard_map/ppermute | solution.py:775
  294.8 33.9 %collective-permute-start.85 = (bf16[128,2048]{1,0:T(8,128)(2,1)S(1)}, bf16[128,2048]{1,0:T(8,128)(2,1)S(1)}, u32[]{:S(2)}, u32[]{:S(2)}) collective-permute-start(bf16[128,2048]{1,0:T(8,128)(2,1)S(1)} %collective-permute-done.83.refs_1_.refs_14_), channel_id=1, source_target_pairs={{0,1},{1,0},{2,3},{3,2},{4,5},{5,4},{6,7},{7,6},{8,9},{9,8},{10,11... | collective-permute-start | bytes 1572872 | tf_op jit(solution)/shard_map/ppermute | solution.py:775
  295.3 19.5 %collective-permute-start.64 = (bf16[64,2048]{1,0:T(8,128)(2,1)S(1)}, bf16[64,2048]{1,0:T(8,128)(2,1)S(1)}, u32[]{:S(2)}, u32[]{:S(2)}) collective-permute-start(bf16[64,2048]{1,0:T(8,128)(2,1)S(1)} %get-tuple-element.95), channel_id=1, source_target_pairs={{0,8},{8,0},{16,24},{24,16},{1,9},{9,1},{17,25},{25,17},{2,10},{10... | collective-permute-start | bytes 786440 | tf_op jit(solution)/shard_map/ppermute | solution.py:775
  296.8 8.3 %collective-permute-start.46 = (f32[40,128]{1,0:T(8,128)S(1)}, f32[40,128]{1,0:T(8,128)S(1)}, u32[]{:S(2)}, u32[]{:S(2)}) collective-permute-start(f32[40,128]{1,0:T(8,128)S(1)} %add_blocks.3.refs_0_), channel_id=1, source_target_pairs={{0,4},{1,5},{2,6},{3,7},{4,0},{5,1},{6,2},{7,3},{8,12},{9,13},{10,... | collective-permute-start | bytes 61448 | tf_op jit(solution)/shard_map/ppermute | solution.py:775
  305.1 9.1 %collective-permute-start.47 = (f32[40,128]{1,0:T(8,128)S(1)}, f32[40,128]{1,0:T(8,128)S(1)}, u32[]{:S(2)}, u32[]{:S(2)}) collective-permute-start(f32[40,128]{1,0:T(8,128)S(1)} %add_blocks.3.refs_0_), channel_id=1, source_target_pairs={{0,6},{1,7},{2,4},{3,5},{4,2},{5,3},{6,0},{7,1},{8,14},{9,15},{10,... | collective-permute-start | bytes 61448 | tf_op jit(solution)/shard_map/ppermute | solution.py:775
  314.2 13.1 %collective-permute-start.65 = (bf16[64,2048]{1,0:T(8,128)(2,1)S(1)}, bf16[64,2048]{1,0:T(8,128)(2,1)S(1)}, u32[]{:S(2)}, u32[]{:S(2)}) collective-permute-start(bf16[64,2048]{1,0:T(8,128)(2,1)S(1)} %get-tuple-element.96), channel_id=1, source_target_pairs={{0,16},{8,24},{16,0},{24,8},{1,17},{9,25},{17,1},{25,9},{2,18},{10... | collective-permute-start | bytes 786440 | tf_op jit(solution)/shard_map/ppermute | solution.py:775
  314.8 12.5 %collective-permute-start.66 = (bf16[64,2048]{1,0:T(8,128)(2,1)S(1)}, bf16[64,2048]{1,0:T(8,128)(2,1)S(1)}, u32[]{:S(2)}, u32[]{:S(2)}) collective-permute-start(bf16[64,2048]{1,0:T(8,128)(2,1)S(1)} %get-tuple-element.97), channel_id=1, source_target_pairs={{0,24},{8,16},{16,8},{24,0},{1,25},{9,17},{17,9},{25,1},{2,26},{10... | collective-permute-start | bytes 786440 | tf_op jit(solution)/shard_map/ppermute | solution.py:775
  327.3 22.6 %collective-permute-start.58 = (bf16[128,2048]{1,0:T(8,128)(2,1)S(1)}, bf16[128,2048]{1,0:T(8,128)(2,1)S(1)}, u32[]{:S(2)}, u32[]{:S(2)}) collective-permute-start(bf16[128,2048]{1,0:T(8,128)(2,1)S(1)} %copy-done.78), channel_id=1, source_target_pairs={{0,1},{1,0},{2,3},{3,2},{4,5},{5,4},{6,7},{7,6},{8,9},{9,8},{10,11... | collective-permute-start | bytes 1572872 | tf_op jit(solution)/shard_map/ppermute | solution.py:775
  327.3 26.6 %collective-permute-start.61 = (bf16[528,768]{1,0:T(8,128)(2,1)S(1)}, bf16[528,768]{1,0:T(8,128)(2,1)S(1)}, u32[]{:S(2)}, u32[]{:S(2)}) collective-permute-start(bf16[528,768]{1,0:T(8,128)(2,1)S(1)} %finish.1.grad_ref.refs_13_.refs_0_), channel_id=1, source_target_pairs={{0,16},{8,24},{16,0},{24,8},{1,17},{9,25},{17,1},{25,9},{2,18},{10... | collective-permute-start | bytes 2433032 | tf_op jit(solution)/shard_map/ppermute | solution.py:775
  328.1 27.4 %collective-permute-start.60 = (bf16[528,768]{1,0:T(8,128)(2,1)S(1)}, bf16[528,768]{1,0:T(8,128)(2,1)S(1)}, u32[]{:S(2)}, u32[]{:S(2)}) collective-permute-start(bf16[528,768]{1,0:T(8,128)(2,1)S(1)} %finish.1.grad_ref.refs_13_.refs_0_), channel_id=1, source_target_pairs={{0,8},{8,0},{16,24},{24,16},{1,9},{9,1},{17,25},{25,17},{2,10},{10... | collective-permute-start | bytes 2433032 | tf_op jit(solution)/shard_map/ppermute | solution.py:775
  328.7 42.9 %collective-permute-start.48 = (bf16[256,2048]{1,0:T(8,128)(2,1)S(1)}, bf16[256,2048]{1,0:T(8,128)(2,1)S(1)}, u32[]{:S(2)}, u32[]{:S(2)}) collective-permute-start(bf16[256,2048]{1,0:T(8,128)(2,1)S(1)} %tokens_back.2), channel_id=1, source_target_pairs={{0,1},{1,0},{2,3},{3,2},{4,5},{5,4},{6,7},{7,6},{8,9},{9,8},{10,11... | collective-permute-start | bytes 3145736 | tf_op jit(solution)/shard_map/ppermute | solution.py:775
  328.7 25.2 %collective-permute-start.67 = (bf16[64,2048]{1,0:T(8,128)(2,1)S(1)}, bf16[64,2048]{1,0:T(8,128)(2,1)S(1)}, u32[]{:S(2)}, u32[]{:S(2)}) collective-permute-start(bf16[64,2048]{1,0:T(8,128)(2,1)S(1)} %add_pieces.1.refs_0_), channel_id=1, source_target_pairs={{0,8},{8,0},{16,24},{24,16},{1,9},{9,1},{17,25},{25,17},{2,10},{10... | collective-permute-start | bytes 786440 | tf_op jit(solution)/shard_map/ppermute | solution.py:775
  350.0 40.3 %collective-permute-start.53 = (bf16[256,2048]{1,0:T(8,128)(2,1)S(1)}, bf16[256,2048]{1,0:T(8,128)(2,1)S(1)}, u32[]{:S(2)}, u32[]{:S(2)}) collective-permute-start(bf16[256,2048]{1,0:T(8,128)(2,1)S(1)} %copy-done.63), channel_id=1, source_target_pairs={{0,1},{1,0},{2,3},{3,2},{4,5},{5,4},{6,7},{7,6},{8,9},{9,8},{10,11... | collective-permute-start | bytes 3145736 | tf_op jit(solution)/shard_map/ppermute | solution.py:775
  353.9 37.4 %collective-permute-start.55 = (bf16[256,2048]{1,0:T(8,128)(2,1)S(1)}, bf16[256,2048]{1,0:T(8,128)(2,1)S(1)}, u32[]{:S(2)}, u32[]{:S(2)}) collective-permute-start(bf16[256,2048]{1,0:T(8,128)(2,1)S(1)} %copy-done.65), channel_id=1, source_target_pairs={{0,1},{1,0},{2,3},{3,2},{4,5},{5,4},{6,7},{7,6},{8,9},{9,8},{10,11... | collective-permute-start | bytes 3145736 | tf_op jit(solution)/shard_map/ppermute | solution.py:775
  353.9 16.0 %collective-permute-start.68 = (bf16[64,2048]{1,0:T(8,128)(2,1)S(1)}, bf16[64,2048]{1,0:T(8,128)(2,1)S(1)}, u32[]{:S(2)}, u32[]{:S(2)}) collective-permute-start(bf16[64,2048]{1,0:T(8,128)(2,1)S(1)} %add_pieces.1.refs_0_), channel_id=1, source_target_pairs={{0,16},{8,24},{16,0},{24,8},{1,17},{9,25},{17,1},{25,9},{2,18},{10... | collective-permute-start | bytes 786440 | tf_op jit(solution)/shard_map/ppermute | solution.py:775
  355.5 14.5 %collective-permute-start.69 = (bf16[64,2048]{1,0:T(8,128)(2,1)S(1)}, bf16[64,2048]{1,0:T(8,128)(2,1)S(1)}, u32[]{:S(2)}, u32[]{:S(2)}) collective-permute-start(bf16[64,2048]{1,0:T(8,128)(2,1)S(1)} %add_pieces.1.refs_0_), channel_id=1, source_target_pairs={{0,24},{8,16},{16,8},{24,0},{1,25},{9,17},{17,9},{25,1},{2,26},{10... | collective-permute-start | bytes 786440 | tf_op jit(solution)/shard_map/ppermute | solution.py:775
  369.9 20.3 %collective-permute-start.59 = (bf16[128,2048]{1,0:T(8,128)(2,1)S(1)}, bf16[128,2048]{1,0:T(8,128)(2,1)S(1)}, u32[]{:S(2)}, u32[]{:S(2)}) collective-permute-start(bf16[128,2048]{1,0:T(8,128)(2,1)S(1)} %collective-permute-done.57.refs_10_), channel_id=1, source_target_pairs={{0,1},{1,0},{2,3},{3,2},{4,5},{5,4},{6,7},{7,6},{8,9},{9,8},{10,11... | collective-permute-start | bytes 1572872 | tf_op jit(solution)/shard_map/ppermute | solution.py:775
  370.0 24.7 %collective-permute-start.63 = (bf16[272,768]{1,0:T(8,128)(2,1)S(1)}, bf16[272,768]{1,0:T(8,128)(2,1)S(1)}, u32[]{:S(2)}, u32[]{:S(2)}) collective-permute-start(bf16[272,768]{1,0:T(8,128)(2,1)S(1)} %slice.95), channel_id=1, source_target_pairs={{0,8},{8,0},{16,24},{24,16},{1,9},{9,1},{17,25},{25,17},{2,10},{10... | collective-permute-start | bytes 1253384 | tf_op jit(solution)/shard_map/ppermute | solution.py:775
  371.6 23.1 %collective-permute-start.62 = (bf16[256,768]{1,0:T(8,128)(2,1)S(1)}, bf16[256,768]{1,0:T(8,128)(2,1)S(1)}, u32[]{:S(2)}, u32[]{:S(2)}) collective-permute-start(bf16[256,768]{1,0:T(8,128)(2,1)S(1)} %slice.94), channel_id=1, source_target_pairs={{0,16},{8,24},{16,0},{24,8},{1,17},{9,25},{17,1},{25,9},{2,18},{10... | collective-permute-start | bytes 1179656 | tf_op jit(solution)/shard_map/ppermute | solution.py:775
  390.2 16.7 %collective-permute-start.49 = (bf16[64,2048]{1,0:T(8,128)(2,1)S(1)}, bf16[64,2048]{1,0:T(8,128)(2,1)S(1)}, u32[]{:S(2)}, u32[]{:S(2)}) collective-permute-start(bf16[64,2048]{1,0:T(8,128)(2,1)S(1)} %get-tuple-element.88), channel_id=1, source_target_pairs={{0,2},{1,3},{2,0},{3,1},{4,6},{5,7},{6,4},{7,5},{8,10},{9,11},{10,... | collective-permute-start | bytes 786440 | tf_op jit(solution)/shard_map/ppermute | solution.py:775
  390.3 21.4 %collective-permute-start.50 = (bf16[64,2048]{1,0:T(8,128)(2,1)S(1)}, bf16[64,2048]{1,0:T(8,128)(2,1)S(1)}, u32[]{:S(2)}, u32[]{:S(2)}) collective-permute-start(bf16[64,2048]{1,0:T(8,128)(2,1)S(1)} %get-tuple-element.89), channel_id=1, source_target_pairs={{0,4},{1,5},{2,6},{3,7},{4,0},{5,1},{6,2},{7,3},{8,12},{9,13},{10,... | collective-permute-start | bytes 786440 | tf_op jit(solution)/shard_map/ppermute | solution.py:775
  391.3 20.4 %collective-permute-start.51 = (bf16[64,2048]{1,0:T(8,128)(2,1)S(1)}, bf16[64,2048]{1,0:T(8,128)(2,1)S(1)}, u32[]{:S(2)}, u32[]{:S(2)}) collective-permute-start(bf16[64,2048]{1,0:T(8,128)(2,1)S(1)} %get-tuple-element.90), channel_id=1, source_target_pairs={{0,6},{1,7},{2,4},{3,5},{4,2},{5,3},{6,0},{7,1},{8,14},{9,15},{10,... | collective-permute-start | bytes 786440 | tf_op jit(solution)/shard_map/ppermute | solution.py:775
  (108 other events, 1033.3 us)
